TPU v7x, 512 devices: a whole 4x4x16 slice. The times are simulated.
512 devices in a mesh: rows: 64 (over y, z), cols: 8 (over x, core).
Axes of the slice: x: 4, y: 4, z: 16, core: 2. Of those that a mesh axis runs over, the one named last changes fastest.
Arguments:
- node_features: bfloat16 [65536, 512], P('rows', 'cols'), may hold values from -6 to 6
- weight: bfloat16 [512, 512], replicated, may hold values from -0.25 to 0.25
- tile_values: bfloat16 [4096, 128, 128], P('rows'), may hold values from -0.1875 to 0.1875
- tile_row: int32 [4096], P('rows'), may hold values from 0 to 7
- source_owner: int32 [4096, 1], P('rows'), may hold values from 0 to 63; in each aligned block of 64 rows (0 to 63, 64 to 127, ...) at most 2 rows name the same one
- source_block: int32 [4096], P('rows'), may hold values from 0 to 7
- labels: int32 [65536], P('rows'), may hold values from 0 to 511
Outputs:
- activations: bfloat16 [65536, 512], P('rows', 'cols')
- weight_grad: float32 [512, 512], P(None, 'cols')
- feature_grad: bfloat16 [65536, 512], P('rows', 'cols')
Inputs may be any that keep to these rules, and one draw needn't show every extreme that they name: `source_owner`: of the 64 tiles of one index of rows, at most 2 name the same owner.
All inputs are finite; a program needn't handle non-finite values.
Results may differ from a plain program's by a relative error of at most 0.0095.
Values may be sent and summed in bfloat16 or wider, within the bound.
A program may use at most 64 MiB of HBM per device.

v0:
```python
import math

import jax
import jax.numpy as jnp
from jax import lax
from jax.sharding import PartitionSpec as P


def slot_ranks(owners):
    positions = jnp.arange(owners.shape[0], dtype=jnp.int32)
    earlier = (owners[:, None] == owners[None, :]) & (positions[None, :] < positions[:, None])
    return jnp.sum(earlier.astype(jnp.int32), axis=1)


def per_device(node_features, weight, tile_values, tile_row, source_owner, source_block, labels):
    local_rows, col_width = node_features.shape
    block_size = tile_values.shape[1]
    local_blocks = local_rows // block_size
    row_devices = lax.axis_size("rows")
    capacity = 2 * tile_values.shape[0] // row_devices
    owners = source_owner[:, 0]
    slot_rank = slot_ranks(owners)
    column_block = owners * local_blocks + source_block
    local_ids = jnp.arange(local_blocks, dtype=jnp.int32)
    row_onehot = (tile_row[:, None] == local_ids[None, :]).astype(jnp.float32)
    gathered = lax.all_gather(node_features, "rows", axis=0, tiled=True)
    all_blocks = gathered.reshape(row_devices * local_blocks, block_size, col_width)
    source_rows = all_blocks[column_block]
    products = jnp.einsum(
        "tij,tjf->tif", tile_values, source_rows, preferred_element_type=jnp.float32
    )
    summed = jnp.einsum("tb,tif->bif", row_onehot, products, precision=lax.Precision.HIGHEST)
    aggregated = summed.reshape(local_rows, col_width).astype(jnp.bfloat16)
    aggregated_all = lax.all_gather(aggregated, "cols", axis=1, tiled=True)
    col_index = lax.axis_index("cols")
    w_columns = lax.dynamic_slice_in_dim(weight, col_index * col_width, col_width, 1)
    w_rows = lax.dynamic_slice_in_dim(weight, col_index * col_width, col_width, 0)
    hidden = jnp.dot(aggregated_all, w_columns, preferred_element_type=jnp.float32)
    sigmoid = jax.nn.sigmoid(hidden)
    activated = hidden * sigmoid
    slopes = sigmoid * (1.0 + hidden * (1.0 - sigmoid))
    feature_ids = col_index * col_width + jnp.arange(col_width, dtype=jnp.int32)
    target = (labels[:, None] == feature_ids[None, :]).astype(jnp.float32)
    out_grad = ((activated - target) * slopes).astype(jnp.bfloat16)
    grad_all = lax.all_gather(out_grad, "cols", axis=1, tiled=True)
    weight_terms = jnp.einsum(
        "nk,nc->kc", aggregated_all, out_grad, preferred_element_type=jnp.float32
    )
    node_total = local_rows * row_devices
    weight_grad = lax.psum(weight_terms, "rows") / math.sqrt(node_total)
    agg_grad = jnp.einsum("nc,kc->nk", grad_all, w_rows, preferred_element_type=jnp.float32).astype(
        jnp.bfloat16
    )
    grad_rows = agg_grad.reshape(local_blocks, block_size, col_width)[tile_row]
    sent_terms = jnp.einsum(
        "tji,tjf->tif", tile_values, grad_rows, preferred_element_type=jnp.float32
    )
    send_terms = (
        jnp.zeros((row_devices, capacity, block_size, col_width), jnp.float32)
        .at[owners, slot_rank]
        .set(sent_terms)
    )
    send_index = (
        jnp.zeros((row_devices, capacity), jnp.int32).at[owners, slot_rank].set(source_block)
    )
    received, recv_index = (
        lax.all_to_all(
            send_terms.astype(jnp.bfloat16), "rows", split_axis=0, concat_axis=0, tiled=True
        ).astype(send_terms.dtype),
        lax.all_to_all(send_index, "rows", split_axis=0, concat_axis=0, tiled=True),
    )
    placing = (recv_index[:, :, None] == local_ids[None, None, :]).astype(jnp.float32)
    filled = (jnp.abs(received).sum(axis=(2, 3)) >= 0.0).astype(jnp.float32)
    feature_grad = jnp.einsum(
        "scb,scif->bif", placing * filled[:, :, None], received, precision=lax.Precision.HIGHEST
    ).reshape(local_rows, col_width)
    return (activated.astype(jnp.bfloat16), weight_grad, feature_grad.astype(jnp.bfloat16))


def solution(mesh):
    return jax.shard_map(
        per_device,
        mesh=mesh,
        in_specs=(
            P("rows", "cols"),
            P(),
            P("rows", None, None),
            P("rows"),
            P("rows", None),
            P("rows"),
            P("rows"),
        ),
        out_specs=(P("rows", "cols"), P(None, "cols"), P("rows", "cols")),
        check_vma=False,
    )
```

profile of v0, /device:TPU:1, one launch (start us, length us, event | category | flops | bytes accessed | tf_op | source)
XLA Modules:
  0.0 580.6 jit_solution(7779311799218977783)
XLA Ops:
  7.2 0.0 copy-start
  7.2 0.0 all-gather.4.cloned.1.call-start
  7.2 0.7 all-gather.4.cloned.1.call-update
  7.9 0.0 all-gather.6.cloned.1.call-start
  8.0 0.7 compare_select_fusion.3
  8.6 157.1 %all-gather.4.cloned.1.call-done = bf16[65536,64]{0,1:T(8,128)(2,1)} async-done(((bf16[1024,64]{0,1:T(8,128)(2,1)}), bf16[65536,64]{0,1:T(8,128)(2,1)}) %all-gather.4.cloned.1.call-update) | async-done | bytes 8388624 | tf_op jit(solution)/shard_map/all_gather | solution.py:26
  165.8 9.0 %copy_bitcast_fusion = bf16[512,128,64]{1,2,0:T(8,128)(2,1)} fusion(bf16[65536,64]{0,1:T(8,128)(2,1)} %all-gather.4.cloned.1.call-done), kind=kLoop, calls=%fused_computation.4 | loop fusion | bytes 16777216 | tf_op jit(solution)/shard_map/reshape | solution.py:27
  174.8 4.1 gather_fusion
  178.9 0.0 copy-done
  179.0 0.0 copy-start.4
  179.0 1.5 convolution_bitcast_fusion.1
  180.5 0.0 copy-done.4
  180.5 0.0 copy-start.5
  180.5 2.0 fusion.10
  182.5 0.0 copy-start.6
  182.5 0.0 copy-start.3
  182.5 0.7 copy.68
  183.2 0.0 all-gather.6.cloned.1.call-update
  183.2 0.0 all-gather.8.cloned.1.call-start
  183.3 34.4 %all-gather.6.cloned.1.call-done = bf16[1024,512]{0,1:T(8,128)(2,1)} async-done(((bf16[1024,64]{0,1:T(8,128)(2,1)}), bf16[1024,512]{0,1:T(8,128)(2,1)}) %all-gather.6.cloned.1.call-update) | async-done | bytes 1048592 | tf_op jit(solution)/shard_map/all_gather | solution.py:34
  217.7 2.4 multiply_convert_fusion
  220.1 0.0 all-gather.8.cloned.1.call-update
  220.1 0.0 copy-done.6
  220.1 0.2 convert_reduce_fusion
  220.3 3.5 scatter_fusion
  223.8 0.7 copy.42
  224.5 15.2 %all-to-all-start = ((s32[64,1,2]{2,1,0:T(1,128)}), s32[64,1,2]{2,1,0:T(1,128)S(1)}, u32[]{:S(2)}, u32[]{:S(2)}) async-start(s32[64,1,2]{2,1,0:T(1,128)} %copy.42), calls=%async_computation | async-start | bytes 65536 | tf_op jit(solution)/shard_map/all_to_all | solution.py:70
  239.8 11.6 %all-gather.8.cloned.1.call-done = bf16[1024,512]{0,1:T(8,128)(2,1)} async-done(((bf16[1024,64]{0,1:T(8,128)(2,1)}), bf16[1024,512]{0,1:T(8,128)(2,1)}) %all-gather.8.cloned.1.call-update) | async-done | bytes 1048592 | tf_op jit(solution)/shard_map/all_gather | solution.py:45
  251.4 1.6 fusion.13
  253.0 0.8 gather_fusion.1
  253.8 2.0 convolution_bitcast_fusion
  255.8 2.5 broadcast_in_dim.10
  258.3 10.7 %scatter_fusion.1 = f32[64,2,128,64]{2,3,1,0:T(8,128)} fusion(f32[64,2,128,64]{2,3,1,0:T(8,128)} %broadcast_in_dim.10, s32[64]{0:T(128)S(1)} %fusion.31, f32[64,128,64]{1,2,0:T(8,128)} %convolution_bitcast_fusion), kind=kCustom, calls=%fused_computation.3 | custom fusion | bytes 6291968 | tf_op jit(solution)/shard_map/scatter | solution.py:61
  268.9 2.7 convert_element_type.49
  271.6 3.5 copy.45
  275.1 0.0 all-to-all-done
  275.1 15.7 %all-to-all-start.1 = ((bf16[64,2,128,64]{2,1,3,0:T(2,128)(2,1)}), bf16[64,2,128,64]{2,1,3,0:T(2,128)(2,1)}, u32[]{:S(2)}, u32[]{:S(2)}) async-start(bf16[64,2,128,64]{2,1,3,0:T(2,128)(2,1)} %copy.45), calls=%async_computation.1 | async-start | bytes 4194304 | tf_op jit(solution)/shard_map/all_to_all | solution.py:67
  290.9 0.0 all-reduce.2.cloned.1.call-start
  290.9 1.1 fusion.33
  292.1 0.0 all-reduce.2.cloned.1.call-update
  292.1 0.1 copy.43
  292.1 271.2 %all-reduce.2.cloned.1.call-done = f32[512,64]{0,1:T(8,128)} async-done(((f32[512,64]{0,1:T(8,128)}), f32[512,64]{0,1:T(8,128)}) %all-reduce.2.cloned.1.call-update) | async-done | bytes 131088 | tf_op jit(solution)/shard_map/psum | solution.py:50
  563.4 1.6 broadcast_multiply_fusion
  564.9 0.0 all-to-all-done.1
  564.9 3.8 abs_reduce_fusion
  568.8 0.1 copy.46
  568.9 4.5 fusion.7
  573.4 0.7 copy.67
  (14 shorter events, 0.1 us)
Async XLA Ops:
  7.2 171.8 %copy-start = (bf16[64,128,128]{2,1,0:T(8,128)(2,1)S(1)}, bf16[64,128,128]{2,1,0:T(8,128)(2,1)}, u32[]{:S(2)}) copy-start(bf16[64,128,128]{2,1,0:T(8,128)(2,1)} %param.9) | copy-start | bytes 6291460
  7.2 158.6 %all-gather.4.cloned.1.call-start = ((), (), s32[]{:S(2)}) async-start(), calls=%async_computation.2 | async-start | bytes 8519680 | tf_op jit(solution)/shard_map/all_gather | solution.py:26
  7.9 209.8 %all-gather.6.cloned.1.call-start = ((), (), s32[]{:S(2)}) async-start(), calls=%async_computation.3 | async-start | bytes 1179648 | tf_op jit(solution)/shard_map/all_gather | solution.py:34
  179.0 1.5 copy-start.4
  180.5 37.2 %copy-start.5 = (s32[1024]{0:T(1024)S(1)}, s32[1024]{0:T(1024)}, u32[]{:S(2)}) copy-start(s32[1024]{0:T(1024)} %param.13) | copy-start | bytes 12292
  182.5 37.6 %copy-start.6 = (s32[64,1]{0,1:T(1,128)S(1)}, s32[64,1]{0,1:T(1,128)}, u32[]{:S(2)}) copy-start(s32[64,1]{0,1:T(1,128)} %param.11) | copy-start | bytes 772
  182.5 37.8 %copy-start.3 = (s32[64]{0:T(128)S(1)}, s32[64]{0:T(128)}, u32[]{:S(2)}) copy-start(s32[64]{0:T(128)} %param.12) | copy-start | bytes 772
  183.2 68.2 %all-gather.8.cloned.1.call-start = ((), (), s32[]{:S(2)}) async-start(), calls=%async_computation.5 | async-start | bytes 1179648 | tf_op jit(solution)/shard_map/all_gather | solution.py:45
  224.5 50.6 %all-to-all-start = ((s32[64,1,2]{2,1,0:T(1,128)}), s32[64,1,2]{2,1,0:T(1,128)S(1)}, u32[]{:S(2)}, u32[]{:S(2)}) async-start(s32[64,1,2]{2,1,0:T(1,128)} %copy.42), calls=%async_computation | async-start | bytes 65536 | tf_op jit(solution)/shard_map/all_to_all | solution.py:70
  275.1 15.8 %copy-start.1 = (bf16[1024,512]{0,1:T(8,128)(2,1)S(1)}, bf16[1024,512]{0,1:T(8,128)(2,1)}, u32[]{:S(2)}) copy-start(bf16[1024,512]{0,1:T(8,128)(2,1)} %all-gather.6.cloned.1.call-done) | copy-start | bytes 3145732
  275.1 15.8 %copy-start.2 = (bf16[1024,64]{0,1:T(8,128)(2,1)S(1)}, bf16[1024,64]{0,1:T(8,128)(2,1)}, u32[]{:S(2)}) copy-start(bf16[1024,64]{0,1:T(8,128)(2,1)} %get-tuple-element.3) | copy-start | bytes 393220
  275.1 289.8 %all-to-all-start.1 = ((bf16[64,2,128,64]{2,1,3,0:T(2,128)(2,1)}), bf16[64,2,128,64]{2,1,3,0:T(2,128)(2,1)}, u32[]{:S(2)}, u32[]{:S(2)}) async-start(bf16[64,2,128,64]{2,1,3,0:T(2,128)(2,1)} %copy.45), calls=%async_computation.1 | async-start | bytes 4194304 | tf_op jit(solution)/shard_map/all_to_all | solution.py:67
  290.9 272.5 %all-reduce.2.cloned.1.call-start = ((), (), s32[]{:S(2)}) async-start(), calls=%async_computation.4 | async-start | bytes 262144 | tf_op jit(solution)/shard_map/psum | solution.py:50
Sparse Core Ops, SparseCore 0:
  11.0 154.7 all-gather.3
  183.3 34.3 all-gather.5
  220.4 30.9 all-gather.7
  295.4 267.9 all-reduce.1
where the time goes:
time: 591 us; the launch traced here: 581 us
  waiting for transfers between devices  475 us (80%)
  local copies, waits for them, and re-layouts  36.3 us (6%)
  starting transfers between devices  31.1 us (5%)
  matrix products  15.1 us (3%)
  between operations  14 us (2%)
  other arithmetic  9.01 us (2%)
    psum x1, waiting for transfers between devices, per_device(): weight_grad = lax.psum(weight_terms, 'rows') / math.sqrt(node_total)  271 us
    all_gather x1, waiting for transfers between devices, per_device(): gathered = lax.all_gather(node_features, 'rows', axis=0, tiled=True)  157 us
    all_gather x1, waiting for transfers between devices, per_device(): aggregated_all = lax.all_gather(aggregated, 'cols', axis=1, tiled=True)  34.4 us
    all_to_all x1, starting transfers between devices, per_device(): lax.all_to_all(send_terms.astype(jnp.bfloat16), 'rows', split_axis=0, con...  15.7 us
    all_to_all x1, starting transfers between devices, per_device(): lax.all_to_all(send_index, 'rows', split_axis=0, concat_axis=0, tiled=True)  15.2 us
  transfers between devices with their start and end apart: 6, of which 4 were waited for; matrix products, arithmetic and copies ran while one was open for 5% of the time, Pallas kernels for 0%

commit v1 on v0

--- a/solution.py
+++ b/solution.py
@@ -12,6 +12,16 @@
     return jnp.sum(earlier.astype(jnp.int32), axis=1)
 
 
+def row_all_reduce(partial):
+    row_devices = lax.axis_size("rows")
+    k, c = partial.shape
+    pieces = partial.reshape(row_devices, k // row_devices, c)
+    gathered = lax.all_to_all(pieces, "rows", split_axis=0, concat_axis=0, tiled=True)
+    reduced = jnp.sum(gathered, axis=0)
+    spread = jnp.broadcast_to(reduced[None], (row_devices,) + reduced.shape)
+    return lax.all_to_all(spread, "rows", split_axis=0, concat_axis=0, tiled=True).reshape(k, c)
+
+
 def per_device(node_features, weight, tile_values, tile_row, source_owner, source_block, labels):
     local_rows, col_width = node_features.shape
     block_size = tile_values.shape[1]
@@ -20,12 +30,14 @@
     capacity = 2 * tile_values.shape[0] // row_devices
     owners = source_owner[:, 0]
     slot_rank = slot_ranks(owners)
-    column_block = owners * local_blocks + source_block
     local_ids = jnp.arange(local_blocks, dtype=jnp.int32)
     row_onehot = (tile_row[:, None] == local_ids[None, :]).astype(jnp.float32)
-    gathered = lax.all_gather(node_features, "rows", axis=0, tiled=True)
-    all_blocks = gathered.reshape(row_devices * local_blocks, block_size, col_width)
-    source_rows = all_blocks[column_block]
+    request = jnp.zeros((row_devices, capacity), jnp.int32).at[owners, slot_rank].set(source_block)
+    wanted = lax.all_to_all(request, "rows", split_axis=0, concat_axis=0, tiled=True)
+    own_blocks = node_features.reshape(local_blocks, block_size, col_width)
+    outgoing = own_blocks[wanted]
+    incoming = lax.all_to_all(outgoing, "rows", split_axis=0, concat_axis=0, tiled=True)
+    source_rows = incoming[owners, slot_rank]
     products = jnp.einsum(
         "tij,tjf->tif", tile_values, source_rows, preferred_element_type=jnp.float32
     )
@@ -47,7 +59,7 @@
         "nk,nc->kc", aggregated_all, out_grad, preferred_element_type=jnp.float32
     )
     node_total = local_rows * row_devices
-    weight_grad = lax.psum(weight_terms, "rows") / math.sqrt(node_total)
+    weight_grad = row_all_reduce(weight_terms) / math.sqrt(node_total)
     agg_grad = jnp.einsum("nc,kc->nk", grad_all, w_rows, preferred_element_type=jnp.float32).astype(
         jnp.bfloat16
     )
@@ -56,23 +68,14 @@
         "tji,tjf->tif", tile_values, grad_rows, preferred_element_type=jnp.float32
     )
     send_terms = (
-        jnp.zeros((row_devices, capacity, block_size, col_width), jnp.float32)
+        jnp.zeros((row_devices, capacity, block_size, col_width), jnp.bfloat16)
         .at[owners, slot_rank]
-        .set(sent_terms)
+        .set(sent_terms.astype(jnp.bfloat16))
     )
-    send_index = (
-        jnp.zeros((row_devices, capacity), jnp.int32).at[owners, slot_rank].set(source_block)
-    )
-    received, recv_index = (
-        lax.all_to_all(
-            send_terms.astype(jnp.bfloat16), "rows", split_axis=0, concat_axis=0, tiled=True
-        ).astype(send_terms.dtype),
-        lax.all_to_all(send_index, "rows", split_axis=0, concat_axis=0, tiled=True),
-    )
-    placing = (recv_index[:, :, None] == local_ids[None, None, :]).astype(jnp.float32)
-    filled = (jnp.abs(received).sum(axis=(2, 3)) >= 0.0).astype(jnp.float32)
+    received = lax.all_to_all(send_terms, "rows", split_axis=0, concat_axis=0, tiled=True)
+    placing = (wanted[:, :, None] == local_ids[None, None, :]).astype(jnp.float32)
     feature_grad = jnp.einsum(
-        "scb,scif->bif", placing * filled[:, :, None], received, precision=lax.Precision.HIGHEST
+        "scb,scif->bif", placing, received.astype(jnp.float32), precision=lax.Precision.HIGHEST
     ).reshape(local_rows, col_width)
     return (activated.astype(jnp.bfloat16), weight_grad, feature_grad.astype(jnp.bfloat16))
 

time: 591 us -> 375 us (0.63)
  the two profiles are of different devices: /device:TPU:1 before, /device:TPU:8 now
where the time goes in v1:
time: 375 us; the launch traced here: 374 us
  waiting for transfers between devices  148 us (39%)
  blocking collectives  103 us (27%)
  starting transfers between devices  56.2 us (15%)
  local copies, waits for them, and re-layouts  33.4 us (9%)
  matrix products  14.4 us (4%)
  between operations  14.2 us (4%)
    all_to_all x1, blocking collectives, per_device(): lax.all_to_all(outgoing, 'rows', split_axis=0, concat_axis=0, tiled=True)  103 us
    all_to_all x1, waiting for transfers between devices, per_device(): lax.all_to_all(send_terms, 'rows', split_axis=0, concat_axis=0, tiled=True)  95.6 us
    all_gather x1, waiting for transfers between devices, per_device(): aggregated_all = lax.all_gather(aggregated, 'cols', axis=1, tiled=True)  24.1 us
    all_to_all x1, starting transfers between devices, per_device(): lax.all_to_all(request, 'rows', split_axis=0, concat_axis=0, tiled=True)  18.7 us
    all_to_all x1, waiting for transfers between devices, row_all_reduce(): lax.all_to_all(pieces, 'rows', split_axis=0, concat_axis=0, tiled=True)  16 us
    all_to_all x1, starting transfers between devices, row_all_reduce(): lax.all_to_all(pieces, 'rows', split_axis=0, concat_axis=0, tiled=True)  15.7 us
    all_to_all x1, starting transfers between devices, per_device(): lax.all_to_all(send_terms, 'rows', split_axis=0, concat_axis=0, tiled=True)  15.3 us
    scatter x2, local copies, waits for them, and re-layouts, per_device(): send_terms = jnp.zeros((row_devices, capacity, block_size, col_width), jn...  13.9 us
  transfers between devices with their start and end apart: 6, of which 4 were waited for; matrix products, arithmetic and copies ran while one was open for 7% of the time, Pallas kernels for 0%

profile of v1, /device:TPU:8, one launch (start us, length us, event | category | flops | bytes accessed | tf_op | source)
XLA Modules:
  0.0 373.5 jit_solution(1679379320810689495)
XLA Ops:
  7.2 0.0 copy-start
  7.2 1.0 convert_reduce_fusion
  8.2 0.7 fusion.30
  8.9 5.7 %scatter_fusion = s32[64,2]{0,1:T(2,128)S(1)} fusion(s32[64,2]{0,1:T(2,128)S(1)} %broadcast.59, s32[64]{0:T(128)S(1)} %get-tuple-element.15, s32[64]{0:T(128)} %param.12), kind=kCustom, calls=%fused_computation.3 | custom fusion | bytes 1280 | tf_op jit(solution)/shard_map/scatter | solution.py:35
  14.6 0.7 copy.35
  15.3 18.7 %all-to-all-start = ((s32[64,1,2]{2,1,0:T(1,128)}), s32[64,1,2]{2,1,0:T(1,128)S(1)}, u32[]{:S(2)}, u32[]{:S(2)}) async-start(s32[64,1,2]{2,1,0:T(1,128)} %copy.35), calls=%async_computation | async-start | bytes 65536 | tf_op jit(solution)/shard_map/all_to_all | solution.py:36
  34.1 0.0 all-gather.3.cloned.1.call-start
  34.1 0.9 copy_bitcast_fusion.3
  35.0 12.5 %all-to-all-done = s32[64,1,2]{2,1,0:T(1,128)S(1)} async-done(((s32[64,1,2]{2,1,0:T(1,128)}), s32[64,1,2]{2,1,0:T(1,128)S(1)}, u32[]{:S(2)}, u32[]{:S(2)}) %all-to-all-start) | async-done | bytes 544 | tf_op jit(solution)/shard_map/all_to_all | solution.py:36
  47.5 0.1 copy.36
  47.6 0.1 copy.37
  47.7 0.1 reshape.80
  47.8 2.2 gather_fusion
  50.0 103.5 %all_to_all.32 = bf16[64,2,128,64]{2,3,1,0:T(8,128)(2,1)} all-to-all(bf16[64,2,128,64]{2,3,1,0:T(8,128)(2,1)} %bitcast.71), channel_id=1, replica_groups=mesh['rows'=64,'cols'=8] {'rows'}, dimensions={0} | all-to-all | bytes 4194304 | tf_op jit(solution)/shard_map/all_to_all | solution.py:39
  153.5 2.4 gather_fusion.1
  155.9 1.5 convolution_bitcast_fusion
  157.4 0.0 copy-start.4
  157.4 2.0 fusion.11
  159.4 0.7 copy.67
  160.1 0.0 all-gather.3.cloned.1.call-update
  160.1 0.0 all-gather.5.cloned.1.call-start
  160.2 24.1 %all-gather.3.cloned.1.call-done = bf16[1024,512]{0,1:T(8,128)(2,1)} async-done(((bf16[1024,64]{0,1:T(8,128)(2,1)}), bf16[1024,512]{0,1:T(8,128)(2,1)}) %all-gather.3.cloned.1.call-update) | async-done | bytes 1048592 | tf_op jit(solution)/shard_map/all_gather | solution.py:46
  184.2 2.5 multiply_convert_fusion
  186.7 0.0 all-gather.5.cloned.1.call-update
  186.8 1.3 convolution_bitcast_fusion.1
  188.1 0.8 reshape.117
  189.0 15.7 %all-to-all-start.2 = ((f32[64,1,512]{2,1,0:T(1,128)}), f32[64,1,512]{2,1,0:T(1,128)S(1)}, u32[]{:S(2)}, u32[]{:S(2)}) async-start(f32[64,1,512]{2,1,0:T(1,128)} %reshape.117), calls=%async_computation.2 | async-start | bytes 262144 | tf_op jit(solution)/shard_map/all_to_all | solution.py:19
  204.7 16.0 %all-to-all-done.2 = f32[64,1,512]{2,1,0:T(1,128)S(1)} async-done(((f32[64,1,512]{2,1,0:T(1,128)}), f32[64,1,512]{2,1,0:T(1,128)S(1)}, u32[]{:S(2)}, u32[]{:S(2)}) %all-to-all-start.2) | async-done | bytes 131104 | tf_op jit(solution)/shard_map/all_to_all | solution.py:19
  220.7 0.5 broadcast.157
  221.3 0.9 reduce
  222.2 0.1 reshape.118
  222.3 0.1 reduce_sum.22
  222.4 0.8 reshape.119
  223.2 6.3 %all-to-all-start.3 = ((f32[64,1,512]{2,1,0:T(1,128)}), f32[64,1,512]{2,1,0:T(1,128)S(1)}, u32[]{:S(2)}, u32[]{:S(2)}) async-start(f32[64,1,512]{2,1,0:T(1,128)} %reshape.119), calls=%async_computation.3 | async-start | bytes 262144 | tf_op jit(solution)/shard_map/all_to_all | solution.py:22
  229.6 0.0 all-gather.5.cloned.1.call-done
  229.6 1.6 fusion.14
  231.2 0.7 gather_fusion.2
  231.9 1.7 fusion.4
  233.6 1.8 broadcast_in_dim.7
  235.4 8.9 %scatter_fusion.1 = bf16[64,2,128,64]{2,3,1,0:T(8,128)(2,1)} fusion(bf16[64,2,128,64]{2,3,1,0:T(8,128)(2,1)} %broadcast_in_dim.7, s32[64]{0:T(128)S(1)} %get-tuple-element.15, bf16[64,128,64]{1,2,0:T(8,128)(2,1)S(1)} %copy-done.1), kind=kCustom, calls=%fused_computation.4 | custom fusion | bytes 3146240 | tf_op jit(solution)/shard_map/scatter | solution.py:73
  244.3 5.1 %copy.43 = bf16[64,2,128,64]{2,1,3,0:T(2,128)(2,1)} copy(bf16[64,2,128,64]{2,3,1,0:T(8,128)(2,1)} %scatter_fusion.1) | data formatting | bytes 4194304 | tf_op jit(solution)/shard_map/scatter | solution.py:73
  249.4 15.3 %all-to-all-start.4 = ((bf16[64,2,128,64]{2,1,3,0:T(2,128)(2,1)}), bf16[64,2,128,64]{2,1,3,0:T(2,128)(2,1)}, u32[]{:S(2)}, u32[]{:S(2)}) async-start(bf16[64,2,128,64]{2,1,3,0:T(2,128)(2,1)} %copy.43), calls=%async_computation.4 | async-start | bytes 4194304 | tf_op jit(solution)/shard_map/all_to_all | solution.py:75
  264.7 0.9 reduce.1
  265.7 0.1 reshape.120
  265.8 0.8 copy.45
  266.6 95.6 %all-to-all-done.4 = bf16[64,2,128,64]{2,1,3,0:T(2,128)(2,1)} async-done(((bf16[64,2,128,64]{2,1,3,0:T(2,128)(2,1)}), bf16[64,2,128,64]{2,1,3,0:T(2,128)(2,1)}, u32[]{:S(2)}, u32[]{:S(2)}) %all-to-all-start.4) | async-done | bytes 2097184 | tf_op jit(solution)/shard_map/all_to_all | solution.py:75
  362.1 3.9 %fusion.8 = bf16[8,128,64]{1,0,2:T(8,128)(2,1)S(1)} fusion(bf16[64,2,128,64]{2,1,3,0:T(2,128)(2,1)} %all-to-all-done.4, s32[64,2]{0,1:T(2,128)S(1)} %bitcast.77), kind=kOutput, calls=%fused_computation.14 | convolution fusion | flops 16843776 | bytes 2228736 | tf_op jit(solution)/shard_map/scb,scif->bif/dot_general | solution.py:77
  366.0 0.7 copy.66
  (18 shorter events, 0.1 us)
Async XLA Ops:
  7.2 148.7 %copy-start = (bf16[64,128,128]{2,1,0:T(8,128)(2,1)S(1)}, bf16[64,128,128]{2,1,0:T(8,128)(2,1)}, u32[]{:S(2)}) copy-start(bf16[64,128,128]{2,1,0:T(8,128)(2,1)} %param.9) | copy-start | bytes 6291460
  15.3 32.2 %all-to-all-start = ((s32[64,1,2]{2,1,0:T(1,128)}), s32[64,1,2]{2,1,0:T(1,128)S(1)}, u32[]{:S(2)}, u32[]{:S(2)}) async-start(s32[64,1,2]{2,1,0:T(1,128)} %copy.35), calls=%async_computation | async-start | bytes 65536 | tf_op jit(solution)/shard_map/all_to_all | solution.py:36
  34.1 150.2 %all-gather.3.cloned.1.call-start = ((), (), s32[]{:S(2)}) async-start(), calls=%async_computation.5 | async-start | bytes 1179648 | tf_op jit(solution)/shard_map/all_gather | solution.py:46
  155.9 1.5 copy-start.3
  157.4 26.8 %copy-start.4 = (s32[1024]{0:T(1024)S(1)}, s32[1024]{0:T(1024)}, u32[]{:S(2)}) copy-start(s32[1024]{0:T(1024)} %param.13) | copy-start | bytes 12292
  160.1 69.5 %all-gather.5.cloned.1.call-start = ((), (), s32[]{:S(2)}) async-start(), calls=%async_computation.6 | async-start | bytes 1179648 | tf_op jit(solution)/shard_map/all_gather | solution.py:57
  184.2 2.5 copy-start.2
  189.0 31.8 %all-to-all-start.2 = ((f32[64,1,512]{2,1,0:T(1,128)}), f32[64,1,512]{2,1,0:T(1,128)S(1)}, u32[]{:S(2)}, u32[]{:S(2)}) async-start(f32[64,1,512]{2,1,0:T(1,128)} %reshape.117), calls=%async_computation.2 | async-start | bytes 262144 | tf_op jit(solution)/shard_map/all_to_all | solution.py:19
  223.2 26.2 %all-to-all-start.3 = ((f32[64,1,512]{2,1,0:T(1,128)}), f32[64,1,512]{2,1,0:T(1,128)S(1)}, u32[]{:S(2)}, u32[]{:S(2)}) async-start(f32[64,1,512]{2,1,0:T(1,128)} %reshape.119), calls=%async_computation.3 | async-start | bytes 262144 | tf_op jit(solution)/shard_map/all_to_all | solution.py:22
  233.6 1.8 copy-start.1
  249.4 112.7 %all-to-all-start.4 = ((bf16[64,2,128,64]{2,1,3,0:T(2,128)(2,1)}), bf16[64,2,128,64]{2,1,3,0:T(2,128)(2,1)}, u32[]{:S(2)}, u32[]{:S(2)}) async-start(bf16[64,2,128,64]{2,1,3,0:T(2,128)(2,1)} %copy.43), calls=%async_computation.4 | async-start | bytes 4194304 | tf_op jit(solution)/shard_map/all_to_all | solution.py:75
Sparse Core Ops, SparseCore 0:
  160.2 23.9 all-gather.2
  187.0 30.9 all-gather.4

commit v2 on v1

--- a/solution.py
+++ b/solution.py
@@ -1,9 +1,70 @@
+import functools
 import math
 
 import jax
 import jax.numpy as jnp
 from jax import lax
+from jax.experimental import pallas as pl
+from jax.experimental.pallas import tpu as pltpu
 from jax.sharding import PartitionSpec as P
+
+MESH = pl.DeviceIdType.MESH
+
+
+def _a2a_kernel(x_hbm, o_hbm, send_sems, recv_sems, local_sem):
+    n = x_hbm.shape[0]
+    me = lax.axis_index("rows")
+    barrier = pltpu.get_barrier_semaphore()
+
+    def greet(k, carry):
+        peer = lax.rem(me + k, n)
+        pl.semaphore_signal(barrier, 1, device_id={"rows": peer}, device_id_type=MESH)
+        return carry
+
+    lax.fori_loop(1, n, greet, 0)
+    pl.semaphore_wait(barrier, n - 1)
+    local = pltpu.make_async_copy(x_hbm.at[me], o_hbm.at[me], local_sem)
+    local.start()
+
+    def outgoing(peer):
+        return pltpu.make_async_remote_copy(
+            src_ref=x_hbm.at[peer], dst_ref=o_hbm.at[me], send_sem=send_sems.at[peer],
+            recv_sem=recv_sems.at[me], device_id={"rows": peer}, device_id_type=MESH)
+
+    def incoming(src):
+        return pltpu.make_async_remote_copy(
+            src_ref=x_hbm.at[src], dst_ref=o_hbm.at[src], send_sem=send_sems.at[src],
+            recv_sem=recv_sems.at[src], device_id={"rows": src}, device_id_type=MESH)
+
+    def start(k, carry):
+        outgoing(lax.rem(me + k, n)).start()
+        return carry
+
+    lax.fori_loop(1, n, start, 0)
+
+    def finish(k, carry):
+        outgoing(lax.rem(me + k, n)).wait_send()
+        incoming(lax.rem(me + n - k, n)).wait_recv()
+        return carry
+
+    lax.fori_loop(1, n, finish, 0)
+    local.wait()
+
+
+def rows_all_to_all(x, collective_id):
+    n = x.shape[0]
+    return pl.pallas_call(
+        _a2a_kernel,
+        out_shape=jax.ShapeDtypeStruct(x.shape, x.dtype),
+        in_specs=[pl.BlockSpec(memory_space=pl.ANY)],
+        out_specs=pl.BlockSpec(memory_space=pl.ANY),
+        scratch_shapes=[
+            pltpu.SemaphoreType.DMA((n,)),
+            pltpu.SemaphoreType.DMA((n,)),
+            pltpu.SemaphoreType.DMA(()),
+        ],
+        compiler_params=pltpu.CompilerParams(collective_id=collective_id, has_side_effects=True),
+    )(x)
 
 
 def slot_ranks(owners):
@@ -35,8 +96,8 @@
     request = jnp.zeros((row_devices, capacity), jnp.int32).at[owners, slot_rank].set(source_block)
     wanted = lax.all_to_all(request, "rows", split_axis=0, concat_axis=0, tiled=True)
     own_blocks = node_features.reshape(local_blocks, block_size, col_width)
-    outgoing = own_blocks[wanted]
-    incoming = lax.all_to_all(outgoing, "rows", split_axis=0, concat_axis=0, tiled=True)
+    outgoing = own_blocks[wanted].reshape(row_devices, block_size, capacity * col_width)
+    incoming = rows_all_to_all(outgoing, 0).reshape(row_devices, capacity, block_size, col_width)
     source_rows = incoming[owners, slot_rank]
     products = jnp.einsum(
         "tij,tjf->tif", tile_values, source_rows, preferred_element_type=jnp.float32
@@ -72,7 +133,9 @@
         .at[owners, slot_rank]
         .set(sent_terms.astype(jnp.bfloat16))
     )
-    received = lax.all_to_all(send_terms, "rows", split_axis=0, concat_axis=0, tiled=True)
+    received = rows_all_to_all(
+        send_terms.reshape(row_devices, block_size, capacity * col_width), 1
+    ).reshape(row_devices, capacity, block_size, col_width)
     placing = (wanted[:, :, None] == local_ids[None, None, :]).astype(jnp.float32)
     feature_grad = jnp.einsum(
         "scb,scif->bif", placing, received.astype(jnp.float32), precision=lax.Precision.HIGHEST

time: 375 us -> 415 us (1.11)
  the two profiles are of different devices: /device:TPU:8 before, /device:TPU:1 now
where the time goes in v2:
time: 415 us; the launch traced here: 413 us
  Pallas kernels  200 us (48%)
  local copies, waits for them, and re-layouts  69.5 us (17%)
  waiting for transfers between devices  55.4 us (13%)
  blocking collectives  29.6 us (7%)
  starting transfers between devices  26.7 us (6%)
  between operations  14.2 us (3%)
  matrix products  14.1 us (3%)
    pallas_call x2, Pallas kernels, rows_all_to_all(): pl.pallas_call(_a2a_kernel, out_shape=jax.ShapeDtypeStruct(x.shape, x.dty...  200 us
    all_to_all x1, blocking collectives, row_all_reduce(): lax.all_to_all(pieces, 'rows', split_axis=0, concat_axis=0, tiled=True)  29.6 us
    all_gather x1, waiting for transfers between devices, per_device(): aggregated_all = lax.all_gather(aggregated, 'cols', axis=1, tiled=True)  29.3 us
    all_to_all x1, starting transfers between devices, per_device(): lax.all_to_all(request, 'rows', split_axis=0, concat_axis=0, tiled=True)  19.3 us
    all_to_all x1, waiting for transfers between devices, row_all_reduce(): lax.all_to_all(spread, 'rows', split_axis=0, concat_axis=0, tiled=True)  13.8 us
    scatter x2, local copies, waits for them, and re-layouts, per_device(): send_terms = jnp.zeros((row_devices, capacity, block_size, col_width), jn...  13.6 us
    all_to_all x1, waiting for transfers between devices, per_device(): lax.all_to_all(request, 'rows', split_axis=0, concat_axis=0, tiled=True)  12.2 us
    reshape x2, local copies, waits for them, and re-layouts, per_device(): received = rows_all_to_all(send_terms.reshape(row_devices, block_size, ca...  11.7 us
  transfers between devices with their start and end apart: 4, of which 3 were waited for; matrix products, arithmetic and copies ran while one was open for 2% of the time, Pallas kernels for 0%

profile of v2, /device:TPU:1, one launch (start us, length us, event | category | flops | bytes accessed | tf_op | source)
XLA Modules:
  0.0 413.0 jit_solution(14140683473685628017)
XLA Ops:
  7.2 1.0 convert_reduce_fusion
  8.2 0.7 fusion.23
  8.9 5.8 %scatter_fusion = s32[64,2]{0,1:T(2,128)S(1)} fusion(s32[64,2]{0,1:T(2,128)S(1)} %broadcast.59, s32[64]{0:T(128)S(1)} %get-tuple-element.15, s32[64]{0:T(128)} %param.12), kind=kCustom, calls=%fused_computation.3 | custom fusion | bytes 1280 | tf_op jit(solution)/shard_map/scatter | solution.py:96
  14.6 0.7 copy.43
  15.3 19.3 %all-to-all-start = ((s32[64,1,2]{2,1,0:T(1,128)}), s32[64,1,2]{2,1,0:T(1,128)S(1)}, u32[]{:S(2)}, u32[]{:S(2)}) async-start(s32[64,1,2]{2,1,0:T(1,128)} %copy.43), calls=%async_computation | async-start | bytes 65536 | tf_op jit(solution)/shard_map/all_to_all | solution.py:97
  34.6 0.0 all-gather.3.cloned.1.call-start
  34.7 0.9 copy_bitcast_fusion.3
  35.6 12.2 %all-to-all-done = s32[64,1,2]{2,1,0:T(1,128)S(1)} async-done(((s32[64,1,2]{2,1,0:T(1,128)}), s32[64,1,2]{2,1,0:T(1,128)S(1)}, u32[]{:S(2)}, u32[]{:S(2)}) %all-to-all-start) | async-done | bytes 544 | tf_op jit(solution)/shard_map/all_to_all | solution.py:97
  47.8 0.1 copy.44
  47.9 0.1 copy.45
  48.0 0.1 reshape.96
  48.2 2.1 gather_fusion
  50.3 4.8 %copy.47 = bf16[128,128,64]{2,1,0:T(8,128)(2,1)} copy(bf16[128,128,64]{1,2,0:T(8,128)(2,1)} %gather_fusion) | data formatting | bytes 4194304 | tf_op jit(solution)/shard_map/gather | solution.py:99
  55.1 6.2 %reshape.88.x_hbm = bf16[64,128,128]{2,1,0:T(8,128)(2,1)} reshape(bf16[128,128,64]{2,1,0:T(8,128)(2,1)} %copy.47) | data formatting | bytes 4194304 | tf_op jit(solution)/shard_map/reshape | solution.py:99
  61.3 98.1 %shard_map.94 = bf16[64,128,128]{2,1,0:T(8,128)(2,1)} custom-call(bf16[64,128,128]{2,1,0:T(8,128)(2,1)} %reshape.88.x_hbm), custom_call_target="tpu_custom_call" | custom-call | tf_op jit(solution)/shard_map/pallas_call | solution.py:56
  159.4 6.1 %reshape.89 = bf16[64,2,128,64]{3,2,1,0:T(8,128)(2,1)} reshape(bf16[64,128,128]{2,1,0:T(8,128)(2,1)} %shard_map.94) | data formatting | bytes 4194304 | tf_op jit(solution)/shard_map/reshape | solution.py:100
  165.5 4.3 %gather_fusion.1 = bf16[64,128,64]{2,1,0:T(8,128)(2,1)} fusion(bf16[64,2,128,64]{3,2,1,0:T(8,128)(2,1)} %reshape.89, s32[64]{0:T(128)S(1)} %bitcast.73), kind=kCustom, calls=%fused_computation.1 | custom fusion | bytes 2097664 | tf_op jit(solution)/shard_map/gather | solution.py:101
  169.8 3.1 convolution_bitcast_fusion
  173.0 2.0 fusion.4
  174.9 0.7 copy.72
  175.6 0.0 all-gather.5.cloned.1.call-start
  175.7 29.3 %all-gather.3.cloned.1.call-done = bf16[1024,512]{0,1:T(8,128)(2,1)} async-done(((bf16[1024,64]{0,1:T(8,128)(2,1)}), bf16[1024,512]{0,1:T(8,128)(2,1)}) %all-gather.3.cloned.1.call-update) | async-done | bytes 1048592 | tf_op jit(solution)/shard_map/all_gather | solution.py:107
  205.0 2.5 multiply_convert_fusion
  207.6 1.3 convolution_bitcast_fusion.2
  208.9 0.2 reshape.134
  209.1 29.6 %all_to_all.22 = f32[64,1,512]{2,1,0:T(1,128)S(1)} all-to-all(f32[64,1,512]{2,1,0:T(1,128)S(1)} %reshape.134), channel_id=1, replica_groups=mesh['rows'=64,'cols'=8] {'rows'}, dimensions={0} | all-to-all | bytes 262144 | tf_op jit(solution)/shard_map/all_to_all | solution.py:80
  238.7 0.5 broadcast.157
  239.2 0.9 reduce
  240.2 0.1 reshape.135
  240.3 0.1 reduce_sum.22
  240.4 0.8 reshape.136
  241.2 7.3 %all-to-all-start.2 = ((f32[64,1,512]{2,1,0:T(1,128)}), f32[64,1,512]{2,1,0:T(1,128)S(1)}, u32[]{:S(2)}, u32[]{:S(2)}) async-start(f32[64,1,512]{2,1,0:T(1,128)} %reshape.136), calls=%async_computation.2 | async-start | bytes 262144 | tf_op jit(solution)/shard_map/all_to_all | solution.py:83
  248.5 13.8 %all-to-all-done.2 = f32[64,1,512]{2,1,0:T(1,128)S(1)} async-done(((f32[64,1,512]{2,1,0:T(1,128)}), f32[64,1,512]{2,1,0:T(1,128)S(1)}, u32[]{:S(2)}, u32[]{:S(2)}) %all-to-all-start.2) | async-done | bytes 131104 | tf_op jit(solution)/shard_map/all_to_all | solution.py:83
  262.4 0.9 reduce.1
  263.3 0.1 reshape.137
  263.5 0.8 copy.55
  264.2 1.6 fusion.7
  265.8 0.7 gather_fusion.2
  266.6 1.7 fusion.2
  268.3 1.8 broadcast_in_dim.7
  270.1 8.9 %scatter_fusion.1 = bf16[64,2,128,64]{2,3,1,0:T(8,128)(2,1)} fusion(bf16[64,2,128,64]{2,3,1,0:T(8,128)(2,1)} %broadcast_in_dim.7, s32[64]{0:T(128)S(1)} %get-tuple-element.15, bf16[64,128,64]{1,2,0:T(8,128)(2,1)S(1)} %copy-done.1), kind=kCustom, calls=%fused_computation.4 | custom fusion | bytes 3146240 | tf_op jit(solution)/shard_map/scatter | solution.py:134
  279.0 4.8 %copy.53 = bf16[64,2,128,64]{3,2,1,0:T(8,128)(2,1)} copy(bf16[64,2,128,64]{2,3,1,0:T(8,128)(2,1)} %scatter_fusion.1) | data formatting | bytes 4194304 | tf_op jit(solution)/shard_map/scatter | solution.py:134
  283.7 6.2 %reshape.92.x_hbm = bf16[64,128,128]{2,1,0:T(8,128)(2,1)} reshape(bf16[64,2,128,64]{3,2,1,0:T(8,128)(2,1)} %copy.53) | data formatting | bytes 4194304 | tf_op jit(solution)/shard_map/reshape | solution.py:137
  290.0 101.7 %shard_map.95 = bf16[64,128,128]{2,1,0:T(8,128)(2,1)} custom-call(bf16[64,128,128]{2,1,0:T(8,128)(2,1)} %reshape.92.x_hbm), custom_call_target="tpu_custom_call" | custom-call | tf_op jit(solution)/shard_map/pallas_call | solution.py:56
  391.7 6.1 %reshape.93 = bf16[64,2,128,64]{3,2,1,0:T(8,128)(2,1)} reshape(bf16[64,128,128]{2,1,0:T(8,128)(2,1)} %shard_map.95) | data formatting | bytes 4194304 | tf_op jit(solution)/shard_map/reshape | solution.py:138
  397.8 5.6 %copy.54 = bf16[64,2,128,64]{2,0,1,3:T(8,128)(2,1)} copy(bf16[64,2,128,64]{3,2,1,0:T(8,128)(2,1)} %reshape.93) | data formatting | bytes 4194304 | tf_op jit(solution)/shard_map/reshape | solution.py:138
  403.5 2.0 fusion.3
  405.5 0.7 copy.71
  (22 shorter events, 0.2 us)
Async XLA Ops:
  7.2 162.7 %copy-start = (bf16[64,128,128]{2,1,0:T(8,128)(2,1)S(1)}, bf16[64,128,128]{2,1,0:T(8,128)(2,1)}, u32[]{:S(2)}) copy-start(bf16[64,128,128]{2,1,0:T(8,128)(2,1)} %param.9) | copy-start | bytes 6291460
  15.3 32.5 %all-to-all-start = ((s32[64,1,2]{2,1,0:T(1,128)}), s32[64,1,2]{2,1,0:T(1,128)S(1)}, u32[]{:S(2)}, u32[]{:S(2)}) async-start(s32[64,1,2]{2,1,0:T(1,128)} %copy.43), calls=%async_computation | async-start | bytes 65536 | tf_op jit(solution)/shard_map/all_to_all | solution.py:97
  34.6 170.4 %all-gather.3.cloned.1.call-start = ((), (), s32[]{:S(2)}) async-start(), calls=%async_computation.3 | async-start | bytes 1179648 | tf_op jit(solution)/shard_map/all_gather | solution.py:107
  169.8 3.1 copy-start.3
  173.0 32.1 %copy-start.4 = (s32[1024]{0:T(1024)S(1)}, s32[1024]{0:T(1024)}, u32[]{:S(2)}) copy-start(s32[1024]{0:T(1024)} %param.13) | copy-start | bytes 12292
  175.6 88.6 %all-gather.5.cloned.1.call-start = ((), (), s32[]{:S(2)}) async-start(), calls=%async_computation.4 | async-start | bytes 1179648 | tf_op jit(solution)/shard_map/all_gather | solution.py:118
  205.0 2.5 copy-start.2
  241.2 21.2 %all-to-all-start.2 = ((f32[64,1,512]{2,1,0:T(1,128)}), f32[64,1,512]{2,1,0:T(1,128)S(1)}, u32[]{:S(2)}, u32[]{:S(2)}) async-start(f32[64,1,512]{2,1,0:T(1,128)} %reshape.136), calls=%async_computation.2 | async-start | bytes 262144 | tf_op jit(solution)/shard_map/all_to_all | solution.py:83
  268.3 1.8 copy-start.1
Sparse Core Ops, SparseCore 0:
  175.8 29.2 all-gather.2
  207.7 30.7 all-gather.4

commit v3 on v1

v3 whole, which is shorter than its diff:
```python
import math

import jax
import jax.numpy as jnp
from jax import lax
from jax.sharding import PartitionSpec as P


def slot_ranks(owners):
    positions = jnp.arange(owners.shape[0], dtype=jnp.int32)
    earlier = (owners[:, None] == owners[None, :]) & (positions[None, :] < positions[:, None])
    return jnp.sum(earlier.astype(jnp.int32), axis=1)


def rows_exchange(x):
    return lax.all_to_all(x, "rows", split_axis=0, concat_axis=0, tiled=True)


def row_all_reduce(partial):
    row_devices = lax.axis_size("rows")
    k, c = partial.shape
    pieces = partial.reshape(row_devices, k // row_devices, c)
    reduced = jnp.sum(rows_exchange(pieces), axis=0)
    spread = jnp.broadcast_to(reduced[None], (row_devices,) + reduced.shape)
    return rows_exchange(spread).reshape(k, c)


def per_device(node_features, weight, tile_values, tile_row, source_owner, source_block, labels):
    local_rows, col_width = node_features.shape
    block_size = tile_values.shape[1]
    local_blocks = local_rows // block_size
    row_devices = lax.axis_size("rows")
    col_devices = lax.axis_size("cols")
    tiles = tile_values.shape[0]
    capacity = 2 * tiles // row_devices
    half = col_width // 2
    owners = source_owner[:, 0]
    slot_rank = slot_ranks(owners)
    local_ids = jnp.arange(local_blocks, dtype=jnp.int32)
    row_onehot = (tile_row[:, None] == local_ids[None, :]).astype(jnp.float32)
    request = jnp.zeros((row_devices, capacity), jnp.int32).at[owners, slot_rank].set(source_block)
    wanted = rows_exchange(request)
    own_blocks = node_features.reshape(local_blocks, block_size, col_width)
    outgoing = own_blocks[wanted]
    col_index = lax.axis_index("cols")
    w_columns = lax.dynamic_slice_in_dim(weight, col_index * col_width, col_width, 1)
    w_rows = lax.dynamic_slice_in_dim(weight, col_index * col_width, col_width, 0)
    w_split = w_columns.reshape(col_devices, col_width, col_width)

    def aggregate(part):
        source_rows = part[owners, slot_rank]
        products = jnp.einsum(
            "tij,tjf->tif", tile_values, source_rows, preferred_element_type=jnp.float32
        )
        summed = jnp.einsum("tb,tif->bif", row_onehot, products, precision=lax.Precision.HIGHEST)
        return summed.reshape(local_rows, part.shape[-1]).astype(jnp.bfloat16)

    first = aggregate(rows_exchange(outgoing[..., :half]))
    second_out, first = lax.optimization_barrier((outgoing[..., half:], first))
    first_all = lax.all_gather(first, "cols", axis=0, tiled=False)
    second = aggregate(rows_exchange(second_out))
    second_all = lax.all_gather(second, "cols", axis=0, tiled=False)
    hidden = jnp.einsum(
        "jnf,jfc->nc", first_all, w_split[:, :half], preferred_element_type=jnp.float32
    ) + jnp.einsum(
        "jnf,jfc->nc", second_all, w_split[:, half:], preferred_element_type=jnp.float32
    )
    sigmoid = jax.nn.sigmoid(hidden)
    activated = hidden * sigmoid
    slopes = sigmoid * (1.0 + hidden * (1.0 - sigmoid))
    feature_ids = col_index * col_width + jnp.arange(col_width, dtype=jnp.int32)
    target = (labels[:, None] == feature_ids[None, :]).astype(jnp.float32)
    out_grad = ((activated - target) * slopes).astype(jnp.bfloat16)
    grad_all = lax.all_gather(out_grad, "cols", axis=1, tiled=True)
    weight_terms = jnp.concatenate(
        [
            jnp.einsum("jnf,nc->jfc", first_all, out_grad, preferred_element_type=jnp.float32),
            jnp.einsum("jnf,nc->jfc", second_all, out_grad, preferred_element_type=jnp.float32),
        ],
        axis=1,
    ).reshape(col_devices * col_width, col_width)
    node_total = local_rows * row_devices
    weight_grad = row_all_reduce(weight_terms) / math.sqrt(node_total)
    agg_grad = jnp.einsum("nc,kc->nk", grad_all, w_rows, preferred_element_type=jnp.float32).astype(
        jnp.bfloat16
    )
    grad_rows = agg_grad.reshape(local_blocks, block_size, col_width)[tile_row]
    sent_terms = jnp.einsum(
        "tji,tjf->tif", tile_values, grad_rows, preferred_element_type=jnp.float32
    ).astype(jnp.bfloat16)
    slot_tile = (
        jnp.full((row_devices, capacity), tiles, jnp.int32)
        .at[owners, slot_rank]
        .set(jnp.arange(tiles, dtype=jnp.int32))
    )
    padded_terms = jnp.concatenate([sent_terms, jnp.zeros_like(sent_terms[:1])], axis=0)
    received = rows_exchange(padded_terms[slot_tile])
    placing = (wanted[:, :, None] == local_ids[None, None, :]).astype(jnp.float32)
    feature_grad = jnp.einsum(
        "scb,scif->bif", placing, received.astype(jnp.float32), precision=lax.Precision.HIGHEST
    ).reshape(local_rows, col_width)
    return (activated.astype(jnp.bfloat16), weight_grad, feature_grad.astype(jnp.bfloat16))


def solution(mesh):
    return jax.shard_map(
        per_device,
        mesh=mesh,
        in_specs=(
            P("rows", "cols"),
            P(),
            P("rows", None, None),
            P("rows"),
            P("rows", None),
            P("rows"),
            P("rows"),
        ),
        out_specs=(P("rows", "cols"), P(None, "cols"), P("rows", "cols")),
        check_vma=False,
    )
```

time: 375 us -> 368 us (0.981)
  waiting for transfers between devices: 148 us -> 168 us
  blocking collectives: 103 us -> 84.8 us
  starting transfers between devices: 56.2 us -> 49.6 us
    all_to_all x1, blocking collectives: 103 us -> 57.7 us  [rows_exchange(): return lax.all_to_all(x, 'rows', split_axis=0, concat_axis=0, tiled=True)]
    all_to_all x4 -> x5, waiting for transfers between devices: 124 us -> 168 us  [rows_exchange(): return lax.all_to_all(x, 'rows', split_axis=0, concat_axis=0, tiled=True)]
    all_gather x0 -> x2, blocking collectives: none -> 27.1 us  [the longest x1 13.6 us: per_device(): second_all = lax.all_gather(second, 'cols', axis=0, tiled=False)]
    all_gather x1 -> x0, waiting for transfers between devices: 24.1 us -> none  [per_device(): aggregated_all = lax.all_gather(aggregated, 'cols', axis=1, tiled=True)]
    scatter x2 -> x1, local copies, waits for them, and re-layouts: 13.9 us -> 3.5 us  [per_device(): slot_tile = jnp.full((row_devices, capacity), tiles, jnp.int32).at[owners...]
    gather x1 -> x4, local copies, waits for them, and re-layouts: 2.39 us -> 11.1 us  [the longest x2 7.2 us: per_device(): received = rows_exchange(padded_terms[slot_tile])]
    all_to_all x4 -> x5, starting transfers between devices: 56.1 us -> 49.6 us  [rows_exchange(): return lax.all_to_all(x, 'rows', split_axis=0, concat_axis=0, tiled=True)]
  transfers between devices with their start and end apart: 6 -> 6, of which waited for: 4 -> 5; matrix products, arithmetic and copies ran while one was open for 7% -> 6% of each run, Pallas kernels for 0% -> 0%
where the time goes in v3:
time: 368 us; the launch traced here: 367 us
  waiting for transfers between devices  168 us (46%)
  blocking collectives  84.8 us (23%)
  starting transfers between devices  49.6 us (13%)
  local copies, waits for them, and re-layouts  34 us (9%)
  between operations  14.4 us (4%)
  matrix products  13.4 us (4%)
  other arithmetic  3.79 us (1%)
    all_to_all x5, waiting for transfers between devices, rows_exchange(): return lax.all_to_all(x, 'rows', split_axis=0, concat_axis=0, tiled=True)  168 us
    all_to_all x1, blocking collectives, rows_exchange(): return lax.all_to_all(x, 'rows', split_axis=0, concat_axis=0, tiled=True)  57.7 us
    all_to_all x5, starting transfers between devices, rows_exchange(): return lax.all_to_all(x, 'rows', split_axis=0, concat_axis=0, tiled=True)  49.6 us
    all_gather x1, blocking collectives, per_device(): second_all = lax.all_gather(second, 'cols', axis=0, tiled=False)  13.6 us
    all_gather x1, blocking collectives, per_device(): first_all = lax.all_gather(first, 'cols', axis=0, tiled=False)  13.5 us
  transfers between devices with their start and end apart: 6, of which 5 were waited for; matrix products, arithmetic and copies ran while one was open for 6% of the time, Pallas kernels for 0%

profile of v3, /device:TPU:8, one launch (start us, length us, event | category | flops | bytes accessed | tf_op | source)
XLA Modules:
  0.0 367.5 jit_solution(6399955172962610033)
XLA Ops:
  7.2 1.0 convert_reduce_fusion
  8.2 0.7 fusion.33
  8.9 5.7 %scatter_fusion = s32[64,2]{0,1:T(2,128)S(1)} fusion(s32[64,2]{0,1:T(2,128)S(1)} %broadcast.61, s32[64]{0:T(128)S(1)} %get-tuple-element.22, s32[64]{0:T(128)} %param.12), kind=kCustom, calls=%fused_computation.5 | custom fusion | bytes 1280 | tf_op jit(solution)/shard_map/scatter | solution.py:41
  14.6 0.7 copy.60
  15.3 18.7 %all-to-all-start = ((s32[64,1,2]{2,1,0:T(1,128)}), s32[64,1,2]{2,1,0:T(1,128)S(1)}, u32[]{:S(2)}, u32[]{:S(2)}) async-start(s32[64,1,2]{2,1,0:T(1,128)} %copy.60), calls=%async_computation | async-start | bytes 65536 | tf_op jit(solution)/shard_map/all_to_all | solution.py:16
  34.1 0.9 copy_bitcast_fusion.2
  35.0 12.5 %all-to-all-done = s32[64,1,2]{2,1,0:T(1,128)S(1)} async-done(((s32[64,1,2]{2,1,0:T(1,128)}), s32[64,1,2]{2,1,0:T(1,128)S(1)}, u32[]{:S(2)}, u32[]{:S(2)}) %all-to-all-start) | async-done | bytes 544 | tf_op jit(solution)/shard_map/all_to_all | solution.py:16
  47.7 0.1 reshape.92
  47.8 2.1 gather_fusion
  50.0 3.0 fusion.35
  53.0 57.7 %all_to_all.37 = bf16[64,2,128,32]{2,3,1,0:T(8,128)(2,1)} all-to-all(bf16[64,2,128,32]{2,3,1,0:T(8,128)(2,1)S(1)} %get-tuple-element.24), channel_id=1, replica_groups=mesh['rows'=64,'cols'=8] {'rows'}, dimensions={0} | all-to-all | bytes 2097152 | tf_op jit(solution)/shard_map/all_to_all | solution.py:16
  110.6 2.0 gather_fusion.1
  112.6 1.2 convolution_bitcast_fusion.1
  113.8 1.1 convolution_convert_fusion.3
  114.9 7.4 %all-to-all-start.2 = ((bf16[64,2,128,32]{2,3,1,0:T(8,128)(2,1)}), bf16[64,2,128,32]{2,3,1,0:T(8,128)(2,1)}, u32[]{:S(2)}, u32[]{:S(2)}) async-start(bf16[64,2,128,32]{2,3,1,0:T(8,128)(2,1)} %get-tuple-element.6), calls=%async_computation.2 | async-start | bytes 2097152 | tf_op jit(solution)/shard_map/all_to_all | solution.py:16
  122.4 1.0 constant_dynamic-slice_fusion
  123.4 13.5 %all-gather = bf16[8192,32]{0,1:T(8,128)(2,1)S(1)} all-gather(bf16[1024,32]{0,1:T(8,128)(2,1)S(1)} %bitcast.106), channel_id=2, replica_groups=mesh['rows'=64,'cols'=8] {'cols'}, dimensions={0}, use_global_device_ids=true | all-gather | bytes 589824 | tf_op jit(solution)/shard_map/all_gather | solution.py:60
  136.9 0.3 copy.84
  137.2 38.6 %all-to-all-done.2 = bf16[64,2,128,32]{2,3,1,0:T(8,128)(2,1)} async-done(((bf16[64,2,128,32]{2,3,1,0:T(8,128)(2,1)}), bf16[64,2,128,32]{2,3,1,0:T(8,128)(2,1)}, u32[]{:S(2)}, u32[]{:S(2)}) %all-to-all-start.2) | async-done | bytes 1048608 | tf_op jit(solution)/shard_map/all_to_all | solution.py:16
  175.7 2.0 gather_fusion.2
  177.7 1.2 convolution_bitcast_fusion
  178.9 1.1 convolution_convert_fusion.2
  180.0 13.6 %all_gather.15 = bf16[8,1024,32]{1,2,0:T(8,128)(2,1)S(1)} all-gather(bf16[1,1024,32]{1,2,0:T(8,128)(2,1)S(1)} %convert_element_type.53), channel_id=1, replica_groups=mesh['rows'=64,'cols'=8] {'cols'}, dimensions={0}, use_global_device_ids=true | all-gather | bytes 589824 | tf_op jit(solution)/shard_map/all_gather | solution.py:62
  193.6 0.2 convolution_bitcast_fusion.2
  193.9 1.0 multiply_convert_fusion
  195.0 3.5 scatter_fusion.1
  198.5 1.2 fusion.15
  199.8 0.3 fusion.17
  200.2 0.8 reshape.149
  201.0 6.9 %all-to-all-start.3 = ((f32[64,1,512]{2,1,0:T(1,128)}), f32[64,1,512]{2,1,0:T(1,128)S(1)}, u32[]{:S(2)}, u32[]{:S(2)}) async-start(f32[64,1,512]{2,1,0:T(1,128)} %reshape.149), calls=%async_computation.3 | async-start | bytes 262144 | tf_op jit(solution)/shard_map/all_to_all | solution.py:16
  208.0 0.1 reshape.120
  208.1 15.9 %all-to-all-done.3 = f32[64,1,512]{2,1,0:T(1,128)S(1)} async-done(((f32[64,1,512]{2,1,0:T(1,128)}), f32[64,1,512]{2,1,0:T(1,128)S(1)}, u32[]{:S(2)}, u32[]{:S(2)}) %all-to-all-start.3) | async-done | bytes 131104 | tf_op jit(solution)/shard_map/all_to_all | solution.py:16
  224.0 0.6 broadcast.177
  224.6 1.0 reduce
  225.8 0.8 reshape.151
  226.6 6.3 %all-to-all-start.4 = ((f32[64,1,512]{2,1,0:T(1,128)}), f32[64,1,512]{2,1,0:T(1,128)S(1)}, u32[]{:S(2)}, u32[]{:S(2)}) async-start(f32[64,1,512]{2,1,0:T(1,128)} %reshape.151), calls=%async_computation.4 | async-start | bytes 262144 | tf_op jit(solution)/shard_map/all_to_all | solution.py:16
  232.9 1.6 fusion.10
  234.5 0.7 gather_fusion.3
  235.3 0.7 fusion.2
  236.1 2.1 gather_fusion.4
  238.2 5.1 %copy.74 = bf16[64,2,128,64]{2,1,3,0:T(2,128)(2,1)} copy(bf16[64,2,128,64]{2,3,1,0:T(8,128)(2,1)} %bitcast.96) | data formatting | bytes 4194304 | tf_op jit(solution)/shard_map/gather | solution.py:97
  243.3 5.0 %all-to-all-done.4 = f32[64,1,512]{2,1,0:T(1,128)S(1)} async-done(((f32[64,1,512]{2,1,0:T(1,128)}), f32[64,1,512]{2,1,0:T(1,128)S(1)}, u32[]{:S(2)}, u32[]{:S(2)}) %all-to-all-start.4) | async-done | bytes 131104 | tf_op jit(solution)/shard_map/all_to_all | solution.py:16
  248.3 10.3 %all-to-all-start.5 = ((bf16[64,2,128,64]{2,1,3,0:T(2,128)(2,1)}), bf16[64,2,128,64]{2,1,3,0:T(2,128)(2,1)}, u32[]{:S(2)}, u32[]{:S(2)}) async-start(bf16[64,2,128,64]{2,1,3,0:T(2,128)(2,1)} %copy.74), calls=%async_computation.5 | async-start | bytes 4194304 | tf_op jit(solution)/shard_map/all_to_all | solution.py:16
  258.6 1.0 reduce.1
  259.7 0.8 copy.76
  260.5 95.6 %all-to-all-done.5 = bf16[64,2,128,64]{2,1,3,0:T(2,128)(2,1)} async-done(((bf16[64,2,128,64]{2,1,3,0:T(2,128)(2,1)}), bf16[64,2,128,64]{2,1,3,0:T(2,128)(2,1)}, u32[]{:S(2)}, u32[]{:S(2)}) %all-to-all-start.5) | async-done | bytes 2097184 | tf_op jit(solution)/shard_map/all_to_all | solution.py:16
  356.1 3.9 %fusion.7 = bf16[8,128,64]{1,0,2:T(8,128)(2,1)S(1)} fusion(bf16[64,2,128,64]{2,1,3,0:T(2,128)(2,1)} %all-to-all-done.5, s32[64,2]{0,1:T(2,128)S(1)} %bitcast.109), kind=kOutput, calls=%fused_computation.17 | convolution fusion | flops 16843776 | bytes 2228736 | tf_op jit(solution)/shard_map/scb,scif->bif/dot_general | solution.py:99
  360.0 0.7 copy.104
  (37 shorter events, 1.0 us)
Async XLA Ops:
  7.2 105.4 %copy-start = (bf16[64,128,128]{2,1,0:T(8,128)(2,1)S(1)}, bf16[64,128,128]{2,1,0:T(8,128)(2,1)}, u32[]{:S(2)}) copy-start(bf16[64,128,128]{2,1,0:T(8,128)(2,1)} %param.9) | copy-start | bytes 6291460
  15.3 32.2 %all-to-all-start = ((s32[64,1,2]{2,1,0:T(1,128)}), s32[64,1,2]{2,1,0:T(1,128)S(1)}, u32[]{:S(2)}, u32[]{:S(2)}) async-start(s32[64,1,2]{2,1,0:T(1,128)} %copy.60), calls=%async_computation | async-start | bytes 65536 | tf_op jit(solution)/shard_map/all_to_all | solution.py:16
  112.6 1.2 copy-start.2
  114.9 60.9 %all-to-all-start.2 = ((bf16[64,2,128,32]{2,3,1,0:T(8,128)(2,1)}), bf16[64,2,128,32]{2,3,1,0:T(8,128)(2,1)}, u32[]{:S(2)}, u32[]{:S(2)}) async-start(bf16[64,2,128,32]{2,3,1,0:T(8,128)(2,1)} %get-tuple-element.6), calls=%async_computation.2 | async-start | bytes 2097152 | tf_op jit(solution)/shard_map/all_to_all | solution.py:16
  122.3 110.6 %all-gather.3.cloned.1.call-start = ((), (), s32[]{:S(2)}) async-start(), calls=%async_computation.6 | async-start | bytes 1179648 | tf_op jit(solution)/shard_map/all_gather | solution.py:74
  178.9 15.0 %copy-start.3 = (s32[1024]{0:T(1024)S(1)}, s32[1024]{0:T(1024)}, u32[]{:S(2)}) copy-start(s32[1024]{0:T(1024)} %param.13) | copy-start | bytes 12292
  194.9 4.8 %copy-start.1 = (bf16[1024,64]{0,1:T(8,128)(2,1)S(1)}, bf16[1024,64]{0,1:T(8,128)(2,1)}, u32[]{:S(2)}) copy-start(bf16[1024,64]{0,1:T(8,128)(2,1)} %get-tuple-element.26) | copy-start | bytes 393220
  201.0 23.0 %all-to-all-start.3 = ((f32[64,1,512]{2,1,0:T(1,128)}), f32[64,1,512]{2,1,0:T(1,128)S(1)}, u32[]{:S(2)}, u32[]{:S(2)}) async-start(f32[64,1,512]{2,1,0:T(1,128)} %reshape.149), calls=%async_computation.3 | async-start | bytes 262144 | tf_op jit(solution)/shard_map/all_to_all | solution.py:16
  226.6 21.7 %all-to-all-start.4 = ((f32[64,1,512]{2,1,0:T(1,128)}), f32[64,1,512]{2,1,0:T(1,128)S(1)}, u32[]{:S(2)}, u32[]{:S(2)}) async-start(f32[64,1,512]{2,1,0:T(1,128)} %reshape.151), calls=%async_computation.4 | async-start | bytes 262144 | tf_op jit(solution)/shard_map/all_to_all | solution.py:16
  248.3 107.8 %all-to-all-start.5 = ((bf16[64,2,128,64]{2,1,3,0:T(2,128)(2,1)}), bf16[64,2,128,64]{2,1,3,0:T(2,128)(2,1)}, u32[]{:S(2)}, u32[]{:S(2)}) async-start(bf16[64,2,128,64]{2,1,3,0:T(2,128)(2,1)} %copy.74), calls=%async_computation.5 | async-start | bytes 4194304 | tf_op jit(solution)/shard_map/all_to_all | solution.py:16
Sparse Core Ops, SparseCore 0:
  195.1 22.9 all-gather.2

commit v4 on v3

--- a/solution.py
+++ b/solution.py
@@ -21,8 +21,7 @@
     k, c = partial.shape
     pieces = partial.reshape(row_devices, k // row_devices, c)
     reduced = jnp.sum(rows_exchange(pieces), axis=0)
-    spread = jnp.broadcast_to(reduced[None], (row_devices,) + reduced.shape)
-    return rows_exchange(spread).reshape(k, c)
+    return lax.all_gather(reduced, "rows", axis=0, tiled=True)
 
 
 def per_device(node_features, weight, tile_values, tile_row, source_owner, source_block, labels):
@@ -38,7 +37,12 @@
     slot_rank = slot_ranks(owners)
     local_ids = jnp.arange(local_blocks, dtype=jnp.int32)
     row_onehot = (tile_row[:, None] == local_ids[None, :]).astype(jnp.float32)
-    request = jnp.zeros((row_devices, capacity), jnp.int32).at[owners, slot_rank].set(source_block)
+    tile_ids = jnp.arange(tiles, dtype=jnp.int32)
+    in_slot = (owners[:, None, None] == jnp.arange(row_devices, dtype=jnp.int32)[None, :, None]) & (
+        slot_rank[:, None, None] == jnp.arange(capacity, dtype=jnp.int32)[None, None, :]
+    )
+    request = jnp.sum(jnp.where(in_slot, source_block[:, None, None], 0), axis=0)
+    slot_tile = jnp.sum(jnp.where(in_slot, tile_ids[:, None, None] - tiles, 0), axis=0) + tiles
     wanted = rows_exchange(request)
     own_blocks = node_features.reshape(local_blocks, block_size, col_width)
     outgoing = own_blocks[wanted]
@@ -88,11 +92,6 @@
     sent_terms = jnp.einsum(
         "tji,tjf->tif", tile_values, grad_rows, preferred_element_type=jnp.float32
     ).astype(jnp.bfloat16)
-    slot_tile = (
-        jnp.full((row_devices, capacity), tiles, jnp.int32)
-        .at[owners, slot_rank]
-        .set(jnp.arange(tiles, dtype=jnp.int32))
-    )
     padded_terms = jnp.concatenate([sent_terms, jnp.zeros_like(sent_terms[:1])], axis=0)
     received = rows_exchange(padded_terms[slot_tile])
     placing = (wanted[:, :, None] == local_ids[None, None, :]).astype(jnp.float32)

time: 368 us -> 419 us (1.14)
  blocking collectives: 84.8 us -> 191 us
  waiting for transfers between devices: 168 us -> 116 us
  local copies, waits for them, and re-layouts: 34 us -> 24 us
  starting transfers between devices: 49.6 us -> 55.5 us
    all_gather x0 -> x1, blocking collectives: none -> 164 us  [row_all_reduce(): return lax.all_gather(reduced, 'rows', axis=0, tiled=True)]
    all_to_all x5, waiting for transfers between devices: 168 us -> 103 us  [rows_exchange(): return lax.all_to_all(x, 'rows', split_axis=0, concat_axis=0, tiled=True)]
    all_to_all x1 -> x0, blocking collectives: 57.7 us -> none  [rows_exchange(): return lax.all_to_all(x, 'rows', split_axis=0, concat_axis=0, tiled=True)]
    all_gather x1, waiting for transfers between devices: 0.02 us -> 12.5 us  [per_device(): grad_all = lax.all_gather(out_grad, 'cols', axis=1, tiled=True)]
    scatter x2 -> x0, local copies, waits for them, and re-layouts: 9.24 us -> none  [the longest x1 5.75 us: per_device(): jnp.zeros((row_devices, capacity), jnp.int32).at[owners, slot_rank]]
    all_to_all x5, starting transfers between devices: 49.6 us -> 55.4 us  [rows_exchange(): return lax.all_to_all(x, 'rows', split_axis=0, concat_axis=0, tiled=True)]
  transfers between devices with their start and end apart: 6 -> 6, of which waited for: 5 -> 4; matrix products, arithmetic and copies ran while one was open for 6% -> 4% of each run, Pallas kernels for 0% -> 0%
where the time goes in v4:
time: 419 us; the launch traced here: 418 us
  blocking collectives  191 us (46%)
  waiting for transfers between devices  116 us (28%)
  starting transfers between devices  55.5 us (13%)
  local copies, waits for them, and re-layouts  24 us (6%)
  between operations  14.4 us (3%)
  matrix products  14.3 us (3%)
    all_gather x1, blocking collectives, row_all_reduce(): return lax.all_gather(reduced, 'rows', axis=0, tiled=True)  164 us
    all_to_all x5, waiting for transfers between devices, rows_exchange(): return lax.all_to_all(x, 'rows', split_axis=0, concat_axis=0, tiled=True)  103 us
    all_to_all x5, starting transfers between devices, rows_exchange(): return lax.all_to_all(x, 'rows', split_axis=0, concat_axis=0, tiled=True)  55.4 us
    all_gather x1, blocking collectives, per_device(): first_all = lax.all_gather(first, 'cols', axis=0, tiled=False)  13.5 us
    all_gather x1, blocking collectives, per_device(): second_all = lax.all_gather(second, 'cols', axis=0, tiled=False)  13.5 us
    all_gather x1, waiting for transfers between devices, per_device(): grad_all = lax.all_gather(out_grad, 'cols', axis=1, tiled=True)  12.5 us
  transfers between devices with their start and end apart: 6, of which 4 were waited for; matrix products, arithmetic and copies ran while one was open for 4% of the time, Pallas kernels for 0%

profile of v4, /device:TPU:8, one launch (start us, length us, event | category | flops | bytes accessed | tf_op | source)
XLA Modules:
  0.0 418.3 jit_solution(6826741657737070376)
XLA Ops:
  7.2 1.0 convert_reduce_fusion
  8.2 0.7 iota_compare_fusion.1
  8.9 0.8 fusion.20
  9.7 0.7 copy.57
  10.4 18.7 %all-to-all-start = ((s32[64,1,2]{2,1,0:T(1,128)}), s32[64,1,2]{2,1,0:T(1,128)S(1)}, u32[]{:S(2)}, u32[]{:S(2)}) async-start(s32[64,1,2]{2,1,0:T(1,128)} %copy.57), calls=%async_computation | async-start | bytes 65536 | tf_op jit(solution)/shard_map/all_to_all | solution.py:16
  29.2 0.9 copy_bitcast_fusion.2
  30.1 12.5 %all-to-all-done = s32[64,1,2]{2,1,0:T(1,128)S(1)} async-done(((s32[64,1,2]{2,1,0:T(1,128)}), s32[64,1,2]{2,1,0:T(1,128)S(1)}, u32[]{:S(2)}, u32[]{:S(2)}) %all-to-all-start) | async-done | bytes 544 | tf_op jit(solution)/shard_map/all_to_all | solution.py:16
  42.7 0.1 copy.59
  42.8 0.1 reshape.162
  43.0 2.2 gather_fusion
  45.1 3.3 fusion.40
  48.4 6.5 %all-to-all-start.1 = ((bf16[64,2,128,32]{2,3,1,0:T(8,128)(2,1)}), bf16[64,2,128,32]{2,3,1,0:T(8,128)(2,1)}, u32[]{:S(2)}, u32[]{:S(2)}) async-start(bf16[64,2,128,32]{2,3,1,0:T(8,128)(2,1)} %get-tuple-element.15), calls=%async_computation.1 | async-start | bytes 2097152 | tf_op jit(solution)/shard_map/all_to_all | solution.py:16
  54.9 52.2 %all-to-all-done.1 = bf16[64,2,128,32]{2,3,1,0:T(8,128)(2,1)} async-done(((bf16[64,2,128,32]{2,3,1,0:T(8,128)(2,1)}), bf16[64,2,128,32]{2,3,1,0:T(8,128)(2,1)}, u32[]{:S(2)}, u32[]{:S(2)}) %all-to-all-start.1) | async-done | bytes 1048608 | tf_op jit(solution)/shard_map/all_to_all | solution.py:16
  107.1 2.0 gather_fusion.1
  109.0 1.2 convolution_bitcast_fusion.1
  110.2 1.1 convolution_convert_fusion.3
  111.3 7.4 %all-to-all-start.2 = ((bf16[64,2,128,32]{2,3,1,0:T(8,128)(2,1)}), bf16[64,2,128,32]{2,3,1,0:T(8,128)(2,1)}, u32[]{:S(2)}, u32[]{:S(2)}) async-start(bf16[64,2,128,32]{2,3,1,0:T(8,128)(2,1)} %get-tuple-element.6), calls=%async_computation.2 | async-start | bytes 2097152 | tf_op jit(solution)/shard_map/all_to_all | solution.py:16
  118.8 1.0 constant_dynamic-slice_fusion
  119.9 13.5 %all-gather = bf16[8192,32]{0,1:T(8,128)(2,1)S(1)} all-gather(bf16[1024,32]{0,1:T(8,128)(2,1)S(1)} %bitcast.101), channel_id=2, replica_groups=mesh['rows'=64,'cols'=8] {'cols'}, dimensions={0}, use_global_device_ids=true | all-gather | bytes 589824 | tf_op jit(solution)/shard_map/all_gather | solution.py:64
  133.3 0.3 copy.81
  133.6 38.6 %all-to-all-done.2 = bf16[64,2,128,32]{2,3,1,0:T(8,128)(2,1)} async-done(((bf16[64,2,128,32]{2,3,1,0:T(8,128)(2,1)}), bf16[64,2,128,32]{2,3,1,0:T(8,128)(2,1)}, u32[]{:S(2)}, u32[]{:S(2)}) %all-to-all-start.2) | async-done | bytes 1048608 | tf_op jit(solution)/shard_map/all_to_all | solution.py:16
  172.2 2.0 gather_fusion.2
  174.1 1.2 convolution_bitcast_fusion
  175.3 1.1 convolution_convert_fusion.2
  176.4 13.5 %all_gather.18 = bf16[8,1024,32]{1,2,0:T(8,128)(2,1)S(1)} all-gather(bf16[1,1024,32]{1,2,0:T(8,128)(2,1)S(1)} %convert_element_type.53), channel_id=1, replica_groups=mesh['rows'=64,'cols'=8] {'cols'}, dimensions={0}, use_global_device_ids=true | all-gather | bytes 589824 | tf_op jit(solution)/shard_map/all_gather | solution.py:66
  189.9 0.2 convolution_bitcast_fusion.2
  190.2 1.0 multiply_convert_fusion
  191.2 0.1 copy.70
  191.3 0.1 reshape.190
  191.5 1.2 fusion.15
  192.7 0.1 copy.66
  192.8 1.2 fusion.17
  194.1 0.8 reshape.206
  194.9 6.9 %all-to-all-start.3 = ((f32[64,1,512]{2,1,0:T(1,128)}), f32[64,1,512]{2,1,0:T(1,128)S(1)}, u32[]{:S(2)}, u32[]{:S(2)}) async-start(f32[64,1,512]{2,1,0:T(1,128)} %reshape.206), calls=%async_computation.3 | async-start | bytes 262144 | tf_op jit(solution)/shard_map/all_to_all | solution.py:16
  201.8 12.5 %all-gather.3.cloned.1.call-done = bf16[1024,512]{0,1:T(8,128)(2,1)} async-done(((bf16[1024,64]{0,1:T(8,128)(2,1)}), bf16[1024,512]{0,1:T(8,128)(2,1)}) %all-gather.3.cloned.1.call-update) | async-done | bytes 1048592 | tf_op jit(solution)/shard_map/all_gather | solution.py:78
  214.3 1.6 fusion.10
  215.9 0.7 gather_fusion.3
  216.6 0.7 fusion.2
  217.4 2.1 gather_fusion.4
  219.5 5.1 %copy.71 = bf16[64,2,128,64]{2,1,3,0:T(2,128)(2,1)} copy(bf16[64,2,128,64]{2,3,1,0:T(8,128)(2,1)} %bitcast.93) | data formatting | bytes 4194304 | tf_op jit(solution)/shard_map/gather | solution.py:96
  224.6 15.9 %all-to-all-start.4 = ((bf16[64,2,128,64]{2,1,3,0:T(2,128)(2,1)}), bf16[64,2,128,64]{2,1,3,0:T(2,128)(2,1)}, u32[]{:S(2)}, u32[]{:S(2)}) async-start(bf16[64,2,128,64]{2,1,3,0:T(2,128)(2,1)} %copy.71), calls=%async_computation.4 | async-start | bytes 4194304 | tf_op jit(solution)/shard_map/all_to_all | solution.py:16
  240.6 0.5 broadcast.179
  241.1 0.9 reduce
  242.0 0.1 reshape.207
  242.2 163.9 %all_gather.19 = f32[512,64]{1,0:T(8,128)S(1)} all-gather(f32[8,64]{1,0:T(8,128)S(1)} %reduce_sum.41), channel_id=1, replica_groups=mesh['rows'=64,'cols'=8] {'rows'}, dimensions={0}, use_global_device_ids=true | all-gather | bytes 133120 | tf_op jit(solution)/shard_map/all_gather | solution.py:24
  406.1 0.8 copy.73
  406.9 3.9 fusion.7
  410.7 0.7 copy.101
  (32 shorter events, 0.5 us)
Async XLA Ops:
  7.2 101.9 %copy-start = (bf16[64,128,128]{2,1,0:T(8,128)(2,1)S(1)}, bf16[64,128,128]{2,1,0:T(8,128)(2,1)}, u32[]{:S(2)}) copy-start(bf16[64,128,128]{2,1,0:T(8,128)(2,1)} %param.9) | copy-start | bytes 6291460
  10.4 32.2 %all-to-all-start = ((s32[64,1,2]{2,1,0:T(1,128)}), s32[64,1,2]{2,1,0:T(1,128)S(1)}, u32[]{:S(2)}, u32[]{:S(2)}) async-start(s32[64,1,2]{2,1,0:T(1,128)} %copy.57), calls=%async_computation | async-start | bytes 65536 | tf_op jit(solution)/shard_map/all_to_all | solution.py:16
  48.4 6.5 %copy-start.2 = (s32[64,1]{0,1:T(1,128)S(1)}, s32[64,1]{0,1:T(1,128)}, u32[]{:S(2)}) copy-start(s32[64,1]{0,1:T(1,128)} %param.11) | copy-start | bytes 772
  48.4 58.7 %all-to-all-start.1 = ((bf16[64,2,128,32]{2,3,1,0:T(8,128)(2,1)}), bf16[64,2,128,32]{2,3,1,0:T(8,128)(2,1)}, u32[]{:S(2)}, u32[]{:S(2)}) async-start(bf16[64,2,128,32]{2,3,1,0:T(8,128)(2,1)} %get-tuple-element.15), calls=%async_computation.1 | async-start | bytes 2097152 | tf_op jit(solution)/shard_map/all_to_all | solution.py:16
  109.0 1.2 copy-start.1
  111.3 60.9 %all-to-all-start.2 = ((bf16[64,2,128,32]{2,3,1,0:T(8,128)(2,1)}), bf16[64,2,128,32]{2,3,1,0:T(8,128)(2,1)}, u32[]{:S(2)}, u32[]{:S(2)}) async-start(bf16[64,2,128,32]{2,3,1,0:T(8,128)(2,1)} %get-tuple-element.6), calls=%async_computation.2 | async-start | bytes 2097152 | tf_op jit(solution)/shard_map/all_to_all | solution.py:16
  118.8 95.5 %all-gather.3.cloned.1.call-start = ((), (), s32[]{:S(2)}) async-start(), calls=%async_computation.5 | async-start | bytes 1179648 | tf_op jit(solution)/shard_map/all_gather | solution.py:78
  175.3 14.8 %copy-start.3 = (s32[1024]{0:T(1024)S(1)}, s32[1024]{0:T(1024)}, u32[]{:S(2)}) copy-start(s32[1024]{0:T(1024)} %param.13) | copy-start | bytes 12292
  194.9 29.7 %all-to-all-start.3 = ((f32[64,1,512]{2,1,0:T(1,128)}), f32[64,1,512]{2,1,0:T(1,128)S(1)}, u32[]{:S(2)}, u32[]{:S(2)}) async-start(f32[64,1,512]{2,1,0:T(1,128)} %reshape.206), calls=%async_computation.3 | async-start | bytes 262144 | tf_op jit(solution)/shard_map/all_to_all | solution.py:16
  224.6 182.2 %all-to-all-start.4 = ((bf16[64,2,128,64]{2,1,3,0:T(2,128)(2,1)}), bf16[64,2,128,64]{2,1,3,0:T(2,128)(2,1)}, u32[]{:S(2)}, u32[]{:S(2)}) async-start(bf16[64,2,128,64]{2,1,3,0:T(2,128)(2,1)} %copy.71), calls=%async_computation.4 | async-start | bytes 4194304 | tf_op jit(solution)/shard_map/all_to_all | solution.py:16
Sparse Core Ops, SparseCore 0:
  191.3 22.9 all-gather.2

commit v5 on v4

--- a/solution.py
+++ b/solution.py
@@ -3,7 +3,64 @@
 import jax
 import jax.numpy as jnp
 from jax import lax
+from jax.experimental import pallas as pl
+from jax.experimental.pallas import tpu as pltpu
 from jax.sharding import PartitionSpec as P
+
+MESH = pl.DeviceIdType.MESH
+
+
+def _index_exchange_kernel(x_ref, o_ref, send_sems, recv_sems):
+    n = x_ref.shape[0]
+    me = lax.axis_index("rows")
+    barrier = pltpu.get_barrier_semaphore()
+
+    def greet(k, carry):
+        pl.semaphore_signal(
+            barrier, 1, device_id={"rows": lax.rem(me + k, n)}, device_id_type=MESH
+        )
+        return carry
+
+    lax.fori_loop(1, n, greet, 0)
+    pl.semaphore_wait(barrier, n - 1)
+
+    def outgoing(peer):
+        return pltpu.make_async_remote_copy(
+            src_ref=x_ref.at[peer], dst_ref=o_ref.at[me], send_sem=send_sems.at[peer],
+            recv_sem=recv_sems.at[me], device_id={"rows": peer}, device_id_type=MESH)
+
+    def incoming(src):
+        return pltpu.make_async_remote_copy(
+            src_ref=x_ref.at[src], dst_ref=o_ref.at[src], send_sem=send_sems.at[src],
+            recv_sem=recv_sems.at[src], device_id={"rows": src}, device_id_type=MESH)
+
+    def start(k, carry):
+        outgoing(lax.rem(me + k, n)).start()
+        return carry
+
+    lax.fori_loop(1, n, start, 0)
+    o_ref[me] = x_ref[me]
+
+    def finish(k, carry):
+        outgoing(lax.rem(me + k, n)).wait_send()
+        incoming(lax.rem(me + n - k, n)).wait_recv()
+        return carry
+
+    lax.fori_loop(1, n, finish, 0)
+
+
+def index_exchange(table):
+    n, width = table.shape
+    padded = jnp.zeros((n, 8, 128), jnp.int32).at[:, 0, :width].set(table)
+    out = pl.pallas_call(
+        _index_exchange_kernel,
+        out_shape=jax.ShapeDtypeStruct(padded.shape, padded.dtype),
+        in_specs=[pl.BlockSpec(memory_space=pltpu.VMEM)],
+        out_specs=pl.BlockSpec(memory_space=pltpu.VMEM),
+        scratch_shapes=[pltpu.SemaphoreType.DMA((n,)), pltpu.SemaphoreType.DMA((n,))],
+        compiler_params=pltpu.CompilerParams(collective_id=0, has_side_effects=True),
+    )(padded)
+    return out[:, 0, :width]
 
 
 def slot_ranks(owners):
@@ -21,7 +78,8 @@
     k, c = partial.shape
     pieces = partial.reshape(row_devices, k // row_devices, c)
     reduced = jnp.sum(rows_exchange(pieces), axis=0)
-    return lax.all_gather(reduced, "rows", axis=0, tiled=True)
+    spread = jnp.broadcast_to(reduced[None], (row_devices,) + reduced.shape)
+    return rows_exchange(spread).reshape(k, c)
 
 
 def per_device(node_features, weight, tile_values, tile_row, source_owner, source_block, labels):
@@ -43,7 +101,7 @@
     )
     request = jnp.sum(jnp.where(in_slot, source_block[:, None, None], 0), axis=0)
     slot_tile = jnp.sum(jnp.where(in_slot, tile_ids[:, None, None] - tiles, 0), axis=0) + tiles
-    wanted = rows_exchange(request)
+    wanted = index_exchange(request)
     own_blocks = node_features.reshape(local_blocks, block_size, col_width)
     outgoing = own_blocks[wanted]
     col_index = lax.axis_index("cols")

time: 419 us -> 369 us (0.88)
  blocking collectives: 191 us -> 26.9 us
  waiting for transfers between devices: 116 us -> 205 us
  Pallas kernels: 0 us -> 33.2 us
  starting transfers between devices: 55.5 us -> 44.2 us
    all_gather x1 -> x0, blocking collectives: 164 us -> none  [row_all_reduce(): return lax.all_gather(reduced, 'rows', axis=0, tiled=True)]
    all_to_all x5, waiting for transfers between devices: 103 us -> 205 us  [rows_exchange(): return lax.all_to_all(x, 'rows', split_axis=0, concat_axis=0, tiled=True)]
    pallas_call x0 -> x1, Pallas kernels: none -> 33.2 us  [index_exchange(): pl.pallas_call(_index_exchange_kernel, out_shape=jax.ShapeDtypeStruct(pad...]
    all_gather x1, waiting for transfers between devices: 12.5 us -> 0.02 us  [per_device(): grad_all = lax.all_gather(out_grad, 'cols', axis=1, tiled=True)]
    all_to_all x5, starting transfers between devices: 55.4 us -> 44.2 us  [rows_exchange(): return lax.all_to_all(x, 'rows', split_axis=0, concat_axis=0, tiled=True)]
  transfers between devices with their start and end apart: 6 -> 6, of which waited for: 4 -> 5; matrix products, arithmetic and copies ran while one was open for 4% -> 5% of each run, Pallas kernels for 0% -> 0%
where the time goes in v5:
time: 369 us; the launch traced here: 368 us
  waiting for transfers between devices  205 us (56%)
  starting transfers between devices  44.2 us (12%)
  Pallas kernels  33.2 us (9%)
  blocking collectives  26.9 us (7%)
  local copies, waits for them, and re-layouts  26.1 us (7%)
  between operations  14.4 us (4%)
  matrix products  14.3 us (4%)
  other arithmetic  4.42 us (1%)
    all_to_all x5, waiting for transfers between devices, rows_exchange(): return lax.all_to_all(x, 'rows', split_axis=0, concat_axis=0, tiled=True)  205 us
    all_to_all x5, starting transfers between devices, rows_exchange(): return lax.all_to_all(x, 'rows', split_axis=0, concat_axis=0, tiled=True)  44.2 us
    pallas_call x1, Pallas kernels, index_exchange(): pl.pallas_call(_index_exchange_kernel, out_shape=jax.ShapeDtypeStruct(pad...  33.2 us
    all_gather x1, blocking collectives, per_device(): first_all = lax.all_gather(first, 'cols', axis=0, tiled=False)  13.5 us
    all_gather x1, blocking collectives, per_device(): second_all = lax.all_gather(second, 'cols', axis=0, tiled=False)  13.5 us
  transfers between devices with their start and end apart: 6, of which 5 were waited for; matrix products, arithmetic and copies ran while one was open for 5% of the time, Pallas kernels for 0%

profile of v5, /device:TPU:8, one launch (start us, length us, event | category | flops | bytes accessed | tf_op | source)
XLA Modules:
  0.0 368.3 jit_solution(7577087353485451199)
XLA Ops:
  7.2 1.0 convert_reduce_fusion
  8.2 0.7 iota_compare_fusion.1
  8.9 0.8 fusion.20
  9.8 0.9 copy_bitcast_fusion.2
  10.8 0.7 scatter.4.x_ref
  11.5 33.2 %shard_map.97 = s32[64,8,128]{2,1,0:T(8,128)} custom-call(s32[64,8,128]{2,1,0:T(8,128)} %scatter.4.x_ref), custom_call_target="tpu_custom_call" | custom-call | tf_op jit(solution)/shard_map/pallas_call | solution.py:55
  44.7 1.0 slice.38
  45.8 0.1 reshape.202
  46.0 2.2 gather_fusion
  48.1 3.3 fusion.40
  51.5 12.4 %all-to-all-start = ((bf16[64,2,128,32]{2,3,1,0:T(8,128)(2,1)}), bf16[64,2,128,32]{2,3,1,0:T(8,128)(2,1)}, u32[]{:S(2)}, u32[]{:S(2)}) async-start(bf16[64,2,128,32]{2,3,1,0:T(8,128)(2,1)} %get-tuple-element.36), calls=%async_computation | async-start | bytes 2097152 | tf_op jit(solution)/shard_map/all_to_all | solution.py:73
  63.9 50.7 %all-to-all-done = bf16[64,2,128,32]{2,3,1,0:T(8,128)(2,1)} async-done(((bf16[64,2,128,32]{2,3,1,0:T(8,128)(2,1)}), bf16[64,2,128,32]{2,3,1,0:T(8,128)(2,1)}, u32[]{:S(2)}, u32[]{:S(2)}) %all-to-all-start) | async-done | bytes 1048608 | tf_op jit(solution)/shard_map/all_to_all | solution.py:73
  114.6 2.0 gather_fusion.1
  116.6 1.2 convolution_bitcast_fusion.1
  117.8 1.1 convolution_convert_fusion.3
  118.9 8.0 %all-to-all-start.1 = ((bf16[64,2,128,32]{2,3,1,0:T(8,128)(2,1)}), bf16[64,2,128,32]{2,3,1,0:T(8,128)(2,1)}, u32[]{:S(2)}, u32[]{:S(2)}) async-start(bf16[64,2,128,32]{2,3,1,0:T(8,128)(2,1)} %get-tuple-element.18), calls=%async_computation.1 | async-start | bytes 2097152 | tf_op jit(solution)/shard_map/all_to_all | solution.py:73
  127.0 1.0 constant_dynamic-slice_fusion
  128.0 13.5 %all-gather = bf16[8192,32]{0,1:T(8,128)(2,1)S(1)} all-gather(bf16[1024,32]{0,1:T(8,128)(2,1)S(1)} %bitcast.103), channel_id=2, replica_groups=mesh['rows'=64,'cols'=8] {'cols'}, dimensions={0}, use_global_device_ids=true | all-gather | bytes 589824 | tf_op jit(solution)/shard_map/all_gather | solution.py:122
  141.5 0.3 copy.96
  141.8 37.5 %all-to-all-done.1 = bf16[64,2,128,32]{2,3,1,0:T(8,128)(2,1)} async-done(((bf16[64,2,128,32]{2,3,1,0:T(8,128)(2,1)}), bf16[64,2,128,32]{2,3,1,0:T(8,128)(2,1)}, u32[]{:S(2)}, u32[]{:S(2)}) %all-to-all-start.1) | async-done | bytes 1048608 | tf_op jit(solution)/shard_map/all_to_all | solution.py:73
  179.2 2.0 gather_fusion.2
  181.2 1.2 convolution_bitcast_fusion
  182.4 1.1 convolution_convert_fusion.2
  183.5 13.5 %all_gather.15 = bf16[8,1024,32]{1,2,0:T(8,128)(2,1)S(1)} all-gather(bf16[1,1024,32]{1,2,0:T(8,128)(2,1)S(1)} %convert_element_type.53), channel_id=1, replica_groups=mesh['rows'=64,'cols'=8] {'cols'}, dimensions={0}, use_global_device_ids=true | all-gather | bytes 589824 | tf_op jit(solution)/shard_map/all_gather | solution.py:124
  196.9 0.2 convolution_bitcast_fusion.2
  197.2 1.0 multiply_convert_fusion
  198.3 1.2 fusion.15
  199.5 1.2 fusion.17
  200.8 0.8 reshape.246
  201.7 7.0 %all-to-all-start.2 = ((f32[64,1,512]{2,1,0:T(1,128)}), f32[64,1,512]{2,1,0:T(1,128)S(1)}, u32[]{:S(2)}, u32[]{:S(2)}) async-start(f32[64,1,512]{2,1,0:T(1,128)} %reshape.246), calls=%async_computation.2 | async-start | bytes 262144 | tf_op jit(solution)/shard_map/all_to_all | solution.py:73
  208.8 0.1 reshape.230
  209.0 15.9 %all-to-all-done.2 = f32[64,1,512]{2,1,0:T(1,128)S(1)} async-done(((f32[64,1,512]{2,1,0:T(1,128)}), f32[64,1,512]{2,1,0:T(1,128)S(1)}, u32[]{:S(2)}, u32[]{:S(2)}) %all-to-all-start.2) | async-done | bytes 131104 | tf_op jit(solution)/shard_map/all_to_all | solution.py:73
  224.8 0.5 broadcast.213
  225.4 0.9 reduce.2
  226.4 0.8 reshape.248
  227.3 6.4 %all-to-all-start.3 = ((f32[64,1,512]{2,1,0:T(1,128)}), f32[64,1,512]{2,1,0:T(1,128)S(1)}, u32[]{:S(2)}, u32[]{:S(2)}) async-start(f32[64,1,512]{2,1,0:T(1,128)} %reshape.248), calls=%async_computation.3 | async-start | bytes 262144 | tf_op jit(solution)/shard_map/all_to_all | solution.py:73
  233.7 1.6 fusion.10
  235.4 0.7 gather_fusion.3
  236.1 0.7 fusion.2
  236.9 2.1 gather_fusion.4
  239.0 5.1 %copy.86 = bf16[64,2,128,64]{2,1,3,0:T(2,128)(2,1)} copy(bf16[64,2,128,64]{2,3,1,0:T(8,128)(2,1)} %bitcast.95) | data formatting | bytes 4194304 | tf_op jit(solution)/shard_map/gather | solution.py:154
  244.1 5.0 %all-to-all-done.3 = f32[64,1,512]{2,1,0:T(1,128)S(1)} async-done(((f32[64,1,512]{2,1,0:T(1,128)}), f32[64,1,512]{2,1,0:T(1,128)S(1)}, u32[]{:S(2)}, u32[]{:S(2)}) %all-to-all-start.3) | async-done | bytes 131104 | tf_op jit(solution)/shard_map/all_to_all | solution.py:73
  249.1 10.3 %all-to-all-start.4 = ((bf16[64,2,128,64]{2,1,3,0:T(2,128)(2,1)}), bf16[64,2,128,64]{2,1,3,0:T(2,128)(2,1)}, u32[]{:S(2)}, u32[]{:S(2)}) async-start(bf16[64,2,128,64]{2,1,3,0:T(2,128)(2,1)} %copy.86), calls=%async_computation.4 | async-start | bytes 4194304 | tf_op jit(solution)/shard_map/all_to_all | solution.py:73
  259.4 0.9 reduce.3
  260.4 0.8 copy.88
  261.2 95.7 %all-to-all-done.4 = bf16[64,2,128,64]{2,1,3,0:T(2,128)(2,1)} async-done(((bf16[64,2,128,64]{2,1,3,0:T(2,128)(2,1)}), bf16[64,2,128,64]{2,1,3,0:T(2,128)(2,1)}, u32[]{:S(2)}, u32[]{:S(2)}) %all-to-all-start.4) | async-done | bytes 2097184 | tf_op jit(solution)/shard_map/all_to_all | solution.py:73
  356.9 3.9 %fusion.7 = bf16[8,128,64]{1,0,2:T(8,128)(2,1)S(1)} fusion(bf16[64,2,128,64]{2,1,3,0:T(2,128)(2,1)} %all-to-all-done.4, s32[64,2]{0,1:T(2,128)S(1)} %bitcast.106), kind=kOutput, calls=%fused_computation.15 | convolution fusion | flops 16843776 | bytes 2228736 | tf_op jit(solution)/shard_map/scb,scif->bif/dot_general | solution.py:156
  360.8 0.7 copy.116
  (38 shorter events, 1.2 us)
Async XLA Ops:
  7.2 109.4 %copy-start = (bf16[64,128,128]{2,1,0:T(8,128)(2,1)S(1)}, bf16[64,128,128]{2,1,0:T(8,128)(2,1)}, u32[]{:S(2)}) copy-start(bf16[64,128,128]{2,1,0:T(8,128)(2,1)} %param.11) | copy-start | bytes 6291460
  51.4 12.5 %copy-start.2 = (s32[64,1]{0,1:T(1,128)S(1)}, s32[64,1]{0,1:T(1,128)}, u32[]{:S(2)}) copy-start(s32[64,1]{0,1:T(1,128)} %param.13) | copy-start | bytes 772
  51.5 63.2 %all-to-all-start = ((bf16[64,2,128,32]{2,3,1,0:T(8,128)(2,1)}), bf16[64,2,128,32]{2,3,1,0:T(8,128)(2,1)}, u32[]{:S(2)}, u32[]{:S(2)}) async-start(bf16[64,2,128,32]{2,3,1,0:T(8,128)(2,1)} %get-tuple-element.36), calls=%async_computation | async-start | bytes 2097152 | tf_op jit(solution)/shard_map/all_to_all | solution.py:73
  116.6 1.2 copy-start.1
  118.9 60.3 %all-to-all-start.1 = ((bf16[64,2,128,32]{2,3,1,0:T(8,128)(2,1)}), bf16[64,2,128,32]{2,3,1,0:T(8,128)(2,1)}, u32[]{:S(2)}, u32[]{:S(2)}) async-start(bf16[64,2,128,32]{2,3,1,0:T(8,128)(2,1)} %get-tuple-element.18), calls=%async_computation.1 | async-start | bytes 2097152 | tf_op jit(solution)/shard_map/all_to_all | solution.py:73
  126.9 106.8 %all-gather.3.cloned.1.call-start = ((), (), s32[]{:S(2)}) async-start(), calls=%async_computation.5 | async-start | bytes 1179648 | tf_op jit(solution)/shard_map/all_gather | solution.py:136
  182.4 14.8 %copy-start.3 = (s32[1024]{0:T(1024)S(1)}, s32[1024]{0:T(1024)}, u32[]{:S(2)}) copy-start(s32[1024]{0:T(1024)} %param.15) | copy-start | bytes 12292
  201.7 23.2 %all-to-all-start.2 = ((f32[64,1,512]{2,1,0:T(1,128)}), f32[64,1,512]{2,1,0:T(1,128)S(1)}, u32[]{:S(2)}, u32[]{:S(2)}) async-start(f32[64,1,512]{2,1,0:T(1,128)} %reshape.246), calls=%async_computation.2 | async-start | bytes 262144 | tf_op jit(solution)/shard_map/all_to_all | solution.py:73
  227.3 21.9 %all-to-all-start.3 = ((f32[64,1,512]{2,1,0:T(1,128)}), f32[64,1,512]{2,1,0:T(1,128)S(1)}, u32[]{:S(2)}, u32[]{:S(2)}) async-start(f32[64,1,512]{2,1,0:T(1,128)} %reshape.248), calls=%async_computation.3 | async-start | bytes 262144 | tf_op jit(solution)/shard_map/all_to_all | solution.py:73
  249.1 107.8 %all-to-all-start.4 = ((bf16[64,2,128,64]{2,1,3,0:T(2,128)(2,1)}), bf16[64,2,128,64]{2,1,3,0:T(2,128)(2,1)}, u32[]{:S(2)}, u32[]{:S(2)}) async-start(bf16[64,2,128,64]{2,1,3,0:T(2,128)(2,1)} %copy.86), calls=%async_computation.4 | async-start | bytes 4194304 | tf_op jit(solution)/shard_map/all_to_all | solution.py:73
Sparse Core Ops, SparseCore 0:
  198.4 23.0 all-gather.2

commit v6 on v5

--- a/solution.py
+++ b/solution.py
@@ -63,6 +63,60 @@
     return out[:, 0, :width]
 
 
+def _rows_gather_kernel(x_ref, o_ref, send_sems, recv_sems):
+    n = o_ref.shape[0]
+    me = lax.axis_index("rows")
+    barrier = pltpu.get_barrier_semaphore()
+
+    def greet(k, carry):
+        pl.semaphore_signal(
+            barrier, 1, device_id={"rows": lax.rem(me + k, n)}, device_id_type=MESH
+        )
+        return carry
+
+    lax.fori_loop(1, n, greet, 0)
+    pl.semaphore_wait(barrier, n - 1)
+
+    def outgoing(peer):
+        return pltpu.make_async_remote_copy(
+            src_ref=x_ref, dst_ref=o_ref.at[me], send_sem=send_sems.at[peer],
+            recv_sem=recv_sems.at[me], device_id={"rows": peer}, device_id_type=MESH)
+
+    def incoming(src):
+        return pltpu.make_async_remote_copy(
+            src_ref=x_ref, dst_ref=o_ref.at[src], send_sem=send_sems.at[src],
+            recv_sem=recv_sems.at[src], device_id={"rows": src}, device_id_type=MESH)
+
+    def start(k, carry):
+        outgoing(lax.rem(me + k, n)).start()
+        return carry
+
+    lax.fori_loop(1, n, start, 0)
+    o_ref[me] = x_ref[...]
+
+    def finish(k, carry):
+        outgoing(lax.rem(me + k, n)).wait_send()
+        incoming(lax.rem(me + n - k, n)).wait_recv()
+        return carry
+
+    lax.fori_loop(1, n, finish, 0)
+
+
+def rows_gather(x):
+    n = lax.axis_size("rows")
+    return pl.pallas_call(
+        _rows_gather_kernel,
+        out_shape=jax.ShapeDtypeStruct((n,) + x.shape, x.dtype),
+        in_specs=[pl.BlockSpec(memory_space=pltpu.VMEM)],
+        out_specs=pl.BlockSpec(memory_space=pltpu.VMEM),
+        scratch_shapes=[pltpu.SemaphoreType.DMA((n,)), pltpu.SemaphoreType.DMA((n,))],
+        compiler_params=pltpu.CompilerParams(collective_id=1, has_side_effects=True),
+        cost_estimate=pl.CostEstimate(
+            flops=0, transcendentals=0, bytes_accessed=2 * n * x.size * x.dtype.itemsize
+        ),
+    )(x)
+
+
 def slot_ranks(owners):
     positions = jnp.arange(owners.shape[0], dtype=jnp.int32)
     earlier = (owners[:, None] == owners[None, :]) & (positions[None, :] < positions[:, None])
@@ -78,8 +132,7 @@
     k, c = partial.shape
     pieces = partial.reshape(row_devices, k // row_devices, c)
     reduced = jnp.sum(rows_exchange(pieces), axis=0)
-    spread = jnp.broadcast_to(reduced[None], (row_devices,) + reduced.shape)
-    return rows_exchange(spread).reshape(k, c)
+    return rows_gather(reduced).reshape(k, c)
 
 
 def per_device(node_features, weight, tile_values, tile_row, source_owner, source_block, labels):

time: 369 us -> 375 us (1.016)
  the two profiles are of different devices: /device:TPU:8 before, /device:TPU:1 now
where the time goes in v6:
time: 375 us; the launch traced here: 374 us
  Pallas kernels  144 us (38%)
  waiting for transfers between devices  92.6 us (25%)
  starting transfers between devices  43.7 us (12%)
  blocking collectives  35.2 us (9%)
  local copies, waits for them, and re-layouts  25.1 us (7%)
  between operations  14.4 us (4%)
  matrix products  14.3 us (4%)
  other arithmetic  5.16 us (1%)
    pallas_call x1, Pallas kernels, rows_gather(): pl.pallas_call(_rows_gather_kernel, out_shape=jax.ShapeDtypeStruct((n,) +...  110 us
    all_to_all x4, waiting for transfers between devices, rows_exchange(): return lax.all_to_all(x, 'rows', split_axis=0, concat_axis=0, tiled=True)  80 us
    all_to_all x4, starting transfers between devices, rows_exchange(): return lax.all_to_all(x, 'rows', split_axis=0, concat_axis=0, tiled=True)  43.7 us
    pallas_call x1, Pallas kernels, index_exchange(): pl.pallas_call(_index_exchange_kernel, out_shape=jax.ShapeDtypeStruct(pad...  33.8 us
    all_gather x1, blocking collectives, per_device(): second_all = lax.all_gather(second, 'cols', axis=0, tiled=False)  19.7 us
    all_gather x1, blocking collectives, per_device(): first_all = lax.all_gather(first, 'cols', axis=0, tiled=False)  15.5 us
    all_gather x1, waiting for transfers between devices, per_device(): grad_all = lax.all_gather(out_grad, 'cols', axis=1, tiled=True)  12.6 us
  transfers between devices with their start and end apart: 5, of which 3 were waited for; matrix products, arithmetic and copies ran while one was open for 5% of the time, Pallas kernels for 29%

profile of v6, /device:TPU:1, one launch (start us, length us, event | category | flops | bytes accessed | tf_op | source)
XLA Modules:
  0.0 374.0 jit_solution(16469526232195275284)
XLA Ops:
  7.2 1.0 convert_reduce_fusion
  8.2 0.7 iota_compare_fusion.1
  8.9 0.8 fusion.20
  9.8 0.9 copy_bitcast_fusion.2
  10.8 0.7 scatter.4.x_ref
  11.5 33.8 %shard_map.97 = s32[64,8,128]{2,1,0:T(8,128)} custom-call(s32[64,8,128]{2,1,0:T(8,128)} %scatter.4.x_ref), custom_call_target="tpu_custom_call" | custom-call | tf_op jit(solution)/shard_map/pallas_call | solution.py:55
  45.3 1.0 slice.38
  46.3 0.1 copy.75
  46.4 0.1 reshape.201
  46.6 2.1 gather_fusion
  48.7 3.3 fusion.40
  52.0 10.5 %all-to-all-start = ((bf16[64,2,128,32]{2,3,1,0:T(8,128)(2,1)}), bf16[64,2,128,32]{2,3,1,0:T(8,128)(2,1)}, u32[]{:S(2)}, u32[]{:S(2)}) async-start(bf16[64,2,128,32]{2,3,1,0:T(8,128)(2,1)} %get-tuple-element.39), calls=%async_computation | async-start | bytes 2097152 | tf_op jit(solution)/shard_map/all_to_all | solution.py:127
  62.5 48.6 %all-to-all-done = bf16[64,2,128,32]{2,3,1,0:T(8,128)(2,1)} async-done(((bf16[64,2,128,32]{2,3,1,0:T(8,128)(2,1)}), bf16[64,2,128,32]{2,3,1,0:T(8,128)(2,1)}, u32[]{:S(2)}, u32[]{:S(2)}) %all-to-all-start) | async-done | bytes 1048608 | tf_op jit(solution)/shard_map/all_to_all | solution.py:127
  111.1 2.0 gather_fusion.1
  113.1 1.2 convolution_bitcast_fusion.1
  114.3 1.1 convolution_convert_fusion.3
  115.4 10.9 %all-to-all-start.1 = ((bf16[64,2,128,32]{2,3,1,0:T(8,128)(2,1)}), bf16[64,2,128,32]{2,3,1,0:T(8,128)(2,1)}, u32[]{:S(2)}, u32[]{:S(2)}) async-start(bf16[64,2,128,32]{2,3,1,0:T(8,128)(2,1)} %get-tuple-element.18), calls=%async_computation.1 | async-start | bytes 2097152 | tf_op jit(solution)/shard_map/all_to_all | solution.py:127
  126.3 1.0 constant_dynamic-slice_fusion
  127.4 15.5 %all-gather = bf16[8192,32]{0,1:T(8,128)(2,1)S(1)} all-gather(bf16[1024,32]{0,1:T(8,128)(2,1)S(1)} %bitcast.103), channel_id=2, replica_groups=mesh['rows'=64,'cols'=8] {'cols'}, dimensions={0}, use_global_device_ids=true | all-gather | bytes 589824 | tf_op jit(solution)/shard_map/all_gather | solution.py:175
  142.9 0.3 copy.97
  143.2 31.4 %all-to-all-done.1 = bf16[64,2,128,32]{2,3,1,0:T(8,128)(2,1)} async-done(((bf16[64,2,128,32]{2,3,1,0:T(8,128)(2,1)}), bf16[64,2,128,32]{2,3,1,0:T(8,128)(2,1)}, u32[]{:S(2)}, u32[]{:S(2)}) %all-to-all-start.1) | async-done | bytes 1048608 | tf_op jit(solution)/shard_map/all_to_all | solution.py:127
  174.6 2.0 gather_fusion.2
  176.5 1.2 convolution_bitcast_fusion
  177.7 1.1 convolution_convert_fusion.2
  178.8 19.7 %all_gather.15 = bf16[8,1024,32]{1,2,0:T(8,128)(2,1)S(1)} all-gather(bf16[1,1024,32]{1,2,0:T(8,128)(2,1)S(1)} %convert_element_type.53), channel_id=1, replica_groups=mesh['rows'=64,'cols'=8] {'cols'}, dimensions={0}, use_global_device_ids=true | all-gather | bytes 589824 | tf_op jit(solution)/shard_map/all_gather | solution.py:177
  198.5 0.2 convolution_bitcast_fusion.2
  198.7 1.0 multiply_convert_fusion
  199.9 0.1 reshape.229
  200.1 1.2 fusion.15
  201.4 1.2 fusion.17
  202.6 0.8 reshape.245
  203.5 6.7 %all-to-all-start.2 = ((f32[64,1,512]{2,1,0:T(1,128)}), f32[64,1,512]{2,1,0:T(1,128)S(1)}, u32[]{:S(2)}, u32[]{:S(2)}) async-start(f32[64,1,512]{2,1,0:T(1,128)} %reshape.245), calls=%async_computation.2 | async-start | bytes 262144 | tf_op jit(solution)/shard_map/all_to_all | solution.py:127
  210.2 12.6 %all-gather.3.cloned.1.call-done = bf16[1024,512]{0,1:T(8,128)(2,1)} async-done(((bf16[1024,64]{0,1:T(8,128)(2,1)}), bf16[1024,512]{0,1:T(8,128)(2,1)}) %all-gather.3.cloned.1.call-update) | async-done | bytes 1048592 | tf_op jit(solution)/shard_map/all_gather | solution.py:189
  222.8 1.6 fusion.10
  224.4 0.7 gather_fusion.3
  225.2 0.7 fusion.2
  225.9 2.1 gather_fusion.4
  228.1 5.1 %copy.87 = bf16[64,2,128,64]{2,1,3,0:T(2,128)(2,1)} copy(bf16[64,2,128,64]{2,3,1,0:T(8,128)(2,1)} %bitcast.95) | data formatting | bytes 4194304 | tf_op jit(solution)/shard_map/gather | solution.py:207
  233.2 15.6 %all-to-all-start.3 = ((bf16[64,2,128,64]{2,1,3,0:T(2,128)(2,1)}), bf16[64,2,128,64]{2,1,3,0:T(2,128)(2,1)}, u32[]{:S(2)}, u32[]{:S(2)}) async-start(bf16[64,2,128,64]{2,1,3,0:T(2,128)(2,1)} %copy.87), calls=%async_computation.3 | async-start | bytes 4194304 | tf_op jit(solution)/shard_map/all_to_all | solution.py:127
  248.8 0.5 broadcast.212
  249.3 0.9 reduce.2
  250.3 0.1 reshape.246
  250.4 0.7 reduce_sum.41.x_ref
  251.0 109.8 %shard_map.98 = f32[64,8,64]{2,1,0:T(8,128)} custom-call(f32[8,64]{1,0:T(8,128)} %reduce_sum.41.x_ref), custom_call_target="tpu_custom_call" | custom-call | bytes 262144 | tf_op jit(solution)/shard_map/pallas_call | solution.py:107
  360.8 1.0 multiply_bitcast_fusion
  361.8 0.8 copy.89
  362.6 3.9 %fusion.7 = bf16[8,128,64]{1,0,2:T(8,128)(2,1)S(1)} fusion(bf16[64,2,128,64]{2,1,3,0:T(2,128)(2,1)} %all-to-all-done.3, s32[64,2]{0,1:T(2,128)S(1)} %bitcast.106), kind=kOutput, calls=%fused_computation.15 | convolution fusion | flops 16843776 | bytes 2228736 | tf_op jit(solution)/shard_map/scb,scif->bif/dot_general | solution.py:209
  366.5 0.7 copy.117
  (33 shorter events, 0.7 us)
Async XLA Ops:
  7.2 105.9 %copy-start = (bf16[64,128,128]{2,1,0:T(8,128)(2,1)S(1)}, bf16[64,128,128]{2,1,0:T(8,128)(2,1)}, u32[]{:S(2)}) copy-start(bf16[64,128,128]{2,1,0:T(8,128)(2,1)} %param.11) | copy-start | bytes 6291460
  52.0 10.5 %copy-start.2 = (s32[64,1]{0,1:T(1,128)S(1)}, s32[64,1]{0,1:T(1,128)}, u32[]{:S(2)}) copy-start(s32[64,1]{0,1:T(1,128)} %param.13) | copy-start | bytes 772
  52.0 59.1 %all-to-all-start = ((bf16[64,2,128,32]{2,3,1,0:T(8,128)(2,1)}), bf16[64,2,128,32]{2,3,1,0:T(8,128)(2,1)}, u32[]{:S(2)}, u32[]{:S(2)}) async-start(bf16[64,2,128,32]{2,3,1,0:T(8,128)(2,1)} %get-tuple-element.39), calls=%async_computation | async-start | bytes 2097152 | tf_op jit(solution)/shard_map/all_to_all | solution.py:127
  113.1 1.2 copy-start.1
  115.4 59.2 %all-to-all-start.1 = ((bf16[64,2,128,32]{2,3,1,0:T(8,128)(2,1)}), bf16[64,2,128,32]{2,3,1,0:T(8,128)(2,1)}, u32[]{:S(2)}, u32[]{:S(2)}) async-start(bf16[64,2,128,32]{2,3,1,0:T(8,128)(2,1)} %get-tuple-element.18), calls=%async_computation.1 | async-start | bytes 2097152 | tf_op jit(solution)/shard_map/all_to_all | solution.py:127
  126.3 96.5 %all-gather.3.cloned.1.call-start = ((), (), s32[]{:S(2)}) async-start(), calls=%async_computation.4 | async-start | bytes 1179648 | tf_op jit(solution)/shard_map/all_gather | solution.py:189
  177.7 21.0 %copy-start.3 = (s32[1024]{0:T(1024)S(1)}, s32[1024]{0:T(1024)}, u32[]{:S(2)}) copy-start(s32[1024]{0:T(1024)} %param.15) | copy-start | bytes 12292
  203.5 29.7 %all-to-all-start.2 = ((f32[64,1,512]{2,1,0:T(1,128)}), f32[64,1,512]{2,1,0:T(1,128)S(1)}, u32[]{:S(2)}, u32[]{:S(2)}) async-start(f32[64,1,512]{2,1,0:T(1,128)} %reshape.245), calls=%async_computation.2 | async-start | bytes 262144 | tf_op jit(solution)/shard_map/all_to_all | solution.py:127
  233.2 129.4 %all-to-all-start.3 = ((bf16[64,2,128,64]{2,1,3,0:T(2,128)(2,1)}), bf16[64,2,128,64]{2,1,3,0:T(2,128)(2,1)}, u32[]{:S(2)}, u32[]{:S(2)}) async-start(bf16[64,2,128,64]{2,1,3,0:T(2,128)(2,1)} %copy.87), calls=%async_computation.3 | async-start | bytes 4194304 | tf_op jit(solution)/shard_map/all_to_all | solution.py:127
Sparse Core Ops, SparseCore 0:
  199.9 22.8 all-gather.2

commit v7 on v1

v7 whole, which is shorter than its diff:
```python
import math

import jax
import jax.numpy as jnp
from jax import lax
from jax.sharding import PartitionSpec as P


def slot_ranks(owners):
    positions = jnp.arange(owners.shape[0], dtype=jnp.int32)
    earlier = (owners[:, None] == owners[None, :]) & (positions[None, :] < positions[:, None])
    return jnp.sum(earlier.astype(jnp.int32), axis=1)


def rows_exchange(x):
    return lax.all_to_all(x, "rows", split_axis=0, concat_axis=0, tiled=True)


def per_device(node_features, weight, tile_values, tile_row, source_owner, source_block, labels):
    local_rows, col_width = node_features.shape
    block_size = tile_values.shape[1]
    local_blocks = local_rows // block_size
    row_devices = lax.axis_size("rows")
    col_devices = lax.axis_size("cols")
    tiles = tile_values.shape[0]
    capacity = 2 * tiles // row_devices
    owners = source_owner[:, 0]
    slot_rank = slot_ranks(owners)
    local_ids = jnp.arange(local_blocks, dtype=jnp.int32)
    row_onehot = (tile_row[:, None] == local_ids[None, :]).astype(jnp.float32)
    tile_ids = jnp.arange(tiles, dtype=jnp.int32)
    in_slot = (owners[:, None, None] == jnp.arange(row_devices, dtype=jnp.int32)[None, :, None]) & (
        slot_rank[:, None, None] == jnp.arange(capacity, dtype=jnp.int32)[None, None, :]
    )
    request = jnp.sum(jnp.where(in_slot, source_block[:, None, None], 0), axis=0)
    slot_tile = jnp.sum(jnp.where(in_slot, tile_ids[:, None, None] - tiles, 0), axis=0) + tiles
    wanted = rows_exchange(request)
    own_blocks = node_features.reshape(local_blocks, block_size, col_width)
    incoming = rows_exchange(own_blocks[wanted])
    source_rows = incoming[owners, slot_rank]
    products = jnp.einsum(
        "tij,tjf->tif", tile_values, source_rows, preferred_element_type=jnp.float32
    )
    summed = jnp.einsum("tb,tif->bif", row_onehot, products, precision=lax.Precision.HIGHEST)
    aggregated = summed.reshape(local_rows, col_width).astype(jnp.bfloat16)
    aggregated_all = lax.all_gather(aggregated, "cols", axis=0, tiled=False)
    col_index = lax.axis_index("cols")
    w_columns = lax.dynamic_slice_in_dim(weight, col_index * col_width, col_width, 1)
    w_rows = lax.dynamic_slice_in_dim(weight, col_index * col_width, col_width, 0)
    w_split = w_columns.reshape(col_devices, col_width, col_width)
    hidden = jnp.einsum("jnf,jfc->nc", aggregated_all, w_split, preferred_element_type=jnp.float32)
    sigmoid = jax.nn.sigmoid(hidden)
    activated = hidden * sigmoid
    slopes = sigmoid * (1.0 + hidden * (1.0 - sigmoid))
    feature_ids = col_index * col_width + jnp.arange(col_width, dtype=jnp.int32)
    target = (labels[:, None] == feature_ids[None, :]).astype(jnp.float32)
    out_grad = ((activated - target) * slopes).astype(jnp.bfloat16)
    grad_all = lax.all_gather(out_grad, "cols", axis=1, tiled=True)
    weight_terms = jnp.einsum(
        "jnf,nc->jfc", aggregated_all, out_grad, preferred_element_type=jnp.float32
    ).reshape(col_devices * col_width, col_width)
    pieces = weight_terms.reshape(row_devices, -1, col_width)
    reduced = jnp.sum(rows_exchange(pieces), axis=0)
    high = reduced.astype(jnp.bfloat16)
    low = (reduced - high.astype(jnp.float32)).astype(jnp.bfloat16)
    chunk = jnp.concatenate([high, low], axis=0)
    chunk_rows = chunk.shape[0]
    agg_grad = jnp.einsum("nc,kc->nk", grad_all, w_rows, preferred_element_type=jnp.float32).astype(
        jnp.bfloat16
    )
    grad_rows = agg_grad.reshape(local_blocks, block_size, col_width)[tile_row]
    sent_terms = jnp.einsum(
        "tji,tjf->tif", tile_values, grad_rows, preferred_element_type=jnp.float32
    ).astype(jnp.bfloat16)
    padded_terms = jnp.concatenate([sent_terms, jnp.zeros_like(sent_terms[:1])], axis=0)
    send_terms = padded_terms[slot_tile].reshape(row_devices, capacity * block_size, col_width)
    payload = jnp.concatenate(
        [send_terms, jnp.broadcast_to(chunk[None], (row_devices,) + chunk.shape)], axis=1
    )
    arrived = rows_exchange(payload)
    received = arrived[:, : capacity * block_size].reshape(
        row_devices, capacity, block_size, col_width
    )
    half = chunk_rows // 2
    chunks = arrived[:, capacity * block_size :]
    total = chunks[:, :half].astype(jnp.float32) + chunks[:, half:].astype(jnp.float32)
    node_total = local_rows * row_devices
    weight_grad = total.reshape(col_devices * col_width, col_width) / math.sqrt(node_total)
    placing = (wanted[:, :, None] == local_ids[None, None, :]).astype(jnp.float32)
    feature_grad = jnp.einsum(
        "scb,scif->bif", placing, received.astype(jnp.float32), precision=lax.Precision.HIGHEST
    ).reshape(local_rows, col_width)
    return (activated.astype(jnp.bfloat16), weight_grad, feature_grad.astype(jnp.bfloat16))


def solution(mesh):
    return jax.shard_map(
        per_device,
        mesh=mesh,
        in_specs=(
            P("rows", "cols"),
            P(),
            P("rows", None, None),
            P("rows"),
            P("rows", None),
            P("rows"),
            P("rows"),
        ),
        out_specs=(P("rows", "cols"), P(None, "cols"), P("rows", "cols")),
        check_vma=False,
    )
```

time: 375 us -> 414 us (1.10)
  the two profiles are of different devices: /device:TPU:8 before, /device:TPU:1 now
where the time goes in v7:
time: 414 us; the launch traced here: 412 us
  blocking collectives  154 us (37%)
  waiting for transfers between devices  148 us (36%)
  starting transfers between devices  40.4 us (10%)
  local copies, waits for them, and re-layouts  35.8 us (9%)
  between operations  14.3 us (3%)
  matrix products  13.3 us (3%)
  other arithmetic  5.78 us (1%)
    all_to_all x1, blocking collectives, rows_exchange(): return lax.all_to_all(x, 'rows', split_axis=0, concat_axis=0, tiled=True)  154 us
    all_to_all x3, waiting for transfers between devices, rows_exchange(): return lax.all_to_all(x, 'rows', split_axis=0, concat_axis=0, tiled=True)  117 us
    all_to_all x3, starting transfers between devices, rows_exchange(): return lax.all_to_all(x, 'rows', split_axis=0, concat_axis=0, tiled=True)  40.3 us
    all_gather x1, waiting for transfers between devices, per_device(): aggregated_all = lax.all_gather(aggregated, 'cols', axis=0, tiled=False)  31.3 us
  transfers between devices with their start and end apart: 5, of which 4 were waited for; matrix products, arithmetic and copies ran while one was open for 1% of the time, Pallas kernels for 0%

profile of v7, /device:TPU:1, one launch (start us, length us, event | category | flops | bytes accessed | tf_op | source)
XLA Modules:
  0.0 411.6 jit_solution(15842052127569564738)
XLA Ops:
  7.2 1.0 convert_reduce_fusion
  8.2 0.7 iota_compare_fusion.1
  8.9 0.8 fusion.20
  9.7 0.7 copy.66
  10.4 19.3 %all-to-all-start = ((s32[64,1,2]{2,1,0:T(1,128)}), s32[64,1,2]{2,1,0:T(1,128)S(1)}, u32[]{:S(2)}, u32[]{:S(2)}) async-start(s32[64,1,2]{2,1,0:T(1,128)} %copy.66), calls=%async_computation | async-start | bytes 65536 | tf_op jit(solution)/shard_map/all_to_all | solution.py:16
  29.7 0.9 copy_bitcast_fusion.2
  30.7 12.3 %all-to-all-done = s32[64,1,2]{2,1,0:T(1,128)S(1)} async-done(((s32[64,1,2]{2,1,0:T(1,128)}), s32[64,1,2]{2,1,0:T(1,128)S(1)}, u32[]{:S(2)}, u32[]{:S(2)}) %all-to-all-start) | async-done | bytes 544 | tf_op jit(solution)/shard_map/all_to_all | solution.py:16
  43.0 0.1 copy.68
  43.1 0.1 reshape.172
  43.3 2.1 gather_fusion
  45.4 5.7 %all-to-all-start.1 = ((bf16[64,2,128,64]{2,3,1,0:T(8,128)(2,1)}), bf16[64,2,128,64]{2,3,1,0:T(8,128)(2,1)}, u32[]{:S(2)}, u32[]{:S(2)}) async-start(bf16[64,2,128,64]{2,3,1,0:T(8,128)(2,1)} %bitcast.75), calls=%async_computation.1 | async-start | bytes 4194304 | tf_op jit(solution)/shard_map/all_to_all | solution.py:16
  51.2 90.7 %all-to-all-done.1 = bf16[64,2,128,64]{2,3,1,0:T(8,128)(2,1)} async-done(((bf16[64,2,128,64]{2,3,1,0:T(8,128)(2,1)}), bf16[64,2,128,64]{2,3,1,0:T(8,128)(2,1)}, u32[]{:S(2)}, u32[]{:S(2)}) %all-to-all-start.1) | async-done | bytes 2097184 | tf_op jit(solution)/shard_map/all_to_all | solution.py:16
  141.9 2.4 gather_fusion.1
  144.3 1.5 convolution_bitcast_fusion
  145.8 2.0 fusion.11
  147.8 0.7 convert_element_type.60
  148.6 1.0 constant_dynamic-slice_fusion
  149.6 31.3 %all-gather.3.cloned.1.call-done = bf16[8,1024,64]{1,2,0:T(8,128)(2,1)} async-done(((bf16[1,1024,64]{1,2,0:T(8,128)(2,1)}), bf16[8,1024,64]{1,2,0:T(8,128)(2,1)}) %all-gather.3.cloned.1.call-update) | async-done | bytes 1048592 | tf_op jit(solution)/shard_map/all_gather | solution.py:46
  181.0 2.4 multiply_convert_fusion
  183.4 1.3 fusion.17
  184.7 0.8 reshape.209
  185.6 15.4 %all-to-all-start.2 = ((f32[64,1,512]{2,1,0:T(1,128)}), f32[64,1,512]{2,1,0:T(1,128)S(1)}, u32[]{:S(2)}, u32[]{:S(2)}) async-start(f32[64,1,512]{2,1,0:T(1,128)} %reshape.209), calls=%async_computation.2 | async-start | bytes 262144 | tf_op jit(solution)/shard_map/all_to_all | solution.py:16
  201.0 0.1 copy.74
  201.1 0.1 reshape.194
  201.2 14.1 %all-to-all-done.2 = f32[64,1,512]{2,1,0:T(1,128)S(1)} async-done(((f32[64,1,512]{2,1,0:T(1,128)}), f32[64,1,512]{2,1,0:T(1,128)S(1)}, u32[]{:S(2)}, u32[]{:S(2)}) %all-to-all-start.2) | async-done | bytes 131104 | tf_op jit(solution)/shard_map/all_to_all | solution.py:16
  215.3 0.5 broadcast.159
  215.9 0.9 reduce
  216.8 0.1 reshape.210
  217.0 0.1 copy.76
  217.1 1.6 fusion.14
  218.7 0.7 gather_fusion.2
  219.5 0.7 fusion.4
  220.3 2.1 gather_fusion.3
  222.4 4.3 %copy.75 = bf16[128,128,64]{1,0,2:T(8,128)(2,1)} copy(bf16[128,128,64]{1,2,0:T(8,128)(2,1)} %gather_fusion.3) | data formatting | bytes 4194304 | tf_op jit(solution)/shard_map/gather | solution.py:76
  226.7 4.0 reshape.168
  230.7 0.1 broadcast_in_dim.26
  230.9 2.1 pad_maximum_fusion
  233.0 1.9 copy.77
  234.9 153.5 %all_to_all.27 = bf16[64,272,64]{1,2,0:T(8,128)(2,1)S(1)} all-to-all(bf16[64,272,64]{1,2,0:T(8,128)(2,1)S(1)} %copy.77), channel_id=1, replica_groups=mesh['rows'=64,'cols'=8] {'rows'}, dimensions={0} | all-to-all | bytes 4456448 | tf_op jit(solution)/shard_map/all_to_all | solution.py:16
  388.4 1.8 fusion.36
  390.2 0.1 copy-done.1
  390.3 1.6 copy.87
  391.9 0.4 copy.86
  392.3 0.8 copy.82
  393.0 3.2 slice.25
  396.2 4.0 reshape.169
  400.2 3.9 fusion.8
  404.1 0.7 copy.104
  (33 shorter events, 0.5 us)
Async XLA Ops:
  7.2 137.1 %copy-start = (bf16[64,128,128]{2,1,0:T(8,128)(2,1)S(1)}, bf16[64,128,128]{2,1,0:T(8,128)(2,1)}, u32[]{:S(2)}) copy-start(bf16[64,128,128]{2,1,0:T(8,128)(2,1)} %param.9) | copy-start | bytes 6291460
  10.4 32.5 %all-to-all-start = ((s32[64,1,2]{2,1,0:T(1,128)}), s32[64,1,2]{2,1,0:T(1,128)S(1)}, u32[]{:S(2)}, u32[]{:S(2)}) async-start(s32[64,1,2]{2,1,0:T(1,128)} %copy.66), calls=%async_computation | async-start | bytes 65536 | tf_op jit(solution)/shard_map/all_to_all | solution.py:16
  45.4 5.7 %copy-start.4 = (s32[64,1]{0,1:T(1,128)S(1)}, s32[64,1]{0,1:T(1,128)}, u32[]{:S(2)}) copy-start(s32[64,1]{0,1:T(1,128)} %param.11) | copy-start | bytes 772
  45.4 96.5 %all-to-all-start.1 = ((bf16[64,2,128,64]{2,3,1,0:T(8,128)(2,1)}), bf16[64,2,128,64]{2,3,1,0:T(8,128)(2,1)}, u32[]{:S(2)}, u32[]{:S(2)}) async-start(bf16[64,2,128,64]{2,3,1,0:T(8,128)(2,1)} %bitcast.75), calls=%async_computation.1 | async-start | bytes 4194304 | tf_op jit(solution)/shard_map/all_to_all | solution.py:16
  51.1 129.9 %all-gather.3.cloned.1.call-start = ((), (), s32[]{:S(2)}) async-start(), calls=%async_computation.4 | async-start | bytes 1179648 | tf_op jit(solution)/shard_map/all_gather | solution.py:46
  144.3 1.5 copy-start.3
  145.8 35.1 %copy-start.5 = (s32[1024]{0:T(1024)S(1)}, s32[1024]{0:T(1024)}, u32[]{:S(2)}) copy-start(s32[1024]{0:T(1024)} %param.13) | copy-start | bytes 12292
  148.5 68.6 %all-gather.5.cloned.1.call-start = ((), (), s32[]{:S(2)}) async-start(), calls=%async_computation.5 | async-start | bytes 1179648 | tf_op jit(solution)/shard_map/all_gather | solution.py:58
  181.0 2.4 copy-start.2
  185.6 29.8 %all-to-all-start.2 = ((f32[64,1,512]{2,1,0:T(1,128)}), f32[64,1,512]{2,1,0:T(1,128)S(1)}, u32[]{:S(2)}, u32[]{:S(2)}) async-start(f32[64,1,512]{2,1,0:T(1,128)} %reshape.209), calls=%async_computation.2 | async-start | bytes 262144 | tf_op jit(solution)/shard_map/all_to_all | solution.py:16
  388.4 1.9 copy-start.1
Sparse Core Ops, SparseCore 0:
  148.7 32.2 all-gather.2
  183.7 30.7 all-gather.4

commit v8 on v7

--- a/solution.py
+++ b/solution.py
@@ -3,7 +3,50 @@
 import jax
 import jax.numpy as jnp
 from jax import lax
+from jax.experimental import pallas as pl
+from jax.experimental.pallas import tpu as pltpu
 from jax.sharding import PartitionSpec as P
+
+MESH = pl.DeviceIdType.MESH
+
+
+def _cols_gather_kernel(x_ref, o_ref, send_sems, recv_sems):
+    n = o_ref.shape[0]
+    me = lax.axis_index("cols")
+    barrier = pltpu.get_barrier_semaphore()
+    for k in range(1, n):
+        pl.semaphore_signal(
+            barrier, 1, device_id={"cols": lax.rem(me + k, n)}, device_id_type=MESH
+        )
+    pl.semaphore_wait(barrier, n - 1)
+    copies = []
+    for k in range(1, n):
+        peer = lax.rem(me + k, n)
+        src = lax.rem(me + n - k, n)
+        out = pltpu.make_async_remote_copy(
+            src_ref=x_ref, dst_ref=o_ref.at[me], send_sem=send_sems.at[k],
+            recv_sem=recv_sems.at[k], device_id={"cols": peer}, device_id_type=MESH)
+        out.start()
+        back = pltpu.make_async_remote_copy(
+            src_ref=x_ref, dst_ref=o_ref.at[src], send_sem=send_sems.at[k],
+            recv_sem=recv_sems.at[k], device_id={"cols": src}, device_id_type=MESH)
+        copies.append((out, back))
+    o_ref[me] = x_ref[...]
+    for out, back in copies:
+        out.wait_send()
+        back.wait_recv()
+
+
+def cols_gather(x):
+    n = lax.axis_size("cols")
+    return pl.pallas_call(
+        _cols_gather_kernel,
+        out_shape=jax.ShapeDtypeStruct((n,) + x.shape, x.dtype),
+        in_specs=[pl.BlockSpec(memory_space=pltpu.VMEM)],
+        out_specs=pl.BlockSpec(memory_space=pltpu.VMEM),
+        scratch_shapes=[pltpu.SemaphoreType.DMA((n,)), pltpu.SemaphoreType.DMA((n,))],
+        compiler_params=pltpu.CompilerParams(collective_id=2, has_side_effects=True),
+    )(x)
 
 
 def slot_ranks(owners):
@@ -43,7 +86,8 @@
     )
     summed = jnp.einsum("tb,tif->bif", row_onehot, products, precision=lax.Precision.HIGHEST)
     aggregated = summed.reshape(local_rows, col_width).astype(jnp.bfloat16)
-    aggregated_all = lax.all_gather(aggregated, "cols", axis=0, tiled=False)
+    packed = cols_gather(aggregated.reshape(local_rows // 2, 2 * col_width))
+    aggregated_all = packed.reshape(col_devices, local_rows, col_width)
     col_index = lax.axis_index("cols")
     w_columns = lax.dynamic_slice_in_dim(weight, col_index * col_width, col_width, 1)
     w_rows = lax.dynamic_slice_in_dim(weight, col_index * col_width, col_width, 0)
@@ -61,10 +105,11 @@
     ).reshape(col_devices * col_width, col_width)
     pieces = weight_terms.reshape(row_devices, -1, col_width)
     reduced = jnp.sum(rows_exchange(pieces), axis=0)
-    high = reduced.astype(jnp.bfloat16)
-    low = (reduced - high.astype(jnp.float32)).astype(jnp.bfloat16)
-    chunk = jnp.concatenate([high, low], axis=0)
-    chunk_rows = chunk.shape[0]
+    spread = jnp.broadcast_to(reduced[None], (row_devices,) + reduced.shape)
+    node_total = local_rows * row_devices
+    weight_grad = rows_exchange(spread).reshape(col_devices * col_width, col_width) / math.sqrt(
+        node_total
+    )
     agg_grad = jnp.einsum("nc,kc->nk", grad_all, w_rows, preferred_element_type=jnp.float32).astype(
         jnp.bfloat16
     )
@@ -73,19 +118,7 @@
         "tji,tjf->tif", tile_values, grad_rows, preferred_element_type=jnp.float32
     ).astype(jnp.bfloat16)
     padded_terms = jnp.concatenate([sent_terms, jnp.zeros_like(sent_terms[:1])], axis=0)
-    send_terms = padded_terms[slot_tile].reshape(row_devices, capacity * block_size, col_width)
-    payload = jnp.concatenate(
-        [send_terms, jnp.broadcast_to(chunk[None], (row_devices,) + chunk.shape)], axis=1
-    )
-    arrived = rows_exchange(payload)
-    received = arrived[:, : capacity * block_size].reshape(
-        row_devices, capacity, block_size, col_width
-    )
-    half = chunk_rows // 2
-    chunks = arrived[:, capacity * block_size :]
-    total = chunks[:, :half].astype(jnp.float32) + chunks[:, half:].astype(jnp.float32)
-    node_total = local_rows * row_devices
-    weight_grad = total.reshape(col_devices * col_width, col_width) / math.sqrt(node_total)
+    received = rows_exchange(padded_terms[slot_tile])
     placing = (wanted[:, :, None] == local_ids[None, None, :]).astype(jnp.float32)
     feature_grad = jnp.einsum(
         "scb,scif->bif", placing, received.astype(jnp.float32), precision=lax.Precision.HIGHEST

time: 414 us -> 352 us (0.85)
  blocking collectives: 154 us -> 0 us
  waiting for transfers between devices: 148 us -> 211 us
  Pallas kernels: 0 us -> 26.9 us
  local copies, waits for them, and re-layouts: 35.8 us -> 26.5 us
  starting transfers between devices: 40.4 us -> 49.3 us
    all_to_all x1 -> x0, blocking collectives: 154 us -> none  [rows_exchange(): return lax.all_to_all(x, 'rows', split_axis=0, concat_axis=0, tiled=True)]
    all_to_all x3 -> x5, waiting for transfers between devices: 117 us -> 211 us  [rows_exchange(): return lax.all_to_all(x, 'rows', split_axis=0, concat_axis=0, tiled=True)]
    all_gather x1 -> x0, waiting for transfers between devices: 31.3 us -> none  [per_device(): aggregated_all = lax.all_gather(aggregated, 'cols', axis=0, tiled=False)]
    pallas_call x0 -> x1, Pallas kernels: none -> 26.9 us  [cols_gather(): pl.pallas_call(_cols_gather_kernel, out_shape=jax.ShapeDtypeStruct((n,) +...]
    all_to_all x3 -> x5, starting transfers between devices: 40.3 us -> 49.2 us  [rows_exchange(): return lax.all_to_all(x, 'rows', split_axis=0, concat_axis=0, tiled=True)]
    slice x2 -> x0, local copies, waits for them, and re-layouts: 5.04 us -> none  [the longest x1 3.19 us: per_device(): arrived[:, :capacity * block_size]]
  transfers between devices with their start and end apart: 5 -> 6, of which waited for: 4 -> 5; matrix products, arithmetic and copies ran while one was open for 1% -> 6% of each run, Pallas kernels for 0% -> 0%
where the time goes in v8:
time: 352 us; the launch traced here: 346 us
  waiting for transfers between devices  211 us (60%)
  starting transfers between devices  49.3 us (14%)
  Pallas kernels  26.9 us (8%)
  local copies, waits for them, and re-layouts  26.5 us (8%)
  between operations  14.3 us (4%)
  matrix products  13.1 us (4%)
  other arithmetic  4.39 us (1%)
    all_to_all x5, waiting for transfers between devices, rows_exchange(): return lax.all_to_all(x, 'rows', split_axis=0, concat_axis=0, tiled=True)  211 us
    all_to_all x5, starting transfers between devices, rows_exchange(): return lax.all_to_all(x, 'rows', split_axis=0, concat_axis=0, tiled=True)  49.2 us
    pallas_call x1, Pallas kernels, cols_gather(): pl.pallas_call(_cols_gather_kernel, out_shape=jax.ShapeDtypeStruct((n,) +...  26.9 us
    gather x2, local copies, waits for them, and re-layouts, per_device(): received = rows_exchange(padded_terms[slot_tile])  7.21 us
  transfers between devices with their start and end apart: 6, of which 5 were waited for; matrix products, arithmetic and copies ran while one was open for 6% of the time, Pallas kernels for 0%

profile of v8, /device:TPU:1, one launch (start us, length us, event | category | flops | bytes accessed | tf_op | source)
XLA Modules:
  0.0 345.6 jit_solution(10655697100281893050)
XLA Ops:
  7.2 1.0 convert_reduce_fusion
  8.2 0.7 iota_compare_fusion.1
  8.9 0.8 fusion.20
  9.7 0.7 copy.53
  10.4 19.3 %all-to-all-start = ((s32[64,1,2]{2,1,0:T(1,128)}), s32[64,1,2]{2,1,0:T(1,128)S(1)}, u32[]{:S(2)}, u32[]{:S(2)}) async-start(s32[64,1,2]{2,1,0:T(1,128)} %copy.53), calls=%async_computation | async-start | bytes 65536 | tf_op jit(solution)/shard_map/all_to_all | solution.py:59
  29.7 0.9 copy_bitcast_fusion.2
  30.7 12.3 %all-to-all-done = s32[64,1,2]{2,1,0:T(1,128)S(1)} async-done(((s32[64,1,2]{2,1,0:T(1,128)}), s32[64,1,2]{2,1,0:T(1,128)S(1)}, u32[]{:S(2)}, u32[]{:S(2)}) %all-to-all-start) | async-done | bytes 544 | tf_op jit(solution)/shard_map/all_to_all | solution.py:59
  43.0 0.1 copy.55
  43.1 0.1 reshape.161
  43.3 2.1 gather_fusion
  45.4 5.7 %all-to-all-start.1 = ((bf16[64,2,128,64]{2,3,1,0:T(8,128)(2,1)}), bf16[64,2,128,64]{2,3,1,0:T(8,128)(2,1)}, u32[]{:S(2)}, u32[]{:S(2)}) async-start(bf16[64,2,128,64]{2,3,1,0:T(8,128)(2,1)} %bitcast.71), calls=%async_computation.1 | async-start | bytes 4194304 | tf_op jit(solution)/shard_map/all_to_all | solution.py:59
  51.2 1.0 constant_dynamic-slice_fusion
  52.2 89.7 %all-to-all-done.1 = bf16[64,2,128,64]{2,3,1,0:T(8,128)(2,1)} async-done(((bf16[64,2,128,64]{2,3,1,0:T(8,128)(2,1)}), bf16[64,2,128,64]{2,3,1,0:T(8,128)(2,1)}, u32[]{:S(2)}, u32[]{:S(2)}) %all-to-all-start.1) | async-done | bytes 2097184 | tf_op jit(solution)/shard_map/all_to_all | solution.py:59
  141.9 2.4 gather_fusion.1
  144.3 1.5 convolution_bitcast_fusion
  145.8 2.0 fusion.11
  147.8 0.2 copy.58
  148.0 0.8 convert_element_type.39.x_ref
  148.8 26.9 %shard_map.97 = bf16[8,512,128]{2,1,0:T(8,128)(2,1)} custom-call(bf16[512,128]{1,0:T(8,128)(2,1)} %convert_element_type.39.x_ref), custom_call_target="tpu_custom_call" | custom-call | tf_op jit(solution)/shard_map/pallas_call | solution.py:42
  175.7 3.9 %reshape.156 = bf16[8,1024,64]{2,1,0:T(8,128)(2,1)} reshape(bf16[8,512,128]{2,1,0:T(8,128)(2,1)} %shard_map.97) | data formatting | bytes 2097152 | tf_op jit(solution)/shard_map/reshape | solution.py:90
  179.6 3.1 multiply_convert_fusion
  182.7 1.9 copy.62
  184.7 0.4 fusion.17
  185.1 0.8 reshape.197
  185.9 7.1 %all-to-all-start.2 = ((f32[64,1,512]{2,1,0:T(1,128)}), f32[64,1,512]{2,1,0:T(1,128)S(1)}, u32[]{:S(2)}, u32[]{:S(2)}) async-start(f32[64,1,512]{2,1,0:T(1,128)} %reshape.197), calls=%async_computation.2 | async-start | bytes 262144 | tf_op jit(solution)/shard_map/all_to_all | solution.py:59
  193.0 0.1 copy.65
  193.1 0.1 reshape.183
  193.3 15.3 %all-to-all-done.2 = f32[64,1,512]{2,1,0:T(1,128)S(1)} async-done(((f32[64,1,512]{2,1,0:T(1,128)}), f32[64,1,512]{2,1,0:T(1,128)S(1)}, u32[]{:S(2)}, u32[]{:S(2)}) %all-to-all-start.2) | async-done | bytes 131104 | tf_op jit(solution)/shard_map/all_to_all | solution.py:59
  208.6 0.5 broadcast.159
  209.1 0.9 reduce
  210.0 0.1 reshape.198
  210.1 0.1 reduce_sum.41
  210.2 0.8 reshape.199
  211.0 6.4 %all-to-all-start.3 = ((f32[64,1,512]{2,1,0:T(1,128)}), f32[64,1,512]{2,1,0:T(1,128)S(1)}, u32[]{:S(2)}, u32[]{:S(2)}) async-start(f32[64,1,512]{2,1,0:T(1,128)} %reshape.199), calls=%async_computation.3 | async-start | bytes 262144 | tf_op jit(solution)/shard_map/all_to_all | solution.py:59
  217.5 1.6 fusion.14
  219.1 0.7 gather_fusion.2
  219.8 0.7 fusion.4
  220.5 0.1 concatenate.7
  220.6 2.1 gather_fusion.3
  222.7 5.1 %copy.66 = bf16[64,2,128,64]{2,1,3,0:T(2,128)(2,1)} copy(bf16[64,2,128,64]{2,3,1,0:T(8,128)(2,1)} %bitcast.72) | data formatting | bytes 4194304 | tf_op jit(solution)/shard_map/gather | solution.py:121
  227.8 3.9 %all-to-all-done.3 = f32[64,1,512]{2,1,0:T(1,128)S(1)} async-done(((f32[64,1,512]{2,1,0:T(1,128)}), f32[64,1,512]{2,1,0:T(1,128)S(1)}, u32[]{:S(2)}, u32[]{:S(2)}) %all-to-all-start.3) | async-done | bytes 131104 | tf_op jit(solution)/shard_map/all_to_all | solution.py:59
  231.7 10.8 %all-to-all-start.4 = ((bf16[64,2,128,64]{2,1,3,0:T(2,128)(2,1)}), bf16[64,2,128,64]{2,1,3,0:T(2,128)(2,1)}, u32[]{:S(2)}, u32[]{:S(2)}) async-start(bf16[64,2,128,64]{2,1,3,0:T(2,128)(2,1)} %copy.66), calls=%async_computation.4 | async-start | bytes 4194304 | tf_op jit(solution)/shard_map/all_to_all | solution.py:59
  242.5 0.9 reduce.1
  243.4 0.1 reshape.200
  243.5 0.8 copy.68
  244.3 89.9 %all-to-all-done.4 = bf16[64,2,128,64]{2,1,3,0:T(2,128)(2,1)} async-done(((bf16[64,2,128,64]{2,1,3,0:T(2,128)(2,1)}), bf16[64,2,128,64]{2,1,3,0:T(2,128)(2,1)}, u32[]{:S(2)}, u32[]{:S(2)}) %all-to-all-start.4) | async-done | bytes 2097184 | tf_op jit(solution)/shard_map/all_to_all | solution.py:59
  334.2 3.9 %fusion.8 = bf16[8,128,64]{1,0,2:T(8,128)(2,1)S(1)} fusion(bf16[64,2,128,64]{2,1,3,0:T(2,128)(2,1)} %all-to-all-done.4, s32[64,2]{0,1:T(2,128)S(1)} %bitcast.78), kind=kOutput, calls=%fused_computation.13 | convolution fusion | flops 16843776 | bytes 2228736 | tf_op jit(solution)/shard_map/scb,scif->bif/dot_general | solution.py:123
  338.0 0.7 copy.89
  (27 shorter events, 0.3 us)
Async XLA Ops:
  7.2 137.1 %copy-start = (bf16[64,128,128]{2,1,0:T(8,128)(2,1)S(1)}, bf16[64,128,128]{2,1,0:T(8,128)(2,1)}, u32[]{:S(2)}) copy-start(bf16[64,128,128]{2,1,0:T(8,128)(2,1)} %param.9) | copy-start | bytes 6291460
  10.4 32.5 %all-to-all-start = ((s32[64,1,2]{2,1,0:T(1,128)}), s32[64,1,2]{2,1,0:T(1,128)S(1)}, u32[]{:S(2)}, u32[]{:S(2)}) async-start(s32[64,1,2]{2,1,0:T(1,128)} %copy.53), calls=%async_computation | async-start | bytes 65536 | tf_op jit(solution)/shard_map/all_to_all | solution.py:59
  45.4 6.8 %copy-start.3 = (s32[64,1]{0,1:T(1,128)S(1)}, s32[64,1]{0,1:T(1,128)}, u32[]{:S(2)}) copy-start(s32[64,1]{0,1:T(1,128)} %param.11) | copy-start | bytes 772
  45.4 96.5 %all-to-all-start.1 = ((bf16[64,2,128,64]{2,3,1,0:T(8,128)(2,1)}), bf16[64,2,128,64]{2,3,1,0:T(8,128)(2,1)}, u32[]{:S(2)}, u32[]{:S(2)}) async-start(bf16[64,2,128,64]{2,3,1,0:T(8,128)(2,1)} %bitcast.71), calls=%async_computation.1 | async-start | bytes 4194304 | tf_op jit(solution)/shard_map/all_to_all | solution.py:59
  51.1 166.4 %all-gather.2.cloned.1.call-start = ((), (), s32[]{:S(2)}) async-start(), calls=%async_computation.5 | async-start | bytes 1179648 | tf_op jit(solution)/shard_map/all_gather | solution.py:102
  144.3 1.5 copy-start.2
  148.8 30.8 %copy-start.4 = (s32[1024]{0:T(1024)S(1)}, s32[1024]{0:T(1024)}, u32[]{:S(2)}) copy-start(s32[1024]{0:T(1024)} %param.13) | copy-start | bytes 12292
  182.7 2.0 copy-start.1
  185.9 22.7 %all-to-all-start.2 = ((f32[64,1,512]{2,1,0:T(1,128)}), f32[64,1,512]{2,1,0:T(1,128)S(1)}, u32[]{:S(2)}, u32[]{:S(2)}) async-start(f32[64,1,512]{2,1,0:T(1,128)} %reshape.197), calls=%async_computation.2 | async-start | bytes 262144 | tf_op jit(solution)/shard_map/all_to_all | solution.py:59
  211.0 20.7 %all-to-all-start.3 = ((f32[64,1,512]{2,1,0:T(1,128)}), f32[64,1,512]{2,1,0:T(1,128)S(1)}, u32[]{:S(2)}, u32[]{:S(2)}) async-start(f32[64,1,512]{2,1,0:T(1,128)} %reshape.199), calls=%async_computation.3 | async-start | bytes 262144 | tf_op jit(solution)/shard_map/all_to_all | solution.py:59
  231.7 102.5 %all-to-all-start.4 = ((bf16[64,2,128,64]{2,1,3,0:T(2,128)(2,1)}), bf16[64,2,128,64]{2,1,3,0:T(2,128)(2,1)}, u32[]{:S(2)}, u32[]{:S(2)}) async-start(bf16[64,2,128,64]{2,1,3,0:T(2,128)(2,1)} %copy.66), calls=%async_computation.4 | async-start | bytes 4194304 | tf_op jit(solution)/shard_map/all_to_all | solution.py:59
Sparse Core Ops, SparseCore 0:
  182.8 23.3 all-gather.1

commit v9 on v8

--- a/solution.py
+++ b/solution.py
@@ -86,13 +86,12 @@
     )
     summed = jnp.einsum("tb,tif->bif", row_onehot, products, precision=lax.Precision.HIGHEST)
     aggregated = summed.reshape(local_rows, col_width).astype(jnp.bfloat16)
-    packed = cols_gather(aggregated.reshape(local_rows // 2, 2 * col_width))
-    aggregated_all = packed.reshape(col_devices, local_rows, col_width)
+    aggregated_all = cols_gather(aggregated.T)
     col_index = lax.axis_index("cols")
     w_columns = lax.dynamic_slice_in_dim(weight, col_index * col_width, col_width, 1)
     w_rows = lax.dynamic_slice_in_dim(weight, col_index * col_width, col_width, 0)
     w_split = w_columns.reshape(col_devices, col_width, col_width)
-    hidden = jnp.einsum("jnf,jfc->nc", aggregated_all, w_split, preferred_element_type=jnp.float32)
+    hidden = jnp.einsum("jfn,jfc->nc", aggregated_all, w_split, preferred_element_type=jnp.float32)
     sigmoid = jax.nn.sigmoid(hidden)
     activated = hidden * sigmoid
     slopes = sigmoid * (1.0 + hidden * (1.0 - sigmoid))
@@ -101,7 +100,7 @@
     out_grad = ((activated - target) * slopes).astype(jnp.bfloat16)
     grad_all = lax.all_gather(out_grad, "cols", axis=1, tiled=True)
     weight_terms = jnp.einsum(
-        "jnf,nc->jfc", aggregated_all, out_grad, preferred_element_type=jnp.float32
+        "jfn,nc->jfc", aggregated_all, out_grad, preferred_element_type=jnp.float32
     ).reshape(col_devices * col_width, col_width)
     pieces = weight_terms.reshape(row_devices, -1, col_width)
     reduced = jnp.sum(rows_exchange(pieces), axis=0)
@@ -115,13 +114,13 @@
     )
     grad_rows = agg_grad.reshape(local_blocks, block_size, col_width)[tile_row]
     sent_terms = jnp.einsum(
-        "tji,tjf->tif", tile_values, grad_rows, preferred_element_type=jnp.float32
+        "tji,tjf->tfi", tile_values, grad_rows, preferred_element_type=jnp.float32
     ).astype(jnp.bfloat16)
     padded_terms = jnp.concatenate([sent_terms, jnp.zeros_like(sent_terms[:1])], axis=0)
     received = rows_exchange(padded_terms[slot_tile])
     placing = (wanted[:, :, None] == local_ids[None, None, :]).astype(jnp.float32)
     feature_grad = jnp.einsum(
-        "scb,scif->bif", placing, received.astype(jnp.float32), precision=lax.Precision.HIGHEST
+        "scb,scfi->bif", placing, received.astype(jnp.float32), precision=lax.Precision.HIGHEST
     ).reshape(local_rows, col_width)
     return (activated.astype(jnp.bfloat16), weight_grad, feature_grad.astype(jnp.bfloat16))
 

time: 352 us -> 346 us (0.983)
  local copies, waits for them, and re-layouts: 26.5 us -> 20.3 us
    reshape x1 -> x0, local copies, waits for them, and re-layouts: 3.86 us -> none  [per_device(): aggregated_all = packed.reshape(col_devices, local_rows, col_width)]
where the time goes in v9:
time: 346 us; the launch traced here: 340 us
  waiting for transfers between devices  211 us (61%)
  starting transfers between devices  49.3 us (14%)
  Pallas kernels  26.8 us (8%)
  local copies, waits for them, and re-layouts  20.3 us (6%)
  between operations  14.3 us (4%)
  matrix products  13.3 us (4%)
  other arithmetic  4.39 us (1%)
    all_to_all x5, waiting for transfers between devices, rows_exchange(): return lax.all_to_all(x, 'rows', split_axis=0, concat_axis=0, tiled=True)  211 us
    all_to_all x5, starting transfers between devices, rows_exchange(): return lax.all_to_all(x, 'rows', split_axis=0, concat_axis=0, tiled=True)  49.2 us
    pallas_call x1, Pallas kernels, cols_gather(): pl.pallas_call(_cols_gather_kernel, out_shape=jax.ShapeDtypeStruct((n,) +...  26.8 us
    gather x2, local copies, waits for them, and re-layouts, per_device(): received = rows_exchange(padded_terms[slot_tile])  7.21 us
  transfers between devices with their start and end apart: 6, of which 5 were waited for; matrix products, arithmetic and copies ran while one was open for 6% of the time, Pallas kernels for 0%

profile of v9, /device:TPU:1, one launch (start us, length us, event | category | flops | bytes accessed | tf_op | source)
XLA Modules:
  0.0 339.5 jit_solution(18408220690720546821)
XLA Ops:
  7.2 1.0 convert_reduce_fusion
  8.2 0.7 iota_compare_fusion.1
  8.9 0.8 fusion.19
  9.7 0.7 copy.42
  10.4 19.3 %all-to-all-start = ((s32[64,1,2]{2,1,0:T(1,128)}), s32[64,1,2]{2,1,0:T(1,128)S(1)}, u32[]{:S(2)}, u32[]{:S(2)}) async-start(s32[64,1,2]{2,1,0:T(1,128)} %copy.42), calls=%async_computation | async-start | bytes 65536 | tf_op jit(solution)/shard_map/all_to_all | solution.py:59
  29.7 0.9 copy_bitcast_fusion.2
  30.7 12.3 %all-to-all-done = s32[64,1,2]{2,1,0:T(1,128)S(1)} async-done(((s32[64,1,2]{2,1,0:T(1,128)}), s32[64,1,2]{2,1,0:T(1,128)S(1)}, u32[]{:S(2)}, u32[]{:S(2)}) %all-to-all-start) | async-done | bytes 544 | tf_op jit(solution)/shard_map/all_to_all | solution.py:59
  42.9 0.1 copy.43
  43.0 0.1 copy.44
  43.1 0.1 reshape.154
  43.3 2.1 gather_fusion
  45.4 5.7 %all-to-all-start.1 = ((bf16[64,2,128,64]{2,3,1,0:T(8,128)(2,1)}), bf16[64,2,128,64]{2,3,1,0:T(8,128)(2,1)}, u32[]{:S(2)}, u32[]{:S(2)}) async-start(bf16[64,2,128,64]{2,3,1,0:T(8,128)(2,1)} %bitcast.78), calls=%async_computation.1 | async-start | bytes 4194304 | tf_op jit(solution)/shard_map/all_to_all | solution.py:59
  51.1 0.0 all-gather.2.cloned.1.call-start
  51.2 1.0 constant_dynamic-slice_fusion
  52.2 89.7 %all-to-all-done.1 = bf16[64,2,128,64]{2,3,1,0:T(8,128)(2,1)} async-done(((bf16[64,2,128,64]{2,3,1,0:T(8,128)(2,1)}), bf16[64,2,128,64]{2,3,1,0:T(8,128)(2,1)}, u32[]{:S(2)}, u32[]{:S(2)}) %all-to-all-start.1) | async-done | bytes 2097184 | tf_op jit(solution)/shard_map/all_to_all | solution.py:59
  141.9 2.4 gather_fusion.1
  144.3 1.5 convolution_bitcast_fusion
  145.9 2.0 fusion.10
  147.8 0.7 copy.77
  148.5 26.8 %shard_map.97 = bf16[8,64,1024]{2,1,0:T(8,128)(2,1)} custom-call(bf16[64,1024]{1,0:T(8,128)(2,1)} %bitcast.82), custom_call_target="tpu_custom_call" | custom-call | tf_op jit(solution)/shard_map/pallas_call | solution.py:42
  175.3 2.4 multiply_convert_fusion
  177.7 1.3 fusion.16
  179.1 0.8 reshape.190
  179.9 7.1 %all-to-all-start.2 = ((f32[64,1,512]{2,1,0:T(1,128)}), f32[64,1,512]{2,1,0:T(1,128)S(1)}, u32[]{:S(2)}, u32[]{:S(2)}) async-start(f32[64,1,512]{2,1,0:T(1,128)} %reshape.190), calls=%async_computation.2 | async-start | bytes 262144 | tf_op jit(solution)/shard_map/all_to_all | solution.py:59
  187.0 0.1 copy.50
  187.1 0.1 reshape.176
  187.2 15.3 %all-to-all-done.2 = f32[64,1,512]{2,1,0:T(1,128)S(1)} async-done(((f32[64,1,512]{2,1,0:T(1,128)}), f32[64,1,512]{2,1,0:T(1,128)S(1)}, u32[]{:S(2)}, u32[]{:S(2)}) %all-to-all-start.2) | async-done | bytes 131104 | tf_op jit(solution)/shard_map/all_to_all | solution.py:59
  202.6 0.5 broadcast.159
  203.1 0.9 reduce
  204.0 0.1 reshape.191
  204.1 0.1 reduce_sum.41
  204.2 0.8 reshape.192
  205.0 6.4 %all-to-all-start.3 = ((f32[64,1,512]{2,1,0:T(1,128)}), f32[64,1,512]{2,1,0:T(1,128)S(1)}, u32[]{:S(2)}, u32[]{:S(2)}) async-start(f32[64,1,512]{2,1,0:T(1,128)} %reshape.192), calls=%async_computation.3 | async-start | bytes 262144 | tf_op jit(solution)/shard_map/all_to_all | solution.py:59
  211.4 0.0 all-gather.2.cloned.1.call-done
  211.4 1.6 fusion.13
  213.1 0.7 gather_fusion.2
  213.8 0.7 convolution_convert_fusion
  214.5 0.1 concatenate.7
  214.6 2.1 gather_fusion.3
  216.7 5.1 %copy.51 = bf16[64,2,64,128]{3,1,2,0:T(2,128)(2,1)} copy(bf16[64,2,64,128]{3,2,1,0:T(8,128)(2,1)} %bitcast.79) | data formatting | bytes 4194304 | tf_op jit(solution)/shard_map/gather | solution.py:120
  221.8 3.9 %all-to-all-done.3 = f32[64,1,512]{2,1,0:T(1,128)S(1)} async-done(((f32[64,1,512]{2,1,0:T(1,128)}), f32[64,1,512]{2,1,0:T(1,128)S(1)}, u32[]{:S(2)}, u32[]{:S(2)}) %all-to-all-start.3) | async-done | bytes 131104 | tf_op jit(solution)/shard_map/all_to_all | solution.py:59
  225.7 10.8 %all-to-all-start.4 = ((bf16[64,2,64,128]{3,1,2,0:T(2,128)(2,1)}), bf16[64,2,64,128]{3,1,2,0:T(2,128)(2,1)}, u32[]{:S(2)}, u32[]{:S(2)}) async-start(bf16[64,2,64,128]{3,1,2,0:T(2,128)(2,1)} %copy.51), calls=%async_computation.4 | async-start | bytes 4194304 | tf_op jit(solution)/shard_map/all_to_all | solution.py:59
  236.5 0.9 reduce.1
  237.3 0.1 reshape.193
  237.5 0.8 copy.54
  238.2 89.9 %all-to-all-done.4 = bf16[64,2,64,128]{3,1,2,0:T(2,128)(2,1)} async-done(((bf16[64,2,64,128]{3,1,2,0:T(2,128)(2,1)}), bf16[64,2,64,128]{3,1,2,0:T(2,128)(2,1)}, u32[]{:S(2)}, u32[]{:S(2)}) %all-to-all-start.4) | async-done | bytes 2097184 | tf_op jit(solution)/shard_map/all_to_all | solution.py:59
  328.1 3.9 %fusion.7 = bf16[64,128,8]{1,2,0:T(8,128)(2,1)S(1)} fusion(bf16[64,2,64,128]{3,1,2,0:T(2,128)(2,1)} %all-to-all-done.4, s32[64,2]{0,1:T(2,128)S(1)} %bitcast.87), kind=kOutput, calls=%fused_computation.12 | convolution fusion | flops 16843776 | bytes 2228736 | tf_op jit(solution)/shard_map/scb,scfi->bif/dot_general | solution.py:122
  332.0 0.7 copy.76
  (24 shorter events, 0.2 us)
Async XLA Ops:
  7.2 137.1 %copy-start = (bf16[64,128,128]{2,1,0:T(8,128)(2,1)S(1)}, bf16[64,128,128]{2,1,0:T(8,128)(2,1)}, u32[]{:S(2)}) copy-start(bf16[64,128,128]{2,1,0:T(8,128)(2,1)} %param.9) | copy-start | bytes 6291460
  10.4 32.5 %all-to-all-start = ((s32[64,1,2]{2,1,0:T(1,128)}), s32[64,1,2]{2,1,0:T(1,128)S(1)}, u32[]{:S(2)}, u32[]{:S(2)}) async-start(s32[64,1,2]{2,1,0:T(1,128)} %copy.42), calls=%async_computation | async-start | bytes 65536 | tf_op jit(solution)/shard_map/all_to_all | solution.py:59
  45.4 6.8 %copy-start.3 = (s32[64,1]{0,1:T(1,128)S(1)}, s32[64,1]{0,1:T(1,128)}, u32[]{:S(2)}) copy-start(s32[64,1]{0,1:T(1,128)} %param.11) | copy-start | bytes 772
  45.4 96.5 %all-to-all-start.1 = ((bf16[64,2,128,64]{2,3,1,0:T(8,128)(2,1)}), bf16[64,2,128,64]{2,3,1,0:T(8,128)(2,1)}, u32[]{:S(2)}, u32[]{:S(2)}) async-start(bf16[64,2,128,64]{2,3,1,0:T(8,128)(2,1)} %bitcast.78), calls=%async_computation.1 | async-start | bytes 4194304 | tf_op jit(solution)/shard_map/all_to_all | solution.py:59
  51.1 160.3 %all-gather.2.cloned.1.call-start = ((), (), s32[]{:S(2)}) async-start(), calls=%async_computation.5 | async-start | bytes 1179648 | tf_op jit(solution)/shard_map/all_gather | solution.py:101
  144.3 1.5 copy-start.2
  145.8 29.4 %copy-start.4 = (s32[1024]{0:T(1024)S(1)}, s32[1024]{0:T(1024)}, u32[]{:S(2)}) copy-start(s32[1024]{0:T(1024)} %param.13) | copy-start | bytes 12292
  175.3 2.5 copy-start.1
  179.9 22.7 %all-to-all-start.2 = ((f32[64,1,512]{2,1,0:T(1,128)}), f32[64,1,512]{2,1,0:T(1,128)S(1)}, u32[]{:S(2)}, u32[]{:S(2)}) async-start(f32[64,1,512]{2,1,0:T(1,128)} %reshape.190), calls=%async_computation.2 | async-start | bytes 262144 | tf_op jit(solution)/shard_map/all_to_all | solution.py:59
  205.0 20.7 %all-to-all-start.3 = ((f32[64,1,512]{2,1,0:T(1,128)}), f32[64,1,512]{2,1,0:T(1,128)S(1)}, u32[]{:S(2)}, u32[]{:S(2)}) async-start(f32[64,1,512]{2,1,0:T(1,128)} %reshape.192), calls=%async_computation.3 | async-start | bytes 262144 | tf_op jit(solution)/shard_map/all_to_all | solution.py:59
  225.7 102.5 %all-to-all-start.4 = ((bf16[64,2,64,128]{3,1,2,0:T(2,128)(2,1)}), bf16[64,2,64,128]{3,1,2,0:T(2,128)(2,1)}, u32[]{:S(2)}, u32[]{:S(2)}) async-start(bf16[64,2,64,128]{3,1,2,0:T(2,128)(2,1)} %copy.51), calls=%async_computation.4 | async-start | bytes 4194304 | tf_op jit(solution)/shard_map/all_to_all | solution.py:59
Sparse Core Ops, SparseCore 0:
  177.8 23.3 all-gather.1

commit v10 on v9

--- a/solution.py
+++ b/solution.py
@@ -71,12 +71,10 @@
     slot_rank = slot_ranks(owners)
     local_ids = jnp.arange(local_blocks, dtype=jnp.int32)
     row_onehot = (tile_row[:, None] == local_ids[None, :]).astype(jnp.float32)
-    tile_ids = jnp.arange(tiles, dtype=jnp.int32)
     in_slot = (owners[:, None, None] == jnp.arange(row_devices, dtype=jnp.int32)[None, :, None]) & (
         slot_rank[:, None, None] == jnp.arange(capacity, dtype=jnp.int32)[None, None, :]
     )
     request = jnp.sum(jnp.where(in_slot, source_block[:, None, None], 0), axis=0)
-    slot_tile = jnp.sum(jnp.where(in_slot, tile_ids[:, None, None] - tiles, 0), axis=0) + tiles
     wanted = rows_exchange(request)
     own_blocks = node_features.reshape(local_blocks, block_size, col_width)
     incoming = rows_exchange(own_blocks[wanted])
@@ -116,11 +114,16 @@
     sent_terms = jnp.einsum(
         "tji,tjf->tfi", tile_values, grad_rows, preferred_element_type=jnp.float32
     ).astype(jnp.bfloat16)
-    padded_terms = jnp.concatenate([sent_terms, jnp.zeros_like(sent_terms[:1])], axis=0)
-    received = rows_exchange(padded_terms[slot_tile])
-    placing = (wanted[:, :, None] == local_ids[None, None, :]).astype(jnp.float32)
+    slot_pick = in_slot.astype(jnp.bfloat16)
+    send_terms = jnp.einsum(
+        "tos,tfi->osfi", slot_pick, sent_terms, preferred_element_type=jnp.float32
+    ).astype(jnp.bfloat16)
+    received = rows_exchange(
+        send_terms.reshape(row_devices, capacity * col_width, block_size)
+    ).reshape(row_devices, capacity, col_width, block_size)
+    placing = (wanted[:, :, None] == local_ids[None, None, :]).astype(jnp.bfloat16)
     feature_grad = jnp.einsum(
-        "scb,scfi->bif", placing, received.astype(jnp.float32), precision=lax.Precision.HIGHEST
+        "scb,scfi->bif", placing, received, preferred_element_type=jnp.float32
     ).reshape(local_rows, col_width)
     return (activated.astype(jnp.bfloat16), weight_grad, feature_grad.astype(jnp.bfloat16))
 

time: 346 us -> 342 us (0.988)
  local copies, waits for them, and re-layouts: 20.3 us -> 15.6 us
  waiting for transfers between devices: 211 us -> 215 us
    gather x2 -> x0, local copies, waits for them, and re-layouts: 7.21 us -> none  [per_device(): received = rows_exchange(padded_terms[slot_tile])]
    all_to_all x5, waiting for transfers between devices: 211 us -> 215 us  [rows_exchange(): return lax.all_to_all(x, 'rows', split_axis=0, concat_axis=0, tiled=True)]
  transfers between devices with their start and end apart: 6 -> 6, of which waited for: 5 -> 5; matrix products, arithmetic and copies ran while one was open for 6% -> 5% of each run, Pallas kernels for 0% -> 0%
where the time goes in v10:
time: 342 us; the launch traced here: 335 us
  waiting for transfers between devices  215 us (63%)
  starting transfers between devices  45.9 us (13%)
  Pallas kernels  26.8 us (8%)
  local copies, waits for them, and re-layouts  15.6 us (5%)
  between operations  14.3 us (4%)
  matrix products  13.3 us (4%)
  other arithmetic  4.45 us (1%)
    all_to_all x5, waiting for transfers between devices, rows_exchange(): return lax.all_to_all(x, 'rows', split_axis=0, concat_axis=0, tiled=True)  215 us
    all_to_all x5, starting transfers between devices, rows_exchange(): return lax.all_to_all(x, 'rows', split_axis=0, concat_axis=0, tiled=True)  45.9 us
    pallas_call x1, Pallas kernels, cols_gather(): pl.pallas_call(_cols_gather_kernel, out_shape=jax.ShapeDtypeStruct((n,) +...  26.8 us
  transfers between devices with their start and end apart: 6, of which 5 were waited for; matrix products, arithmetic and copies ran while one was open for 5% of the time, Pallas kernels for 0%

profile of v10, /device:TPU:1, one launch (start us, length us, event | category | flops | bytes accessed | tf_op | source)
XLA Modules:
  0.0 335.1 jit_solution(15147770353458619106)
XLA Ops:
  7.2 0.0 copy-start
  7.2 0.9 convert_reduce_fusion
  8.1 0.7 iota_compare_fusion.1
  8.8 0.8 fusion.20
  9.5 0.7 copy.28
  10.3 19.3 %all-to-all-start = ((s32[64,1,2]{2,1,0:T(1,128)}), s32[64,1,2]{2,1,0:T(1,128)S(1)}, u32[]{:S(2)}, u32[]{:S(2)}) async-start(s32[64,1,2]{2,1,0:T(1,128)} %copy.28), calls=%async_computation | async-start | bytes 65536 | tf_op jit(solution)/shard_map/all_to_all | solution.py:59
  29.5 0.9 copy_bitcast_fusion.2
  30.5 12.3 %all-to-all-done = s32[64,1,2]{2,1,0:T(1,128)S(1)} async-done(((s32[64,1,2]{2,1,0:T(1,128)}), s32[64,1,2]{2,1,0:T(1,128)S(1)}, u32[]{:S(2)}, u32[]{:S(2)}) %all-to-all-start) | async-done | bytes 544 | tf_op jit(solution)/shard_map/all_to_all | solution.py:59
  42.8 0.1 copy.29
  42.8 0.1 copy.30
  42.9 0.1 reshape.137
  43.1 2.1 gather_fusion
  45.2 5.7 %all-to-all-start.1 = ((bf16[64,2,128,64]{2,3,1,0:T(8,128)(2,1)}), bf16[64,2,128,64]{2,3,1,0:T(8,128)(2,1)}, u32[]{:S(2)}, u32[]{:S(2)}) async-start(bf16[64,2,128,64]{2,3,1,0:T(8,128)(2,1)} %bitcast.81), calls=%async_computation.1 | async-start | bytes 4194304 | tf_op jit(solution)/shard_map/all_to_all | solution.py:59
  50.9 0.0 all-gather.2.cloned.1.call-start
  51.0 1.0 constant_dynamic-slice_fusion
  52.0 89.7 %all-to-all-done.1 = bf16[64,2,128,64]{2,3,1,0:T(8,128)(2,1)} async-done(((bf16[64,2,128,64]{2,3,1,0:T(8,128)(2,1)}), bf16[64,2,128,64]{2,3,1,0:T(8,128)(2,1)}, u32[]{:S(2)}, u32[]{:S(2)}) %all-to-all-start.1) | async-done | bytes 2097184 | tf_op jit(solution)/shard_map/all_to_all | solution.py:59
  141.7 2.4 gather_fusion.1
  144.1 1.5 convolution_bitcast_fusion
  145.7 0.0 copy-start.4
  145.7 2.0 fusion.10
  147.6 0.7 copy.68
  148.3 26.8 %shard_map.97 = bf16[8,64,1024]{2,1,0:T(8,128)(2,1)} custom-call(bf16[64,1024]{1,0:T(8,128)(2,1)} %bitcast.85), custom_call_target="tpu_custom_call" | custom-call | tf_op jit(solution)/shard_map/pallas_call | solution.py:42
  175.1 2.4 multiply_convert_fusion
  177.5 0.0 all-gather.2.cloned.1.call-update
  177.5 1.3 fusion.18
  178.9 0.8 reshape.166
  179.7 7.1 %all-to-all-start.2 = ((f32[64,1,512]{2,1,0:T(1,128)}), f32[64,1,512]{2,1,0:T(1,128)S(1)}, u32[]{:S(2)}, u32[]{:S(2)}) async-start(f32[64,1,512]{2,1,0:T(1,128)} %reshape.166), calls=%async_computation.2 | async-start | bytes 262144 | tf_op jit(solution)/shard_map/all_to_all | solution.py:59
  186.8 15.6 %all-to-all-done.2 = f32[64,1,512]{2,1,0:T(1,128)S(1)} async-done(((f32[64,1,512]{2,1,0:T(1,128)}), f32[64,1,512]{2,1,0:T(1,128)S(1)}, u32[]{:S(2)}, u32[]{:S(2)}) %all-to-all-start.2) | async-done | bytes 131104 | tf_op jit(solution)/shard_map/all_to_all | solution.py:59
  202.4 0.6 broadcast.111
  203.0 1.0 reduce
  204.0 0.1 reshape.167
  204.1 0.1 reduce_sum.32
  204.2 0.8 reshape.168
  205.0 6.4 %all-to-all-start.3 = ((f32[64,1,512]{2,1,0:T(1,128)}), f32[64,1,512]{2,1,0:T(1,128)S(1)}, u32[]{:S(2)}, u32[]{:S(2)}) async-start(f32[64,1,512]{2,1,0:T(1,128)} %reshape.168), calls=%async_computation.3 | async-start | bytes 262144 | tf_op jit(solution)/shard_map/all_to_all | solution.py:59
  211.4 0.0 all-gather.2.cloned.1.call-done
  211.4 1.6 fusion.13
  213.0 0.7 gather_fusion.2
  213.8 0.7 convolution_convert_fusion.1
  214.5 1.0 convolution_convert_fusion
  215.5 2.7 copy.37
  218.2 7.5 %all-to-all-done.3 = f32[64,1,512]{2,1,0:T(1,128)S(1)} async-done(((f32[64,1,512]{2,1,0:T(1,128)}), f32[64,1,512]{2,1,0:T(1,128)S(1)}, u32[]{:S(2)}, u32[]{:S(2)}) %all-to-all-start.3) | async-done | bytes 131104 | tf_op jit(solution)/shard_map/all_to_all | solution.py:59
  225.7 7.5 %all-to-all-start.4 = ((bf16[64,128,128]{2,1,0:T(8,128)(2,1)}), bf16[64,128,128]{2,1,0:T(8,128)(2,1)}, u32[]{:S(2)}, u32[]{:S(2)}) async-start(bf16[64,128,128]{2,1,0:T(8,128)(2,1)} %copy.37), calls=%async_computation.4 | async-start | bytes 4194304 | tf_op jit(solution)/shard_map/all_to_all | solution.py:59
  233.1 1.0 reduce.1
  234.1 0.1 reshape.169
  234.3 0.8 copy.40
  235.0 89.8 %all-to-all-done.4 = bf16[64,128,128]{2,1,0:T(8,128)(2,1)} async-done(((bf16[64,128,128]{2,1,0:T(8,128)(2,1)}), bf16[64,128,128]{2,1,0:T(8,128)(2,1)}, u32[]{:S(2)}, u32[]{:S(2)}) %all-to-all-start.4) | async-done | bytes 2097184 | tf_op jit(solution)/shard_map/all_to_all | solution.py:59
  324.8 2.8 fusion.7
  327.6 0.7 copy.67
  (18 shorter events, 0.1 us)
Async XLA Ops:
  7.2 136.9 %copy-start = (bf16[64,128,128]{2,1,0:T(8,128)(2,1)S(1)}, bf16[64,128,128]{2,1,0:T(8,128)(2,1)}, u32[]{:S(2)}) copy-start(bf16[64,128,128]{2,1,0:T(8,128)(2,1)} %param.9) | copy-start | bytes 6291460
  10.3 32.5 %all-to-all-start = ((s32[64,1,2]{2,1,0:T(1,128)}), s32[64,1,2]{2,1,0:T(1,128)S(1)}, u32[]{:S(2)}, u32[]{:S(2)}) async-start(s32[64,1,2]{2,1,0:T(1,128)} %copy.28), calls=%async_computation | async-start | bytes 65536 | tf_op jit(solution)/shard_map/all_to_all | solution.py:59
  45.2 6.8 %copy-start.3 = (s32[64,1]{0,1:T(1,128)S(1)}, s32[64,1]{0,1:T(1,128)}, u32[]{:S(2)}) copy-start(s32[64,1]{0,1:T(1,128)} %param.11) | copy-start | bytes 772
  45.2 96.5 %all-to-all-start.1 = ((bf16[64,2,128,64]{2,3,1,0:T(8,128)(2,1)}), bf16[64,2,128,64]{2,3,1,0:T(8,128)(2,1)}, u32[]{:S(2)}, u32[]{:S(2)}) async-start(bf16[64,2,128,64]{2,3,1,0:T(8,128)(2,1)} %bitcast.81), calls=%async_computation.1 | async-start | bytes 4194304 | tf_op jit(solution)/shard_map/all_to_all | solution.py:59
  50.9 160.5 %all-gather.2.cloned.1.call-start = ((), (), s32[]{:S(2)}) async-start(), calls=%async_computation.5 | async-start | bytes 1179648 | tf_op jit(solution)/shard_map/all_gather | solution.py:99
  144.1 1.5 copy-start.2
  145.7 29.4 %copy-start.4 = (s32[1024]{0:T(1024)S(1)}, s32[1024]{0:T(1024)}, u32[]{:S(2)}) copy-start(s32[1024]{0:T(1024)} %param.13) | copy-start | bytes 12292
  175.1 2.5 copy-start.1
  179.7 22.7 %all-to-all-start.2 = ((f32[64,1,512]{2,1,0:T(1,128)}), f32[64,1,512]{2,1,0:T(1,128)S(1)}, u32[]{:S(2)}, u32[]{:S(2)}) async-start(f32[64,1,512]{2,1,0:T(1,128)} %reshape.166), calls=%async_computation.2 | async-start | bytes 262144 | tf_op jit(solution)/shard_map/all_to_all | solution.py:59
  205.0 20.7 %all-to-all-start.3 = ((f32[64,1,512]{2,1,0:T(1,128)}), f32[64,1,512]{2,1,0:T(1,128)S(1)}, u32[]{:S(2)}, u32[]{:S(2)}) async-start(f32[64,1,512]{2,1,0:T(1,128)} %reshape.168), calls=%async_computation.3 | async-start | bytes 262144 | tf_op jit(solution)/shard_map/all_to_all | solution.py:59
  225.7 99.1 %all-to-all-start.4 = ((bf16[64,128,128]{2,1,0:T(8,128)(2,1)}), bf16[64,128,128]{2,1,0:T(8,128)(2,1)}, u32[]{:S(2)}, u32[]{:S(2)}) async-start(bf16[64,128,128]{2,1,0:T(8,128)(2,1)} %copy.37), calls=%async_computation.4 | async-start | bytes 4194304 | tf_op jit(solution)/shard_map/all_to_all | solution.py:59
Sparse Core Ops, SparseCore 0:
  177.7 23.3 all-gather.1

commit v11 on v10

--- a/solution.py
+++ b/solution.py
@@ -37,7 +37,7 @@
         back.wait_recv()
 
 
-def cols_gather(x):
+def cols_gather(x, collective_id):
     n = lax.axis_size("cols")
     return pl.pallas_call(
         _cols_gather_kernel,
@@ -45,7 +45,7 @@
         in_specs=[pl.BlockSpec(memory_space=pltpu.VMEM)],
         out_specs=pl.BlockSpec(memory_space=pltpu.VMEM),
         scratch_shapes=[pltpu.SemaphoreType.DMA((n,)), pltpu.SemaphoreType.DMA((n,))],
-        compiler_params=pltpu.CompilerParams(collective_id=2, has_side_effects=True),
+        compiler_params=pltpu.CompilerParams(collective_id=collective_id, has_side_effects=True),
     )(x)
 
 
@@ -84,7 +84,7 @@
     )
     summed = jnp.einsum("tb,tif->bif", row_onehot, products, precision=lax.Precision.HIGHEST)
     aggregated = summed.reshape(local_rows, col_width).astype(jnp.bfloat16)
-    aggregated_all = cols_gather(aggregated.T)
+    aggregated_all = cols_gather(aggregated.T, 2)
     col_index = lax.axis_index("cols")
     w_columns = lax.dynamic_slice_in_dim(weight, col_index * col_width, col_width, 1)
     w_rows = lax.dynamic_slice_in_dim(weight, col_index * col_width, col_width, 0)
@@ -96,7 +96,7 @@
     feature_ids = col_index * col_width + jnp.arange(col_width, dtype=jnp.int32)
     target = (labels[:, None] == feature_ids[None, :]).astype(jnp.float32)
     out_grad = ((activated - target) * slopes).astype(jnp.bfloat16)
-    grad_all = lax.all_gather(out_grad, "cols", axis=1, tiled=True)
+    grad_all = cols_gather(out_grad.T, 3)
     weight_terms = jnp.einsum(
         "jfn,nc->jfc", aggregated_all, out_grad, preferred_element_type=jnp.float32
     ).reshape(col_devices * col_width, col_width)
@@ -107,9 +107,12 @@
     weight_grad = rows_exchange(spread).reshape(col_devices * col_width, col_width) / math.sqrt(
         node_total
     )
-    agg_grad = jnp.einsum("nc,kc->nk", grad_all, w_rows, preferred_element_type=jnp.float32).astype(
-        jnp.bfloat16
-    )
+    agg_grad = jnp.einsum(
+        "jcn,kjc->nk",
+        grad_all,
+        w_rows.reshape(col_width, col_devices, col_width),
+        preferred_element_type=jnp.float32,
+    ).astype(jnp.bfloat16)
     grad_rows = agg_grad.reshape(local_blocks, block_size, col_width)[tile_row]
     sent_terms = jnp.einsum(
         "tji,tjf->tfi", tile_values, grad_rows, preferred_element_type=jnp.float32

time: 342 us -> 342 us (level); the launches traced: 335 us -> 339 us
  Pallas kernels: 26.8 us -> 44.6 us
  between operations: 14.3 us -> 0.89 us
  waiting for transfers between devices: 215 us -> 205 us
  starting transfers between devices: 45.9 us -> 53.4 us
    pallas_call x1 -> x2, Pallas kernels: 26.8 us -> 44.6 us  [cols_gather(): pl.pallas_call(_cols_gather_kernel, out_shape=jax.ShapeDtypeStruct((n,) +...]
    all_to_all x5, waiting for transfers between devices: 215 us -> 205 us  [rows_exchange(): return lax.all_to_all(x, 'rows', split_axis=0, concat_axis=0, tiled=True)]
    all_to_all x5, starting transfers between devices: 45.9 us -> 53.4 us  [rows_exchange(): return lax.all_to_all(x, 'rows', split_axis=0, concat_axis=0, tiled=True)]
  transfers between devices with their start and end apart: 6 -> 5, of which waited for: 5 -> 4; matrix products, arithmetic and copies ran while one was open for 5% -> 4% of each run, Pallas kernels for 0% -> 5%
where the time goes in v11:
time: 342 us; the launch traced here: 339 us
  waiting for transfers between devices  205 us (60%)
  starting transfers between devices  53.4 us (16%)
  Pallas kernels  44.6 us (13%)
  local copies, waits for them, and re-layouts  16.5 us (5%)
  matrix products  13.5 us (4%)
  other arithmetic  5.19 us (2%)
    all_to_all x5, waiting for transfers between devices, rows_exchange(): return lax.all_to_all(x, 'rows', split_axis=0, concat_axis=0, tiled=True)  205 us
    all_to_all x5, starting transfers between devices, rows_exchange(): return lax.all_to_all(x, 'rows', split_axis=0, concat_axis=0, tiled=True)  53.4 us
    pallas_call x2, Pallas kernels, cols_gather(): pl.pallas_call(_cols_gather_kernel, out_shape=jax.ShapeDtypeStruct((n,) +...  44.6 us
  transfers between devices with their start and end apart: 5, of which 4 were waited for; matrix products, arithmetic and copies ran while one was open for 4% of the time, Pallas kernels for 5%

profile of v11, /device:TPU:1, one launch (start us, length us, event | category | flops | bytes accessed | tf_op | source)
XLA Modules:
  0.0 339.2 jit_solution(7658371923625778141)
XLA Ops:
  0.6 0.0 copy-start
  0.6 0.9 convert_reduce_fusion
  1.6 0.7 iota_compare_fusion.1
  2.2 0.8 fusion.39
  3.0 0.7 copy.30
  3.7 19.3 %all-to-all-start = ((s32[64,1,2]{2,1,0:T(1,128)}), s32[64,1,2]{2,1,0:T(1,128)S(1)}, u32[]{:S(2)}, u32[]{:S(2)}) async-start(s32[64,1,2]{2,1,0:T(1,128)} %copy.30), calls=%async_computation | async-start | bytes 65536 | tf_op jit(solution)/shard_map/all_to_all | solution.py:59
  23.0 0.9 copy_bitcast_fusion.2
  23.9 12.3 %all-to-all-done = s32[64,1,2]{2,1,0:T(1,128)S(1)} async-done(((s32[64,1,2]{2,1,0:T(1,128)}), s32[64,1,2]{2,1,0:T(1,128)S(1)}, u32[]{:S(2)}, u32[]{:S(2)}) %all-to-all-start) | async-done | bytes 544 | tf_op jit(solution)/shard_map/all_to_all | solution.py:59
  36.2 0.1 copy.31
  36.3 0.1 copy.32
  36.4 0.1 reshape.141
  36.6 2.1 gather_fusion
  38.7 5.7 %all-to-all-start.1 = ((bf16[64,2,128,64]{2,3,1,0:T(8,128)(2,1)}), bf16[64,2,128,64]{2,3,1,0:T(8,128)(2,1)}, u32[]{:S(2)}, u32[]{:S(2)}) async-start(bf16[64,2,128,64]{2,3,1,0:T(8,128)(2,1)} %bitcast.140), calls=%async_computation.1 | async-start | bytes 4194304 | tf_op jit(solution)/shard_map/all_to_all | solution.py:59
  44.4 0.8 constant_dynamic-slice_fusion
  45.3 0.1 reshape.135
  45.4 1.0 constant_dynamic-slice_fusion.1
  46.5 88.7 %all-to-all-done.1 = bf16[64,2,128,64]{2,3,1,0:T(8,128)(2,1)} async-done(((bf16[64,2,128,64]{2,3,1,0:T(8,128)(2,1)}), bf16[64,2,128,64]{2,3,1,0:T(8,128)(2,1)}, u32[]{:S(2)}, u32[]{:S(2)}) %all-to-all-start.1) | async-done | bytes 2097184 | tf_op jit(solution)/shard_map/all_to_all | solution.py:59
  135.2 2.4 gather_fusion.1
  137.6 1.5 convolution_bitcast_fusion
  139.1 2.0 fusion.11
  141.1 0.0 copy-start.1
  141.1 0.7 copy.73
  141.8 26.7 %shard_map.97 = bf16[8,64,1024]{2,1,0:T(8,128)(2,1)} custom-call(bf16[64,1024]{1,0:T(8,128)(2,1)} %bitcast.143), custom_call_target="tpu_custom_call" | custom-call | tf_op jit(solution)/shard_map/pallas_call | solution.py:42
  168.5 2.2 fusion.37
  170.8 1.7 fusion.32
  172.5 0.8 reshape.171
  173.3 7.1 %all-to-all-start.2 = ((f32[64,1,512]{2,1,0:T(1,128)}), f32[64,1,512]{2,1,0:T(1,128)S(1)}, u32[]{:S(2)}, u32[]{:S(2)}) async-start(f32[64,1,512]{2,1,0:T(1,128)} %reshape.171), calls=%async_computation.2 | async-start | bytes 262144 | tf_op jit(solution)/shard_map/all_to_all | solution.py:59
  180.4 0.8 fusion.22.x_ref
  181.2 17.9 %shard_map.98 = bf16[8,64,1024]{2,1,0:T(8,128)(2,1)} custom-call(bf16[64,1024]{1,0:T(8,128)(2,1)} %fusion.22.x_ref), custom_call_target="tpu_custom_call" | custom-call | tf_op jit(solution)/shard_map/pallas_call | solution.py:42
  199.1 1.6 fusion.14
  200.7 0.7 gather_fusion.2
  201.5 0.5 broadcast.126
  202.0 0.9 reduce
  203.0 0.1 reshape.172
  203.1 0.1 reduce_sum.32
  203.2 0.8 reshape.173
  204.0 14.7 %all-to-all-start.3 = ((f32[64,1,512]{2,1,0:T(1,128)}), f32[64,1,512]{2,1,0:T(1,128)S(1)}, u32[]{:S(2)}, u32[]{:S(2)}) async-start(f32[64,1,512]{2,1,0:T(1,128)} %reshape.173), calls=%async_computation.3 | async-start | bytes 262144 | tf_op jit(solution)/shard_map/all_to_all | solution.py:59
  218.8 0.7 convolution_convert_fusion.1
  219.5 1.0 convolution_convert_fusion
  220.5 2.7 copy.40
  223.1 10.9 %all-to-all-done.3 = f32[64,1,512]{2,1,0:T(1,128)S(1)} async-done(((f32[64,1,512]{2,1,0:T(1,128)}), f32[64,1,512]{2,1,0:T(1,128)S(1)}, u32[]{:S(2)}, u32[]{:S(2)}) %all-to-all-start.3) | async-done | bytes 131104 | tf_op jit(solution)/shard_map/all_to_all | solution.py:59
  234.1 6.6 %all-to-all-start.4 = ((bf16[64,128,128]{2,1,0:T(8,128)(2,1)}), bf16[64,128,128]{2,1,0:T(8,128)(2,1)}, u32[]{:S(2)}, u32[]{:S(2)}) async-start(bf16[64,128,128]{2,1,0:T(8,128)(2,1)} %copy.40), calls=%async_computation.4 | async-start | bytes 4194304 | tf_op jit(solution)/shard_map/all_to_all | solution.py:59
  240.7 1.0 reduce.1
  241.7 0.1 reshape.174
  241.8 0.8 copy.43
  242.6 93.2 %all-to-all-done.4 = bf16[64,128,128]{2,1,0:T(8,128)(2,1)} async-done(((bf16[64,128,128]{2,1,0:T(8,128)(2,1)}), bf16[64,128,128]{2,1,0:T(8,128)(2,1)}, u32[]{:S(2)}, u32[]{:S(2)}) %all-to-all-start.4) | async-done | bytes 2097184 | tf_op jit(solution)/shard_map/all_to_all | solution.py:59
  335.7 2.8 fusion.8
  338.5 0.7 copy.72
  (17 shorter events, 0.1 us)
Async XLA Ops:
  0.6 136.9 %copy-start = (bf16[64,128,128]{2,1,0:T(8,128)(2,1)S(1)}, bf16[64,128,128]{2,1,0:T(8,128)(2,1)}, u32[]{:S(2)}) copy-start(bf16[64,128,128]{2,1,0:T(8,128)(2,1)} %param.9) | copy-start | bytes 6291460
  3.7 32.5 %all-to-all-start = ((s32[64,1,2]{2,1,0:T(1,128)}), s32[64,1,2]{2,1,0:T(1,128)S(1)}, u32[]{:S(2)}, u32[]{:S(2)}) async-start(s32[64,1,2]{2,1,0:T(1,128)} %copy.30), calls=%async_computation | async-start | bytes 65536 | tf_op jit(solution)/shard_map/all_to_all | solution.py:59
  38.7 7.7 %copy-start.2 = (s32[64]{0:T(128)S(1)}, s32[64]{0:T(128)}, u32[]{:S(2)}) copy-start(s32[64]{0:T(128)} %param.10) | copy-start | bytes 772
  38.7 7.8 %copy-start.3 = (s32[64,1]{0,1:T(1,128)S(1)}, s32[64,1]{0,1:T(1,128)}, u32[]{:S(2)}) copy-start(s32[64,1]{0,1:T(1,128)} %param.11) | copy-start | bytes 772
  38.7 96.5 %all-to-all-start.1 = ((bf16[64,2,128,64]{2,3,1,0:T(8,128)(2,1)}), bf16[64,2,128,64]{2,3,1,0:T(8,128)(2,1)}, u32[]{:S(2)}, u32[]{:S(2)}) async-start(bf16[64,2,128,64]{2,3,1,0:T(8,128)(2,1)} %bitcast.140), calls=%async_computation.1 | async-start | bytes 4194304 | tf_op jit(solution)/shard_map/all_to_all | solution.py:59
  141.1 29.7 %copy-start.1 = (s32[1024]{0:T(1024)S(1)}, s32[1024]{0:T(1024)}, u32[]{:S(2)}) copy-start(s32[1024]{0:T(1024)} %param.13) | copy-start | bytes 12292
  173.3 28.2 %all-to-all-start.2 = ((f32[64,1,512]{2,1,0:T(1,128)}), f32[64,1,512]{2,1,0:T(1,128)S(1)}, u32[]{:S(2)}, u32[]{:S(2)}) async-start(f32[64,1,512]{2,1,0:T(1,128)} %reshape.171), calls=%async_computation.2 | async-start | bytes 262144 | tf_op jit(solution)/shard_map/all_to_all | solution.py:59
  204.0 30.1 %all-to-all-start.3 = ((f32[64,1,512]{2,1,0:T(1,128)}), f32[64,1,512]{2,1,0:T(1,128)S(1)}, u32[]{:S(2)}, u32[]{:S(2)}) async-start(f32[64,1,512]{2,1,0:T(1,128)} %reshape.173), calls=%async_computation.3 | async-start | bytes 262144 | tf_op jit(solution)/shard_map/all_to_all | solution.py:59
  234.1 101.6 %all-to-all-start.4 = ((bf16[64,128,128]{2,1,0:T(8,128)(2,1)}), bf16[64,128,128]{2,1,0:T(8,128)(2,1)}, u32[]{:S(2)}, u32[]{:S(2)}) async-start(bf16[64,128,128]{2,1,0:T(8,128)(2,1)} %copy.40), calls=%async_computation.4 | async-start | bytes 4194304 | tf_op jit(solution)/shard_map/all_to_all | solution.py:59

commit v12 on v11

--- a/solution.py
+++ b/solution.py
@@ -10,31 +10,56 @@
 MESH = pl.DeviceIdType.MESH
 
 
-def _cols_gather_kernel(x_ref, o_ref, send_sems, recv_sems):
+def _cols_gather_kernel(x_ref, o_ref, send_sems, recv_sems, pass_sems, take_sems):
     n = o_ref.shape[0]
+    chips = n // 2
     me = lax.axis_index("cols")
+    partner = me + 1 - 2 * lax.rem(me, 2)
     barrier = pltpu.get_barrier_semaphore()
-    for k in range(1, n):
+    for k in range(1, chips):
         pl.semaphore_signal(
-            barrier, 1, device_id={"cols": lax.rem(me + k, n)}, device_id_type=MESH
+            barrier, 1, device_id={"cols": lax.rem(me + 2 * k, n)}, device_id_type=MESH
         )
-    pl.semaphore_wait(barrier, n - 1)
-    copies = []
-    for k in range(1, n):
-        peer = lax.rem(me + k, n)
-        src = lax.rem(me + n - k, n)
+    pl.semaphore_signal(barrier, 1, device_id={"cols": partner}, device_id_type=MESH)
+    pl.semaphore_wait(barrier, chips)
+    far = []
+    for k in range(1, chips):
         out = pltpu.make_async_remote_copy(
             src_ref=x_ref, dst_ref=o_ref.at[me], send_sem=send_sems.at[k],
-            recv_sem=recv_sems.at[k], device_id={"cols": peer}, device_id_type=MESH)
+            recv_sem=recv_sems.at[k], device_id={"cols": lax.rem(me + 2 * k, n)},
+            device_id_type=MESH)
         out.start()
+        src = lax.rem(me + n - 2 * k, n)
         back = pltpu.make_async_remote_copy(
             src_ref=x_ref, dst_ref=o_ref.at[src], send_sem=send_sems.at[k],
             recv_sem=recv_sems.at[k], device_id={"cols": src}, device_id_type=MESH)
-        copies.append((out, back))
+        far.append((out, back))
+    near = [
+        pltpu.make_async_remote_copy(
+            src_ref=x_ref, dst_ref=o_ref.at[me], send_sem=pass_sems.at[0],
+            recv_sem=take_sems.at[0], device_id={"cols": partner}, device_id_type=MESH)
+    ]
+    near[0].start()
     o_ref[me] = x_ref[...]
-    for out, back in copies:
+    for k in range(1, chips):
+        out, back = far[k - 1]
+        back.wait_recv()
+        piece = lax.rem(me + n - 2 * k, n)
+        hop = pltpu.make_async_remote_copy(
+            src_ref=o_ref.at[piece], dst_ref=o_ref.at[piece], send_sem=pass_sems.at[k],
+            recv_sem=take_sems.at[k], device_id={"cols": partner}, device_id_type=MESH)
+        hop.start()
+        near.append(hop)
+    for k in range(chips):
+        piece = lax.rem(partner + n - 2 * k, n)
+        pltpu.make_async_remote_copy(
+            src_ref=o_ref.at[piece], dst_ref=o_ref.at[piece], send_sem=pass_sems.at[k],
+            recv_sem=take_sems.at[k], device_id={"cols": partner}, device_id_type=MESH
+        ).wait_recv()
+    for out, back in far:
         out.wait_send()
-        back.wait_recv()
+    for hop in near:
+        hop.wait_send()
 
 
 def cols_gather(x, collective_id):
@@ -44,7 +69,7 @@
         out_shape=jax.ShapeDtypeStruct((n,) + x.shape, x.dtype),
         in_specs=[pl.BlockSpec(memory_space=pltpu.VMEM)],
         out_specs=pl.BlockSpec(memory_space=pltpu.VMEM),
-        scratch_shapes=[pltpu.SemaphoreType.DMA((n,)), pltpu.SemaphoreType.DMA((n,))],
+        scratch_shapes=[pltpu.SemaphoreType.DMA((n,))] * 4,
         compiler_params=pltpu.CompilerParams(collective_id=collective_id, has_side_effects=True),
     )(x)
 

time: 342 us -> 334 us (0.977); the launches traced: 339 us -> 328 us
  Pallas kernels: 44.6 us -> 36.3 us
  waiting for transfers between devices: 205 us -> 201 us
    pallas_call x2, Pallas kernels: 44.6 us -> 36.3 us  [cols_gather(): pl.pallas_call(_cols_gather_kernel, out_shape=jax.ShapeDtypeStruct((n,) +...]
    all_to_all x5, waiting for transfers between devices: 205 us -> 201 us  [rows_exchange(): return lax.all_to_all(x, 'rows', split_axis=0, concat_axis=0, tiled=True)]
  transfers between devices with their start and end apart: 5 -> 5, of which waited for: 4 -> 4; matrix products, arithmetic and copies ran while one was open for 4% -> 4% of each run, Pallas kernels for 5% -> 4%
where the time goes in v12:
time: 334 us; the launch traced here: 328 us
  waiting for transfers between devices  201 us (60%)
  starting transfers between devices  54.2 us (16%)
  Pallas kernels  36.3 us (11%)
  local copies, waits for them, and re-layouts  16.5 us (5%)
  matrix products  13.5 us (4%)
  other arithmetic  5.19 us (2%)
    all_to_all x5, waiting for transfers between devices, rows_exchange(): return lax.all_to_all(x, 'rows', split_axis=0, concat_axis=0, tiled=True)  201 us
    all_to_all x5, starting transfers between devices, rows_exchange(): return lax.all_to_all(x, 'rows', split_axis=0, concat_axis=0, tiled=True)  54.2 us
    pallas_call x2, Pallas kernels, cols_gather(): pl.pallas_call(_cols_gather_kernel, out_shape=jax.ShapeDtypeStruct((n,) +...  36.3 us
  transfers between devices with their start and end apart: 5, of which 4 were waited for; matrix products, arithmetic and copies ran while one was open for 4% of the time, Pallas kernels for 4%

profile of v12, /device:TPU:1, one launch (start us, length us, event | category | flops | bytes accessed | tf_op | source)
XLA Modules:
  0.0 327.5 jit_solution(18396149452478615063)
XLA Ops:
  0.6 0.0 copy-start
  0.6 0.9 convert_reduce_fusion
  1.6 0.7 iota_compare_fusion.1
  2.2 0.8 fusion.39
  3.0 0.7 copy.30
  3.7 19.3 %all-to-all-start = ((s32[64,1,2]{2,1,0:T(1,128)}), s32[64,1,2]{2,1,0:T(1,128)S(1)}, u32[]{:S(2)}, u32[]{:S(2)}) async-start(s32[64,1,2]{2,1,0:T(1,128)} %copy.30), calls=%async_computation | async-start | bytes 65536 | tf_op jit(solution)/shard_map/all_to_all | solution.py:84
  23.0 0.9 copy_bitcast_fusion.2
  23.9 12.3 %all-to-all-done = s32[64,1,2]{2,1,0:T(1,128)S(1)} async-done(((s32[64,1,2]{2,1,0:T(1,128)}), s32[64,1,2]{2,1,0:T(1,128)S(1)}, u32[]{:S(2)}, u32[]{:S(2)}) %all-to-all-start) | async-done | bytes 544 | tf_op jit(solution)/shard_map/all_to_all | solution.py:84
  36.2 0.1 copy.31
  36.3 0.1 copy.32
  36.4 0.1 reshape.141
  36.6 2.1 gather_fusion
  38.7 5.7 %all-to-all-start.1 = ((bf16[64,2,128,64]{2,3,1,0:T(8,128)(2,1)}), bf16[64,2,128,64]{2,3,1,0:T(8,128)(2,1)}, u32[]{:S(2)}, u32[]{:S(2)}) async-start(bf16[64,2,128,64]{2,3,1,0:T(8,128)(2,1)} %bitcast.140), calls=%async_computation.1 | async-start | bytes 4194304 | tf_op jit(solution)/shard_map/all_to_all | solution.py:84
  44.4 0.8 constant_dynamic-slice_fusion
  45.3 0.1 reshape.135
  45.4 1.0 constant_dynamic-slice_fusion.1
  46.5 88.7 %all-to-all-done.1 = bf16[64,2,128,64]{2,3,1,0:T(8,128)(2,1)} async-done(((bf16[64,2,128,64]{2,3,1,0:T(8,128)(2,1)}), bf16[64,2,128,64]{2,3,1,0:T(8,128)(2,1)}, u32[]{:S(2)}, u32[]{:S(2)}) %all-to-all-start.1) | async-done | bytes 2097184 | tf_op jit(solution)/shard_map/all_to_all | solution.py:84
  135.2 2.4 gather_fusion.1
  137.6 1.5 convolution_bitcast_fusion
  139.1 2.0 fusion.11
  141.1 0.0 copy-start.1
  141.1 0.7 copy.73
  141.8 22.1 %shard_map.97 = bf16[8,64,1024]{2,1,0:T(8,128)(2,1)} custom-call(bf16[64,1024]{1,0:T(8,128)(2,1)} %bitcast.143), custom_call_target="tpu_custom_call" | custom-call | tf_op jit(solution)/shard_map/pallas_call | solution.py:67
  163.9 2.2 fusion.37
  166.2 1.7 fusion.32
  167.9 0.8 reshape.171
  168.7 7.2 %all-to-all-start.2 = ((f32[64,1,512]{2,1,0:T(1,128)}), f32[64,1,512]{2,1,0:T(1,128)S(1)}, u32[]{:S(2)}, u32[]{:S(2)}) async-start(f32[64,1,512]{2,1,0:T(1,128)} %reshape.171), calls=%async_computation.2 | async-start | bytes 262144 | tf_op jit(solution)/shard_map/all_to_all | solution.py:84
  176.0 0.8 fusion.22.x_ref
  176.8 14.1 %shard_map.98 = bf16[8,64,1024]{2,1,0:T(8,128)(2,1)} custom-call(bf16[64,1024]{1,0:T(8,128)(2,1)} %fusion.22.x_ref), custom_call_target="tpu_custom_call" | custom-call | tf_op jit(solution)/shard_map/pallas_call | solution.py:67
  190.9 1.6 fusion.14
  192.5 0.7 gather_fusion.2
  193.3 0.5 broadcast.126
  193.8 0.9 reduce
  194.8 0.1 reshape.172
  194.9 0.1 reduce_sum.32
  195.0 0.8 reshape.173
  195.8 14.7 %all-to-all-start.3 = ((f32[64,1,512]{2,1,0:T(1,128)}), f32[64,1,512]{2,1,0:T(1,128)S(1)}, u32[]{:S(2)}, u32[]{:S(2)}) async-start(f32[64,1,512]{2,1,0:T(1,128)} %reshape.173), calls=%async_computation.3 | async-start | bytes 262144 | tf_op jit(solution)/shard_map/all_to_all | solution.py:84
  210.5 0.7 convolution_convert_fusion.1
  211.2 1.0 convolution_convert_fusion
  212.2 2.7 copy.40
  214.9 10.3 %all-to-all-done.3 = f32[64,1,512]{2,1,0:T(1,128)S(1)} async-done(((f32[64,1,512]{2,1,0:T(1,128)}), f32[64,1,512]{2,1,0:T(1,128)S(1)}, u32[]{:S(2)}, u32[]{:S(2)}) %all-to-all-start.3) | async-done | bytes 131104 | tf_op jit(solution)/shard_map/all_to_all | solution.py:84
  225.2 7.3 %all-to-all-start.4 = ((bf16[64,128,128]{2,1,0:T(8,128)(2,1)}), bf16[64,128,128]{2,1,0:T(8,128)(2,1)}, u32[]{:S(2)}, u32[]{:S(2)}) async-start(bf16[64,128,128]{2,1,0:T(8,128)(2,1)} %copy.40), calls=%async_computation.4 | async-start | bytes 4194304 | tf_op jit(solution)/shard_map/all_to_all | solution.py:84
  232.5 1.0 reduce.1
  233.4 0.1 reshape.174
  233.6 0.8 copy.43
  234.3 89.7 %all-to-all-done.4 = bf16[64,128,128]{2,1,0:T(8,128)(2,1)} async-done(((bf16[64,128,128]{2,1,0:T(8,128)(2,1)}), bf16[64,128,128]{2,1,0:T(8,128)(2,1)}, u32[]{:S(2)}, u32[]{:S(2)}) %all-to-all-start.4) | async-done | bytes 2097184 | tf_op jit(solution)/shard_map/all_to_all | solution.py:84
  324.1 2.8 fusion.8
  326.9 0.7 copy.72
  (17 shorter events, 0.1 us)
Async XLA Ops:
  0.6 136.9 %copy-start = (bf16[64,128,128]{2,1,0:T(8,128)(2,1)S(1)}, bf16[64,128,128]{2,1,0:T(8,128)(2,1)}, u32[]{:S(2)}) copy-start(bf16[64,128,128]{2,1,0:T(8,128)(2,1)} %param.9) | copy-start | bytes 6291460
  3.7 32.5 %all-to-all-start = ((s32[64,1,2]{2,1,0:T(1,128)}), s32[64,1,2]{2,1,0:T(1,128)S(1)}, u32[]{:S(2)}, u32[]{:S(2)}) async-start(s32[64,1,2]{2,1,0:T(1,128)} %copy.30), calls=%async_computation | async-start | bytes 65536 | tf_op jit(solution)/shard_map/all_to_all | solution.py:84
  38.7 7.7 %copy-start.2 = (s32[64]{0:T(128)S(1)}, s32[64]{0:T(128)}, u32[]{:S(2)}) copy-start(s32[64]{0:T(128)} %param.10) | copy-start | bytes 772
  38.7 7.8 %copy-start.3 = (s32[64,1]{0,1:T(1,128)S(1)}, s32[64,1]{0,1:T(1,128)}, u32[]{:S(2)}) copy-start(s32[64,1]{0,1:T(1,128)} %param.11) | copy-start | bytes 772
  38.7 96.5 %all-to-all-start.1 = ((bf16[64,2,128,64]{2,3,1,0:T(8,128)(2,1)}), bf16[64,2,128,64]{2,3,1,0:T(8,128)(2,1)}, u32[]{:S(2)}, u32[]{:S(2)}) async-start(bf16[64,2,128,64]{2,3,1,0:T(8,128)(2,1)} %bitcast.140), calls=%async_computation.1 | async-start | bytes 4194304 | tf_op jit(solution)/shard_map/all_to_all | solution.py:84
  141.1 25.1 %copy-start.1 = (s32[1024]{0:T(1024)S(1)}, s32[1024]{0:T(1024)}, u32[]{:S(2)}) copy-start(s32[1024]{0:T(1024)} %param.13) | copy-start | bytes 12292
  168.7 24.5 %all-to-all-start.2 = ((f32[64,1,512]{2,1,0:T(1,128)}), f32[64,1,512]{2,1,0:T(1,128)S(1)}, u32[]{:S(2)}, u32[]{:S(2)}) async-start(f32[64,1,512]{2,1,0:T(1,128)} %reshape.171), calls=%async_computation.2 | async-start | bytes 262144 | tf_op jit(solution)/shard_map/all_to_all | solution.py:84
  195.8 29.4 %all-to-all-start.3 = ((f32[64,1,512]{2,1,0:T(1,128)}), f32[64,1,512]{2,1,0:T(1,128)S(1)}, u32[]{:S(2)}, u32[]{:S(2)}) async-start(f32[64,1,512]{2,1,0:T(1,128)} %reshape.173), calls=%async_computation.3 | async-start | bytes 262144 | tf_op jit(solution)/shard_map/all_to_all | solution.py:84
  225.2 98.9 %all-to-all-start.4 = ((bf16[64,128,128]{2,1,0:T(8,128)(2,1)}), bf16[64,128,128]{2,1,0:T(8,128)(2,1)}, u32[]{:S(2)}, u32[]{:S(2)}) async-start(bf16[64,128,128]{2,1,0:T(8,128)(2,1)} %copy.40), calls=%async_computation.4 | async-start | bytes 4194304 | tf_op jit(solution)/shard_map/all_to_all | solution.py:84

commit v13 on v12

--- a/solution.py
+++ b/solution.py
@@ -127,11 +127,6 @@
     ).reshape(col_devices * col_width, col_width)
     pieces = weight_terms.reshape(row_devices, -1, col_width)
     reduced = jnp.sum(rows_exchange(pieces), axis=0)
-    spread = jnp.broadcast_to(reduced[None], (row_devices,) + reduced.shape)
-    node_total = local_rows * row_devices
-    weight_grad = rows_exchange(spread).reshape(col_devices * col_width, col_width) / math.sqrt(
-        node_total
-    )
     agg_grad = jnp.einsum(
         "jcn,kjc->nk",
         grad_all,
@@ -149,6 +144,12 @@
     received = rows_exchange(
         send_terms.reshape(row_devices, capacity * col_width, block_size)
     ).reshape(row_devices, capacity, col_width, block_size)
+    reduced, received = lax.optimization_barrier((reduced, received))
+    spread = jnp.broadcast_to(reduced[None], (row_devices,) + reduced.shape)
+    node_total = local_rows * row_devices
+    weight_grad = rows_exchange(spread).reshape(col_devices * col_width, col_width) / math.sqrt(
+        node_total
+    )
     placing = (wanted[:, :, None] == local_ids[None, None, :]).astype(jnp.bfloat16)
     feature_grad = jnp.einsum(
         "scb,scfi->bif", placing, received, preferred_element_type=jnp.float32

time: 334 us -> 337 us (level); the launches traced: 328 us -> 335 us
  starting transfers between devices: 54.2 us -> 60.8 us
    all_to_all x5, starting transfers between devices: 54.2 us -> 60.8 us  [rows_exchange(): return lax.all_to_all(x, 'rows', split_axis=0, concat_axis=0, tiled=True)]
where the time goes in v13:
time: 337 us; the launch traced here: 335 us
  waiting for transfers between devices  202 us (60%)
  starting transfers between devices  60.8 us (18%)
  Pallas kernels  36.3 us (11%)
  local copies, waits for them, and re-layouts  16.5 us (5%)
  matrix products  13.5 us (4%)
  other arithmetic  5.11 us (2%)
    all_to_all x5, waiting for transfers between devices, rows_exchange(): return lax.all_to_all(x, 'rows', split_axis=0, concat_axis=0, tiled=True)  202 us
    all_to_all x5, starting transfers between devices, rows_exchange(): return lax.all_to_all(x, 'rows', split_axis=0, concat_axis=0, tiled=True)  60.8 us
    pallas_call x2, Pallas kernels, cols_gather(): pl.pallas_call(_cols_gather_kernel, out_shape=jax.ShapeDtypeStruct((n,) +...  36.3 us
  transfers between devices with their start and end apart: 5, of which 4 were waited for; matrix products, arithmetic and copies ran while one was open for 4% of the time, Pallas kernels for 4%

profile of v13, /device:TPU:1, one launch (start us, length us, event | category | flops | bytes accessed | tf_op | source)
XLA Modules:
  0.0 335.0 jit_solution(10748000168708494485)
XLA Ops:
  0.6 0.0 copy-start
  0.6 0.9 convert_reduce_fusion
  1.6 0.7 iota_compare_fusion.1
  2.2 0.8 fusion.39
  3.0 0.7 copy.30
  3.7 19.3 %all-to-all-start = ((s32[64,1,2]{2,1,0:T(1,128)}), s32[64,1,2]{2,1,0:T(1,128)S(1)}, u32[]{:S(2)}, u32[]{:S(2)}) async-start(s32[64,1,2]{2,1,0:T(1,128)} %copy.30), calls=%async_computation | async-start | bytes 65536 | tf_op jit(solution)/shard_map/all_to_all | solution.py:84
  23.0 0.9 copy_bitcast_fusion.2
  23.9 12.3 %all-to-all-done = s32[64,1,2]{2,1,0:T(1,128)S(1)} async-done(((s32[64,1,2]{2,1,0:T(1,128)}), s32[64,1,2]{2,1,0:T(1,128)S(1)}, u32[]{:S(2)}, u32[]{:S(2)}) %all-to-all-start) | async-done | bytes 544 | tf_op jit(solution)/shard_map/all_to_all | solution.py:84
  36.2 0.1 copy.31
  36.3 0.1 copy.32
  36.4 0.1 reshape.141
  36.6 2.1 gather_fusion
  38.7 5.7 %all-to-all-start.1 = ((bf16[64,2,128,64]{2,3,1,0:T(8,128)(2,1)}), bf16[64,2,128,64]{2,3,1,0:T(8,128)(2,1)}, u32[]{:S(2)}, u32[]{:S(2)}) async-start(bf16[64,2,128,64]{2,3,1,0:T(8,128)(2,1)} %bitcast.140), calls=%async_computation.1 | async-start | bytes 4194304 | tf_op jit(solution)/shard_map/all_to_all | solution.py:84
  44.4 0.8 constant_dynamic-slice_fusion
  45.3 0.1 reshape.135
  45.4 1.0 constant_dynamic-slice_fusion.1
  46.5 88.7 %all-to-all-done.1 = bf16[64,2,128,64]{2,3,1,0:T(8,128)(2,1)} async-done(((bf16[64,2,128,64]{2,3,1,0:T(8,128)(2,1)}), bf16[64,2,128,64]{2,3,1,0:T(8,128)(2,1)}, u32[]{:S(2)}, u32[]{:S(2)}) %all-to-all-start.1) | async-done | bytes 2097184 | tf_op jit(solution)/shard_map/all_to_all | solution.py:84
  135.2 2.4 gather_fusion.1
  137.6 1.5 convolution_bitcast_fusion
  139.1 2.0 fusion.11
  141.1 0.0 copy-start.1
  141.1 0.7 copy.73
  141.8 22.1 %shard_map.97 = bf16[8,64,1024]{2,1,0:T(8,128)(2,1)} custom-call(bf16[64,1024]{1,0:T(8,128)(2,1)} %bitcast.143), custom_call_target="tpu_custom_call" | custom-call | tf_op jit(solution)/shard_map/pallas_call | solution.py:67
  163.9 2.2 fusion.37
  166.2 1.8 fusion.32
  167.9 0.8 fusion.22.x_ref
  168.7 0.8 reshape.171
  169.6 7.2 %all-to-all-start.2 = ((f32[64,1,512]{2,1,0:T(1,128)}), f32[64,1,512]{2,1,0:T(1,128)S(1)}, u32[]{:S(2)}, u32[]{:S(2)}) async-start(f32[64,1,512]{2,1,0:T(1,128)} %reshape.171), calls=%async_computation.2 | async-start | bytes 262144 | tf_op jit(solution)/shard_map/all_to_all | solution.py:84
  176.8 14.1 %shard_map.98 = bf16[8,64,1024]{2,1,0:T(8,128)(2,1)} custom-call(bf16[64,1024]{1,0:T(8,128)(2,1)} %fusion.22.x_ref), custom_call_target="tpu_custom_call" | custom-call | tf_op jit(solution)/shard_map/pallas_call | solution.py:67
  190.9 1.6 fusion.14
  192.5 0.7 gather_fusion.2
  193.3 0.7 convolution_convert_fusion.1
  193.9 1.0 convolution_convert_fusion
  195.0 2.7 copy.40
  197.6 15.0 %all-to-all-start.3 = ((bf16[64,128,128]{2,1,0:T(8,128)(2,1)}), bf16[64,128,128]{2,1,0:T(8,128)(2,1)}, u32[]{:S(2)}, u32[]{:S(2)}) async-start(bf16[64,128,128]{2,1,0:T(8,128)(2,1)} %copy.40), calls=%async_computation.3 | async-start | bytes 4194304 | tf_op jit(solution)/shard_map/all_to_all | solution.py:84
  212.6 0.5 broadcast.126
  213.2 0.9 reduce
  214.1 0.1 reshape.172
  214.2 0.1 reduce_sum.32
  214.3 90.3 %all-to-all-done.3 = bf16[64,128,128]{2,1,0:T(8,128)(2,1)} async-done(((bf16[64,128,128]{2,1,0:T(8,128)(2,1)}), bf16[64,128,128]{2,1,0:T(8,128)(2,1)}, u32[]{:S(2)}, u32[]{:S(2)}) %all-to-all-start.3) | async-done | bytes 2097184 | tf_op jit(solution)/shard_map/all_to_all | solution.py:84
  304.6 0.8 reshape.173
  305.4 13.6 %all-to-all-start.4 = ((f32[64,1,512]{2,1,0:T(1,128)}), f32[64,1,512]{2,1,0:T(1,128)S(1)}, u32[]{:S(2)}, u32[]{:S(2)}) async-start(f32[64,1,512]{2,1,0:T(1,128)} %reshape.173), calls=%async_computation.4 | async-start | bytes 262144 | tf_op jit(solution)/shard_map/all_to_all | solution.py:84
  319.0 2.8 fusion.8
  321.8 0.7 copy.72
  322.5 10.7 %all-to-all-done.4 = f32[64,1,512]{2,1,0:T(1,128)S(1)} async-done(((f32[64,1,512]{2,1,0:T(1,128)}), f32[64,1,512]{2,1,0:T(1,128)S(1)}, u32[]{:S(2)}, u32[]{:S(2)}) %all-to-all-start.4) | async-done | bytes 131104 | tf_op jit(solution)/shard_map/all_to_all | solution.py:84
  333.2 0.9 reduce.1
  334.1 0.1 reshape.174
  334.3 0.8 copy.43
  (17 shorter events, 0.1 us)
Async XLA Ops:
  0.6 136.9 %copy-start = (bf16[64,128,128]{2,1,0:T(8,128)(2,1)S(1)}, bf16[64,128,128]{2,1,0:T(8,128)(2,1)}, u32[]{:S(2)}) copy-start(bf16[64,128,128]{2,1,0:T(8,128)(2,1)} %param.9) | copy-start | bytes 6291460
  3.7 32.5 %all-to-all-start = ((s32[64,1,2]{2,1,0:T(1,128)}), s32[64,1,2]{2,1,0:T(1,128)S(1)}, u32[]{:S(2)}, u32[]{:S(2)}) async-start(s32[64,1,2]{2,1,0:T(1,128)} %copy.30), calls=%async_computation | async-start | bytes 65536 | tf_op jit(solution)/shard_map/all_to_all | solution.py:84
  38.7 6.7 %copy-start.2 = (s32[64]{0:T(128)S(1)}, s32[64]{0:T(128)}, u32[]{:S(2)}) copy-start(s32[64]{0:T(128)} %param.10) | copy-start | bytes 772
  38.7 7.8 %copy-start.3 = (s32[64,1]{0,1:T(1,128)S(1)}, s32[64,1]{0,1:T(1,128)}, u32[]{:S(2)}) copy-start(s32[64,1]{0,1:T(1,128)} %param.11) | copy-start | bytes 772
  38.7 96.5 %all-to-all-start.1 = ((bf16[64,2,128,64]{2,3,1,0:T(8,128)(2,1)}), bf16[64,2,128,64]{2,3,1,0:T(8,128)(2,1)}, u32[]{:S(2)}, u32[]{:S(2)}) async-start(bf16[64,2,128,64]{2,3,1,0:T(8,128)(2,1)} %bitcast.140), calls=%async_computation.1 | async-start | bytes 4194304 | tf_op jit(solution)/shard_map/all_to_all | solution.py:84
  141.1 25.1 %copy-start.1 = (s32[1024]{0:T(1024)S(1)}, s32[1024]{0:T(1024)}, u32[]{:S(2)}) copy-start(s32[1024]{0:T(1024)} %param.13) | copy-start | bytes 12292
  169.6 28.1 %all-to-all-start.2 = ((f32[64,1,512]{2,1,0:T(1,128)}), f32[64,1,512]{2,1,0:T(1,128)S(1)}, u32[]{:S(2)}, u32[]{:S(2)}) async-start(f32[64,1,512]{2,1,0:T(1,128)} %reshape.171), calls=%async_computation.2 | async-start | bytes 262144 | tf_op jit(solution)/shard_map/all_to_all | solution.py:84
  197.6 106.9 %all-to-all-start.3 = ((bf16[64,128,128]{2,1,0:T(8,128)(2,1)}), bf16[64,128,128]{2,1,0:T(8,128)(2,1)}, u32[]{:S(2)}, u32[]{:S(2)}) async-start(bf16[64,128,128]{2,1,0:T(8,128)(2,1)} %copy.40), calls=%async_computation.3 | async-start | bytes 4194304 | tf_op jit(solution)/shard_map/all_to_all | solution.py:84
  305.4 27.8 %all-to-all-start.4 = ((f32[64,1,512]{2,1,0:T(1,128)}), f32[64,1,512]{2,1,0:T(1,128)S(1)}, u32[]{:S(2)}, u32[]{:S(2)}) async-start(f32[64,1,512]{2,1,0:T(1,128)} %reshape.173), calls=%async_computation.4 | async-start | bytes 262144 | tf_op jit(solution)/shard_map/all_to_all | solution.py:84

commit v14 on v12

--- a/solution.py
+++ b/solution.py
@@ -102,8 +102,14 @@
     request = jnp.sum(jnp.where(in_slot, source_block[:, None, None], 0), axis=0)
     wanted = rows_exchange(request)
     own_blocks = node_features.reshape(local_blocks, block_size, col_width)
-    incoming = rows_exchange(own_blocks[wanted])
-    source_rows = incoming[owners, slot_rank]
+    wanted_pick = (wanted[:, :, None] == local_ids[None, None, :]).astype(jnp.bfloat16)
+    outgoing = jnp.einsum(
+        "osb,bif->osif", wanted_pick, own_blocks, preferred_element_type=jnp.float32
+    ).astype(jnp.bfloat16)
+    incoming = rows_exchange(outgoing)
+    source_rows = jnp.einsum(
+        "tos,osif->tif", in_slot.astype(jnp.bfloat16), incoming, preferred_element_type=jnp.float32
+    ).astype(jnp.bfloat16)
     products = jnp.einsum(
         "tij,tjf->tif", tile_values, source_rows, preferred_element_type=jnp.float32
     )

time: 334 us -> 336 us (level)
  matrix products: 13.5 us -> 17.4 us
    gather x2 -> x0, local copies, waits for them, and re-layouts: 4.51 us -> none  [the longest x1 2.38 us: per_device(): source_rows = incoming[owners, slot_rank]]
    dot_general x0 -> x2, matrix products: none -> 3.85 us  [the longest x1 3.09 us: per_device(): jnp.einsum('tos,osif->tif', in_slot.astype(jnp.bfloat16), incoming, prefe...]
where the time goes in v14:
time: 336 us; the launch traced here: 329 us
  waiting for transfers between devices  201 us (60%)
  starting transfers between devices  54.1 us (16%)
  Pallas kernels  36.3 us (11%)
  matrix products  17.4 us (5%)
  local copies, waits for them, and re-layouts  14.3 us (4%)
  other arithmetic  5.16 us (2%)
    all_to_all x5, waiting for transfers between devices, rows_exchange(): return lax.all_to_all(x, 'rows', split_axis=0, concat_axis=0, tiled=True)  201 us
    all_to_all x5, starting transfers between devices, rows_exchange(): return lax.all_to_all(x, 'rows', split_axis=0, concat_axis=0, tiled=True)  54.1 us
    pallas_call x2, Pallas kernels, cols_gather(): pl.pallas_call(_cols_gather_kernel, out_shape=jax.ShapeDtypeStruct((n,) +...  36.3 us
  transfers between devices with their start and end apart: 5, of which 4 were waited for; matrix products, arithmetic and copies ran while one was open for 4% of the time, Pallas kernels for 4%

profile of v14, /device:TPU:1, one launch (start us, length us, event | category | flops | bytes accessed | tf_op | source)
XLA Modules:
  0.0 329.3 jit_solution(12755104644541843338)
XLA Ops:
  0.6 0.0 copy-start
  0.6 0.9 convert_reduce_fusion
  1.6 0.7 iota_compare_fusion.1
  2.2 0.8 fusion.44
  3.0 0.7 copy.17
  3.7 19.3 %all-to-all-start = ((s32[64,1,2]{2,1,0:T(1,128)}), s32[64,1,2]{2,1,0:T(1,128)S(1)}, u32[]{:S(2)}, u32[]{:S(2)}) async-start(s32[64,1,2]{2,1,0:T(1,128)} %copy.17), calls=%async_computation | async-start | bytes 65536 | tf_op jit(solution)/shard_map/all_to_all | solution.py:84
  23.0 0.9 copy.41
  23.9 12.3 %all-to-all-done = s32[64,1,2]{2,1,0:T(1,128)S(1)} async-done(((s32[64,1,2]{2,1,0:T(1,128)}), s32[64,1,2]{2,1,0:T(1,128)S(1)}, u32[]{:S(2)}, u32[]{:S(2)}) %all-to-all-start) | async-done | bytes 544 | tf_op jit(solution)/shard_map/all_to_all | solution.py:84
  36.2 0.1 copy.18
  36.3 0.8 convolution_convert_fusion.1
  37.1 2.6 copy.19
  39.7 5.7 %all-to-all-start.1 = ((bf16[64,2,128,64]{2,3,1,0:T(8,128)(2,1)}), bf16[64,2,128,64]{2,3,1,0:T(8,128)(2,1)}, u32[]{:S(2)}, u32[]{:S(2)}) async-start(bf16[64,2,128,64]{2,3,1,0:T(8,128)(2,1)} %copy.19), calls=%async_computation.1 | async-start | bytes 4194304 | tf_op jit(solution)/shard_map/all_to_all | solution.py:84
  45.4 0.8 constant_dynamic-slice_fusion
  46.3 0.1 reshape.94
  46.4 1.0 constant_dynamic-slice_fusion.1
  47.4 88.7 %all-to-all-done.1 = bf16[64,2,128,64]{2,3,1,0:T(8,128)(2,1)} async-done(((bf16[64,2,128,64]{2,3,1,0:T(8,128)(2,1)}), bf16[64,2,128,64]{2,3,1,0:T(8,128)(2,1)}, u32[]{:S(2)}, u32[]{:S(2)}) %all-to-all-start.1) | async-done | bytes 2097184 | tf_op jit(solution)/shard_map/all_to_all | solution.py:84
  136.2 3.1 bitcast_convert_fusion
  139.3 1.6 convolution_bitcast_fusion
  140.9 2.0 fusion.15
  142.8 0.0 copy-start.1
  142.9 0.7 copy.70
  143.5 22.1 %shard_map.97 = bf16[8,64,1024]{2,1,0:T(8,128)(2,1)} custom-call(bf16[64,1024]{1,0:T(8,128)(2,1)} %bitcast.142), custom_call_target="tpu_custom_call" | custom-call | tf_op jit(solution)/shard_map/pallas_call | solution.py:67
  165.7 2.2 fusion.42
  167.9 1.7 fusion.37
  169.7 0.8 reshape.119
  170.5 7.4 %all-to-all-start.2 = ((f32[64,1,512]{2,1,0:T(1,128)}), f32[64,1,512]{2,1,0:T(1,128)S(1)}, u32[]{:S(2)}, u32[]{:S(2)}) async-start(f32[64,1,512]{2,1,0:T(1,128)} %reshape.119), calls=%async_computation.2 | async-start | bytes 262144 | tf_op jit(solution)/shard_map/all_to_all | solution.py:84
  177.9 0.8 fusion.27.x_ref
  178.7 14.1 %shard_map.98 = bf16[8,64,1024]{2,1,0:T(8,128)(2,1)} custom-call(bf16[64,1024]{1,0:T(8,128)(2,1)} %fusion.27.x_ref), custom_call_target="tpu_custom_call" | custom-call | tf_op jit(solution)/shard_map/pallas_call | solution.py:67
  192.8 1.6 fusion.18
  194.4 0.7 gather_fusion
  195.2 0.0 all-to-all-done.2
  195.2 0.5 broadcast.67
  195.7 0.9 reduce
  196.7 0.1 reshape.120
  196.8 0.1 reduce_sum.29
  196.9 0.8 reshape.121
  197.7 14.4 %all-to-all-start.3 = ((f32[64,1,512]{2,1,0:T(1,128)}), f32[64,1,512]{2,1,0:T(1,128)S(1)}, u32[]{:S(2)}, u32[]{:S(2)}) async-start(f32[64,1,512]{2,1,0:T(1,128)} %reshape.121), calls=%async_computation.3 | async-start | bytes 262144 | tf_op jit(solution)/shard_map/all_to_all | solution.py:84
  212.1 0.7 convolution_convert_fusion.2
  212.8 1.0 convolution_convert_fusion
  213.8 2.6 copy.29
  216.5 10.3 %all-to-all-done.3 = f32[64,1,512]{2,1,0:T(1,128)S(1)} async-done(((f32[64,1,512]{2,1,0:T(1,128)}), f32[64,1,512]{2,1,0:T(1,128)S(1)}, u32[]{:S(2)}, u32[]{:S(2)}) %all-to-all-start.3) | async-done | bytes 131104 | tf_op jit(solution)/shard_map/all_to_all | solution.py:84
  226.8 7.4 %all-to-all-start.4 = ((bf16[64,128,128]{2,1,0:T(8,128)(2,1)}), bf16[64,128,128]{2,1,0:T(8,128)(2,1)}, u32[]{:S(2)}, u32[]{:S(2)}) async-start(bf16[64,128,128]{2,1,0:T(8,128)(2,1)} %copy.29), calls=%async_computation.4 | async-start | bytes 4194304 | tf_op jit(solution)/shard_map/all_to_all | solution.py:84
  234.2 1.0 reduce.1
  235.2 0.1 reshape.122
  235.3 0.8 copy.31
  236.1 89.7 %all-to-all-done.4 = bf16[64,128,128]{2,1,0:T(8,128)(2,1)} async-done(((bf16[64,128,128]{2,1,0:T(8,128)(2,1)}), bf16[64,128,128]{2,1,0:T(8,128)(2,1)}, u32[]{:S(2)}, u32[]{:S(2)}) %all-to-all-start.4) | async-done | bytes 2097184 | tf_op jit(solution)/shard_map/all_to_all | solution.py:84
  325.8 2.8 fusion.12
  328.6 0.7 copy.69
  (11 shorter events, 0.1 us)
Async XLA Ops:
  0.6 138.7 %copy-start = (bf16[64,128,128]{2,1,0:T(8,128)(2,1)S(1)}, bf16[64,128,128]{2,1,0:T(8,128)(2,1)}, u32[]{:S(2)}) copy-start(bf16[64,128,128]{2,1,0:T(8,128)(2,1)} %param.9) | copy-start | bytes 6291460
  3.7 32.5 %all-to-all-start = ((s32[64,1,2]{2,1,0:T(1,128)}), s32[64,1,2]{2,1,0:T(1,128)S(1)}, u32[]{:S(2)}, u32[]{:S(2)}) async-start(s32[64,1,2]{2,1,0:T(1,128)} %copy.17), calls=%async_computation | async-start | bytes 65536 | tf_op jit(solution)/shard_map/all_to_all | solution.py:84
  39.7 7.7 %copy-start.2 = (s32[64]{0:T(128)S(1)}, s32[64]{0:T(128)}, u32[]{:S(2)}) copy-start(s32[64]{0:T(128)} %param.10) | copy-start | bytes 772
  39.7 96.5 %all-to-all-start.1 = ((bf16[64,2,128,64]{2,3,1,0:T(8,128)(2,1)}), bf16[64,2,128,64]{2,3,1,0:T(8,128)(2,1)}, u32[]{:S(2)}, u32[]{:S(2)}) async-start(bf16[64,2,128,64]{2,3,1,0:T(8,128)(2,1)} %copy.19), calls=%async_computation.1 | async-start | bytes 4194304 | tf_op jit(solution)/shard_map/all_to_all | solution.py:84
  142.8 25.1 %copy-start.1 = (s32[1024]{0:T(1024)S(1)}, s32[1024]{0:T(1024)}, u32[]{:S(2)}) copy-start(s32[1024]{0:T(1024)} %param.13) | copy-start | bytes 12292
  170.5 24.7 %all-to-all-start.2 = ((f32[64,1,512]{2,1,0:T(1,128)}), f32[64,1,512]{2,1,0:T(1,128)S(1)}, u32[]{:S(2)}, u32[]{:S(2)}) async-start(f32[64,1,512]{2,1,0:T(1,128)} %reshape.119), calls=%async_computation.2 | async-start | bytes 262144 | tf_op jit(solution)/shard_map/all_to_all | solution.py:84
  197.7 29.1 %all-to-all-start.3 = ((f32[64,1,512]{2,1,0:T(1,128)}), f32[64,1,512]{2,1,0:T(1,128)S(1)}, u32[]{:S(2)}, u32[]{:S(2)}) async-start(f32[64,1,512]{2,1,0:T(1,128)} %reshape.121), calls=%async_computation.3 | async-start | bytes 262144 | tf_op jit(solution)/shard_map/all_to_all | solution.py:84
  226.8 99.0 %all-to-all-start.4 = ((bf16[64,128,128]{2,1,0:T(8,128)(2,1)}), bf16[64,128,128]{2,1,0:T(8,128)(2,1)}, u32[]{:S(2)}, u32[]{:S(2)}) async-start(bf16[64,128,128]{2,1,0:T(8,128)(2,1)} %copy.29), calls=%async_computation.4 | async-start | bytes 4194304 | tf_op jit(solution)/shard_map/all_to_all | solution.py:84

commit v15 on v13

--- a/solution.py
+++ b/solution.py
@@ -127,6 +127,9 @@
     ).reshape(col_devices * col_width, col_width)
     pieces = weight_terms.reshape(row_devices, -1, col_width)
     reduced = jnp.sum(rows_exchange(pieces), axis=0)
+    high = reduced.astype(jnp.bfloat16)
+    low = (reduced - high.astype(jnp.float32)).astype(jnp.bfloat16)
+    chunk = jnp.concatenate([high, low], axis=0).reshape(-1, block_size)
     agg_grad = jnp.einsum(
         "jcn,kjc->nk",
         grad_all,
@@ -141,15 +144,22 @@
     send_terms = jnp.einsum(
         "tos,tfi->osfi", slot_pick, sent_terms, preferred_element_type=jnp.float32
     ).astype(jnp.bfloat16)
-    received = rows_exchange(
-        send_terms.reshape(row_devices, capacity * col_width, block_size)
-    ).reshape(row_devices, capacity, col_width, block_size)
-    reduced, received = lax.optimization_barrier((reduced, received))
-    spread = jnp.broadcast_to(reduced[None], (row_devices,) + reduced.shape)
+    payload = jnp.concatenate(
+        [
+            send_terms.reshape(row_devices, capacity * col_width, block_size),
+            jnp.broadcast_to(chunk[None], (row_devices,) + chunk.shape),
+        ],
+        axis=1,
+    )
+    arrived = rows_exchange(payload)
+    received = arrived[:, : capacity * col_width].reshape(
+        row_devices, capacity, col_width, block_size
+    )
+    parts = arrived[:, capacity * col_width :].reshape(row_devices, 2, -1, col_width)
     node_total = local_rows * row_devices
-    weight_grad = rows_exchange(spread).reshape(col_devices * col_width, col_width) / math.sqrt(
-        node_total
-    )
+    weight_grad = (parts[:, 0].astype(jnp.float32) + parts[:, 1].astype(jnp.float32)).reshape(
+        col_devices * col_width, col_width
+    ) / math.sqrt(node_total)
     placing = (wanted[:, :, None] == local_ids[None, None, :]).astype(jnp.bfloat16)
     feature_grad = jnp.einsum(
         "scb,scfi->bif", placing, received, preferred_element_type=jnp.float32

time: 337 us -> 325 us (0.964)
  blocking collectives: 0 us -> 119 us
  waiting for transfers between devices: 202 us -> 101 us
  starting transfers between devices: 60.8 us -> 32.4 us
    all_to_all x0 -> x1, blocking collectives: none -> 119 us  [rows_exchange(): return lax.all_to_all(x, 'rows', split_axis=0, concat_axis=0, tiled=True)]
    all_to_all x5 -> x3, waiting for transfers between devices: 202 us -> 101 us  [rows_exchange(): return lax.all_to_all(x, 'rows', split_axis=0, concat_axis=0, tiled=True)]
    all_to_all x5 -> x3, starting transfers between devices: 60.8 us -> 32.4 us  [rows_exchange(): return lax.all_to_all(x, 'rows', split_axis=0, concat_axis=0, tiled=True)]
  transfers between devices with their start and end apart: 5 -> 3, of which waited for: 4 -> 2; matrix products, arithmetic and copies ran while one was open for 4% -> 3% of each run, Pallas kernels for 4% -> 4%
where the time goes in v15:
time: 325 us; the launch traced here: 324 us
  blocking collectives  119 us (37%)
  waiting for transfers between devices  101 us (31%)
  Pallas kernels  36.3 us (11%)
  starting transfers between devices  32.4 us (10%)
  local copies, waits for them, and re-layouts  16.1 us (5%)
  matrix products  11.9 us (4%)
  other arithmetic  6.06 us (2%)
    all_to_all x1, blocking collectives, rows_exchange(): return lax.all_to_all(x, 'rows', split_axis=0, concat_axis=0, tiled=True)  119 us
    all_to_all x3, waiting for transfers between devices, rows_exchange(): return lax.all_to_all(x, 'rows', split_axis=0, concat_axis=0, tiled=True)  101 us
    pallas_call x2, Pallas kernels, cols_gather(): pl.pallas_call(_cols_gather_kernel, out_shape=jax.ShapeDtypeStruct((n,) +...  36.3 us
    all_to_all x3, starting transfers between devices, rows_exchange(): return lax.all_to_all(x, 'rows', split_axis=0, concat_axis=0, tiled=True)  32.4 us
  transfers between devices with their start and end apart: 3, of which 2 were waited for; matrix products, arithmetic and copies ran while one was open for 3% of the time, Pallas kernels for 4%

profile of v15, /device:TPU:1, one launch (start us, length us, event | category | flops | bytes accessed | tf_op | source)
XLA Modules:
  0.0 324.0 jit_solution(3178687840297050430)
XLA Ops:
  0.6 0.0 copy-start
  0.6 0.9 convert_reduce_fusion
  1.6 0.7 iota_compare_fusion.1
  2.2 0.8 fusion.39
  3.0 0.7 copy.30
  3.7 19.3 %all-to-all-start = ((s32[64,1,2]{2,1,0:T(1,128)}), s32[64,1,2]{2,1,0:T(1,128)S(1)}, u32[]{:S(2)}, u32[]{:S(2)}) async-start(s32[64,1,2]{2,1,0:T(1,128)} %copy.30), calls=%async_computation | async-start | bytes 65536 | tf_op jit(solution)/shard_map/all_to_all | solution.py:84
  23.0 0.9 copy_bitcast_fusion.2
  23.9 12.3 %all-to-all-done = s32[64,1,2]{2,1,0:T(1,128)S(1)} async-done(((s32[64,1,2]{2,1,0:T(1,128)}), s32[64,1,2]{2,1,0:T(1,128)S(1)}, u32[]{:S(2)}, u32[]{:S(2)}) %all-to-all-start) | async-done | bytes 544 | tf_op jit(solution)/shard_map/all_to_all | solution.py:84
  36.2 0.1 copy.31
  36.3 0.1 copy.32
  36.4 0.1 reshape.150
  36.6 2.1 gather_fusion
  38.7 5.7 %all-to-all-start.1 = ((bf16[64,2,128,64]{2,3,1,0:T(8,128)(2,1)}), bf16[64,2,128,64]{2,3,1,0:T(8,128)(2,1)}, u32[]{:S(2)}, u32[]{:S(2)}) async-start(bf16[64,2,128,64]{2,3,1,0:T(8,128)(2,1)} %bitcast.140), calls=%async_computation.1 | async-start | bytes 4194304 | tf_op jit(solution)/shard_map/all_to_all | solution.py:84
  44.4 0.8 constant_dynamic-slice_fusion
  45.3 0.1 reshape.143
  45.4 0.0 copy-done.2
  45.4 1.0 constant_dynamic-slice_fusion.1
  46.5 88.7 %all-to-all-done.1 = bf16[64,2,128,64]{2,3,1,0:T(8,128)(2,1)} async-done(((bf16[64,2,128,64]{2,3,1,0:T(8,128)(2,1)}), bf16[64,2,128,64]{2,3,1,0:T(8,128)(2,1)}, u32[]{:S(2)}, u32[]{:S(2)}) %all-to-all-start.1) | async-done | bytes 2097184 | tf_op jit(solution)/shard_map/all_to_all | solution.py:84
  135.2 2.4 gather_fusion.1
  137.6 1.5 convolution_bitcast_fusion
  139.1 2.0 fusion.11
  141.1 0.0 copy-start.1
  141.1 0.7 copy.73
  141.8 22.1 %shard_map.97 = bf16[8,64,1024]{2,1,0:T(8,128)(2,1)} custom-call(bf16[64,1024]{1,0:T(8,128)(2,1)} %bitcast.144), custom_call_target="tpu_custom_call" | custom-call | tf_op jit(solution)/shard_map/pallas_call | solution.py:67
  163.9 2.2 fusion.37
  166.2 1.8 fusion.32
  167.9 0.8 fusion.22.x_ref
  168.7 0.8 reshape.180
  169.6 7.4 %all-to-all-start.2 = ((f32[64,1,512]{2,1,0:T(1,128)}), f32[64,1,512]{2,1,0:T(1,128)S(1)}, u32[]{:S(2)}, u32[]{:S(2)}) async-start(f32[64,1,512]{2,1,0:T(1,128)} %reshape.180), calls=%async_computation.2 | async-start | bytes 262144 | tf_op jit(solution)/shard_map/all_to_all | solution.py:84
  176.9 14.1 %shard_map.98 = bf16[8,64,1024]{2,1,0:T(8,128)(2,1)} custom-call(bf16[64,1024]{1,0:T(8,128)(2,1)} %fusion.22.x_ref), custom_call_target="tpu_custom_call" | custom-call | tf_op jit(solution)/shard_map/pallas_call | solution.py:67
  191.1 1.6 fusion.14
  192.7 0.7 gather_fusion.2
  193.4 0.7 convolution_convert_fusion.1
  194.1 1.0 convolution_convert_fusion
  195.1 2.7 copy.40
  197.8 0.0 all-to-all-done.2
  197.8 0.5 broadcast.125
  198.4 0.9 reduce
  199.3 0.1 reshape.181
  199.4 0.1 reduce_sum.32
  199.5 0.1 broadcast_in_dim.21
  199.6 1.8 pad_maximum_fusion
  201.4 119.4 %all_to_all.27 = bf16[64,136,128]{2,1,0:T(8,128)(2,1)S(1)} all-to-all(bf16[64,136,128]{2,1,0:T(8,128)(2,1)S(1)} %pad_maximum_fusion), channel_id=1, replica_groups=mesh['rows'=64,'cols'=8] {'rows'}, dimensions={0} | all-to-all | bytes 4456448 | tf_op jit(solution)/shard_map/all_to_all | solution.py:84
  320.9 0.3 slice.25
  321.1 1.2 fusion.8
  322.4 0.7 copy.72
  323.0 0.1 reshape.146
  323.2 0.8 copy.43
  (18 shorter events, 0.2 us)
Async XLA Ops:
  0.6 136.9 %copy-start = (bf16[64,128,128]{2,1,0:T(8,128)(2,1)S(1)}, bf16[64,128,128]{2,1,0:T(8,128)(2,1)}, u32[]{:S(2)}) copy-start(bf16[64,128,128]{2,1,0:T(8,128)(2,1)} %param.9) | copy-start | bytes 6291460
  3.7 32.5 %all-to-all-start = ((s32[64,1,2]{2,1,0:T(1,128)}), s32[64,1,2]{2,1,0:T(1,128)S(1)}, u32[]{:S(2)}, u32[]{:S(2)}) async-start(s32[64,1,2]{2,1,0:T(1,128)} %copy.30), calls=%async_computation | async-start | bytes 65536 | tf_op jit(solution)/shard_map/all_to_all | solution.py:84
  38.7 6.7 %copy-start.2 = (s32[64]{0:T(128)S(1)}, s32[64]{0:T(128)}, u32[]{:S(2)}) copy-start(s32[64]{0:T(128)} %param.10) | copy-start | bytes 772
  38.7 7.8 %copy-start.3 = (s32[64,1]{0,1:T(1,128)S(1)}, s32[64,1]{0,1:T(1,128)}, u32[]{:S(2)}) copy-start(s32[64,1]{0,1:T(1,128)} %param.11) | copy-start | bytes 772
  38.7 96.5 %all-to-all-start.1 = ((bf16[64,2,128,64]{2,3,1,0:T(8,128)(2,1)}), bf16[64,2,128,64]{2,3,1,0:T(8,128)(2,1)}, u32[]{:S(2)}, u32[]{:S(2)}) async-start(bf16[64,2,128,64]{2,3,1,0:T(8,128)(2,1)} %bitcast.140), calls=%async_computation.1 | async-start | bytes 4194304 | tf_op jit(solution)/shard_map/all_to_all | solution.py:84
  141.1 25.1 %copy-start.1 = (s32[1024]{0:T(1024)S(1)}, s32[1024]{0:T(1024)}, u32[]{:S(2)}) copy-start(s32[1024]{0:T(1024)} %param.13) | copy-start | bytes 12292
  169.6 28.3 %all-to-all-start.2 = ((f32[64,1,512]{2,1,0:T(1,128)}), f32[64,1,512]{2,1,0:T(1,128)S(1)}, u32[]{:S(2)}, u32[]{:S(2)}) async-start(f32[64,1,512]{2,1,0:T(1,128)} %reshape.180), calls=%async_computation.2 | async-start | bytes 262144 | tf_op jit(solution)/shard_map/all_to_all | solution.py:84

commit v16 on v15

--- a/solution.py
+++ b/solution.py
@@ -22,8 +22,15 @@
         )
     pl.semaphore_signal(barrier, 1, device_id={"cols": partner}, device_id_type=MESH)
     pl.semaphore_wait(barrier, chips)
-    far = []
-    for k in range(1, chips):
+    near = [
+        pltpu.make_async_remote_copy(
+            src_ref=x_ref, dst_ref=o_ref.at[me], send_sem=pass_sems.at[0],
+            recv_sem=take_sems.at[0], device_id={"cols": partner}, device_id_type=MESH)
+    ]
+    near[0].start()
+    order = [chips // 2] + [k for k in range(1, chips) if k != chips // 2]
+    far = {}
+    for k in order:
         out = pltpu.make_async_remote_copy(
             src_ref=x_ref, dst_ref=o_ref.at[me], send_sem=send_sems.at[k],
             recv_sem=recv_sems.at[k], device_id={"cols": lax.rem(me + 2 * k, n)},
@@ -33,16 +40,10 @@
         back = pltpu.make_async_remote_copy(
             src_ref=x_ref, dst_ref=o_ref.at[src], send_sem=send_sems.at[k],
             recv_sem=recv_sems.at[k], device_id={"cols": src}, device_id_type=MESH)
-        far.append((out, back))
-    near = [
-        pltpu.make_async_remote_copy(
-            src_ref=x_ref, dst_ref=o_ref.at[me], send_sem=pass_sems.at[0],
-            recv_sem=take_sems.at[0], device_id={"cols": partner}, device_id_type=MESH)
-    ]
-    near[0].start()
+        far[k] = (out, back)
     o_ref[me] = x_ref[...]
     for k in range(1, chips):
-        out, back = far[k - 1]
+        out, back = far[k]
         back.wait_recv()
         piece = lax.rem(me + n - 2 * k, n)
         hop = pltpu.make_async_remote_copy(
@@ -56,7 +57,7 @@
             src_ref=o_ref.at[piece], dst_ref=o_ref.at[piece], send_sem=pass_sems.at[k],
             recv_sem=take_sems.at[k], device_id={"cols": partner}, device_id_type=MESH
         ).wait_recv()
-    for out, back in far:
+    for out, back in far.values():
         out.wait_send()
     for hop in near:
         hop.wait_send()

time: 325 us -> 325 us (level)
  no operation moved by 1% of the time
where the time goes in v16:
time: 325 us; the launch traced here: 324 us
  blocking collectives  119 us (37%)
  waiting for transfers between devices  101 us (31%)
  Pallas kernels  36.4 us (11%)
  starting transfers between devices  32.6 us (10%)
  local copies, waits for them, and re-layouts  16.1 us (5%)
  matrix products  11.9 us (4%)
  other arithmetic  6.06 us (2%)
    all_to_all x1, blocking collectives, rows_exchange(): return lax.all_to_all(x, 'rows', split_axis=0, concat_axis=0, tiled=True)  119 us
    all_to_all x3, waiting for transfers between devices, rows_exchange(): return lax.all_to_all(x, 'rows', split_axis=0, concat_axis=0, tiled=True)  101 us
    pallas_call x2, Pallas kernels, cols_gather(): pl.pallas_call(_cols_gather_kernel, out_shape=jax.ShapeDtypeStruct((n,) +...  36.4 us
    all_to_all x3, starting transfers between devices, rows_exchange(): return lax.all_to_all(x, 'rows', split_axis=0, concat_axis=0, tiled=True)  32.6 us
  transfers between devices with their start and end apart: 3, of which 2 were waited for; matrix products, arithmetic and copies ran while one was open for 3% of the time, Pallas kernels for 4%

profile of v16, /device:TPU:1, one launch (start us, length us, event | category | flops | bytes accessed | tf_op | source)
XLA Modules:
  0.0 324.3 jit_solution(7848774044077656192)
XLA Ops:
  0.6 0.0 copy-start
  0.6 0.9 convert_reduce_fusion
  1.6 0.7 iota_compare_fusion.1
  2.2 0.8 fusion.39
  3.0 0.7 copy.30
  3.7 19.3 %all-to-all-start = ((s32[64,1,2]{2,1,0:T(1,128)}), s32[64,1,2]{2,1,0:T(1,128)S(1)}, u32[]{:S(2)}, u32[]{:S(2)}) async-start(s32[64,1,2]{2,1,0:T(1,128)} %copy.30), calls=%async_computation | async-start | bytes 65536 | tf_op jit(solution)/shard_map/all_to_all | solution.py:85
  23.0 0.9 copy_bitcast_fusion.2
  23.9 12.3 %all-to-all-done = s32[64,1,2]{2,1,0:T(1,128)S(1)} async-done(((s32[64,1,2]{2,1,0:T(1,128)}), s32[64,1,2]{2,1,0:T(1,128)S(1)}, u32[]{:S(2)}, u32[]{:S(2)}) %all-to-all-start) | async-done | bytes 544 | tf_op jit(solution)/shard_map/all_to_all | solution.py:85
  36.2 0.1 copy.31
  36.3 0.1 copy.32
  36.4 0.1 reshape.150
  36.6 2.1 gather_fusion
  38.7 5.7 %all-to-all-start.1 = ((bf16[64,2,128,64]{2,3,1,0:T(8,128)(2,1)}), bf16[64,2,128,64]{2,3,1,0:T(8,128)(2,1)}, u32[]{:S(2)}, u32[]{:S(2)}) async-start(bf16[64,2,128,64]{2,3,1,0:T(8,128)(2,1)} %bitcast.140), calls=%async_computation.1 | async-start | bytes 4194304 | tf_op jit(solution)/shard_map/all_to_all | solution.py:85
  44.4 0.8 constant_dynamic-slice_fusion
  45.3 0.1 reshape.143
  45.4 1.0 constant_dynamic-slice_fusion.1
  46.5 88.7 %all-to-all-done.1 = bf16[64,2,128,64]{2,3,1,0:T(8,128)(2,1)} async-done(((bf16[64,2,128,64]{2,3,1,0:T(8,128)(2,1)}), bf16[64,2,128,64]{2,3,1,0:T(8,128)(2,1)}, u32[]{:S(2)}, u32[]{:S(2)}) %all-to-all-start.1) | async-done | bytes 2097184 | tf_op jit(solution)/shard_map/all_to_all | solution.py:85
  135.2 2.4 gather_fusion.1
  137.6 1.5 convolution_bitcast_fusion
  139.1 2.0 fusion.11
  141.1 0.0 copy-start.1
  141.1 0.7 copy.73
  141.8 22.1 %shard_map.97 = bf16[8,64,1024]{2,1,0:T(8,128)(2,1)} custom-call(bf16[64,1024]{1,0:T(8,128)(2,1)} %bitcast.144), custom_call_target="tpu_custom_call" | custom-call | tf_op jit(solution)/shard_map/pallas_call | solution.py:68
  163.8 2.2 fusion.37
  166.1 0.0 copy-done.1
  166.1 1.7 fusion.32
  167.8 0.8 fusion.22.x_ref
  168.6 0.8 reshape.180
  169.5 7.6 %all-to-all-start.2 = ((f32[64,1,512]{2,1,0:T(1,128)}), f32[64,1,512]{2,1,0:T(1,128)S(1)}, u32[]{:S(2)}, u32[]{:S(2)}) async-start(f32[64,1,512]{2,1,0:T(1,128)} %reshape.180), calls=%async_computation.2 | async-start | bytes 262144 | tf_op jit(solution)/shard_map/all_to_all | solution.py:85
  177.1 14.3 %shard_map.98 = bf16[8,64,1024]{2,1,0:T(8,128)(2,1)} custom-call(bf16[64,1024]{1,0:T(8,128)(2,1)} %fusion.22.x_ref), custom_call_target="tpu_custom_call" | custom-call | tf_op jit(solution)/shard_map/pallas_call | solution.py:68
  191.4 1.6 fusion.14
  193.0 0.7 gather_fusion.2
  193.7 0.7 convolution_convert_fusion.1
  194.4 1.0 convolution_convert_fusion
  195.5 2.7 copy.40
  198.2 0.0 all-to-all-done.2
  198.2 0.5 broadcast.125
  198.7 0.9 reduce
  199.6 0.1 reshape.181
  199.7 0.1 reduce_sum.32
  199.8 0.1 broadcast_in_dim.21
  199.9 1.8 pad_maximum_fusion
  201.7 119.4 %all_to_all.27 = bf16[64,136,128]{2,1,0:T(8,128)(2,1)S(1)} all-to-all(bf16[64,136,128]{2,1,0:T(8,128)(2,1)S(1)} %pad_maximum_fusion), channel_id=1, replica_groups=mesh['rows'=64,'cols'=8] {'rows'}, dimensions={0} | all-to-all | bytes 4456448 | tf_op jit(solution)/shard_map/all_to_all | solution.py:85
  321.2 0.3 slice.25
  321.5 1.2 fusion.8
  322.7 0.7 copy.72
  323.4 0.1 reshape.146
  323.6 0.8 copy.43
  (18 shorter events, 0.2 us)
Async XLA Ops:
  0.6 136.9 %copy-start = (bf16[64,128,128]{2,1,0:T(8,128)(2,1)S(1)}, bf16[64,128,128]{2,1,0:T(8,128)(2,1)}, u32[]{:S(2)}) copy-start(bf16[64,128,128]{2,1,0:T(8,128)(2,1)} %param.9) | copy-start | bytes 6291460
  3.7 32.5 %all-to-all-start = ((s32[64,1,2]{2,1,0:T(1,128)}), s32[64,1,2]{2,1,0:T(1,128)S(1)}, u32[]{:S(2)}, u32[]{:S(2)}) async-start(s32[64,1,2]{2,1,0:T(1,128)} %copy.30), calls=%async_computation | async-start | bytes 65536 | tf_op jit(solution)/shard_map/all_to_all | solution.py:85
  38.7 6.7 %copy-start.2 = (s32[64]{0:T(128)S(1)}, s32[64]{0:T(128)}, u32[]{:S(2)}) copy-start(s32[64]{0:T(128)} %param.10) | copy-start | bytes 772
  38.7 7.8 %copy-start.3 = (s32[64,1]{0,1:T(1,128)S(1)}, s32[64,1]{0,1:T(1,128)}, u32[]{:S(2)}) copy-start(s32[64,1]{0,1:T(1,128)} %param.11) | copy-start | bytes 772
  38.7 96.5 %all-to-all-start.1 = ((bf16[64,2,128,64]{2,3,1,0:T(8,128)(2,1)}), bf16[64,2,128,64]{2,3,1,0:T(8,128)(2,1)}, u32[]{:S(2)}, u32[]{:S(2)}) async-start(bf16[64,2,128,64]{2,3,1,0:T(8,128)(2,1)} %bitcast.140), calls=%async_computation.1 | async-start | bytes 4194304 | tf_op jit(solution)/shard_map/all_to_all | solution.py:85
  141.1 25.0 %copy-start.1 = (s32[1024]{0:T(1024)S(1)}, s32[1024]{0:T(1024)}, u32[]{:S(2)}) copy-start(s32[1024]{0:T(1024)} %param.13) | copy-start | bytes 12292
  169.5 28.7 %all-to-all-start.2 = ((f32[64,1,512]{2,1,0:T(1,128)}), f32[64,1,512]{2,1,0:T(1,128)S(1)}, u32[]{:S(2)}, u32[]{:S(2)}) async-start(f32[64,1,512]{2,1,0:T(1,128)} %reshape.180), calls=%async_computation.2 | async-start | bytes 262144 | tf_op jit(solution)/shard_map/all_to_all | solution.py:85

commit v17 on v15

--- a/solution.py
+++ b/solution.py
@@ -13,8 +13,10 @@
 def _cols_gather_kernel(x_ref, o_ref, send_sems, recv_sems, pass_sems, take_sems):
     n = o_ref.shape[0]
     chips = n // 2
+    far_k = chips // 2
     me = lax.axis_index("cols")
-    partner = me + 1 - 2 * lax.rem(me, 2)
+    core = lax.rem(me, 2)
+    partner = me + 1 - 2 * core
     barrier = pltpu.get_barrier_semaphore()
     for k in range(1, chips):
         pl.semaphore_signal(
@@ -22,28 +24,45 @@
         )
     pl.semaphore_signal(barrier, 1, device_id={"cols": partner}, device_id_type=MESH)
     pl.semaphore_wait(barrier, chips)
-    far = []
-    for k in range(1, chips):
-        out = pltpu.make_async_remote_copy(
+
+    def direct(k):
+        return pltpu.make_async_remote_copy(
             src_ref=x_ref, dst_ref=o_ref.at[me], send_sem=send_sems.at[k],
             recv_sem=recv_sems.at[k], device_id={"cols": lax.rem(me + 2 * k, n)},
             device_id_type=MESH)
-        out.start()
+
+    def arrival(k):
         src = lax.rem(me + n - 2 * k, n)
-        back = pltpu.make_async_remote_copy(
+        return pltpu.make_async_remote_copy(
             src_ref=x_ref, dst_ref=o_ref.at[src], send_sem=send_sems.at[k],
             recv_sem=recv_sems.at[k], device_id={"cols": src}, device_id_type=MESH)
-        far.append((out, back))
+
+    relay_from = lax.rem(me + 2, n)
+    relay = pltpu.make_async_remote_copy(
+        src_ref=o_ref.at[relay_from], dst_ref=o_ref.at[relay_from], send_sem=send_sems.at[far_k],
+        recv_sem=recv_sems.at[far_k], device_id={"cols": lax.rem(me + n - 2, n)},
+        device_id_type=MESH)
     near = [
         pltpu.make_async_remote_copy(
             src_ref=x_ref, dst_ref=o_ref.at[me], send_sem=pass_sems.at[0],
             recv_sem=take_sems.at[0], device_id={"cols": partner}, device_id_type=MESH)
     ]
     near[0].start()
+    for k in range(1, chips):
+        if k == far_k:
+            @pl.when(core == 0)
+            def _():
+                direct(k).start()
+        else:
+            direct(k).start()
     o_ref[me] = x_ref[...]
-    for k in range(1, chips):
-        out, back = far[k - 1]
-        back.wait_recv()
+    order = [chips - 1] + [k for k in range(1, chips - 1)]
+    for k in order:
+        arrival(k).wait_recv()
+        if k == chips - 1:
+            @pl.when(core == 1)
+            def _():
+                relay.start()
         piece = lax.rem(me + n - 2 * k, n)
         hop = pltpu.make_async_remote_copy(
             src_ref=o_ref.at[piece], dst_ref=o_ref.at[piece], send_sem=pass_sems.at[k],
@@ -56,8 +75,8 @@
             src_ref=o_ref.at[piece], dst_ref=o_ref.at[piece], send_sem=pass_sems.at[k],
             recv_sem=take_sems.at[k], device_id={"cols": partner}, device_id_type=MESH
         ).wait_recv()
-    for out, back in far:
-        out.wait_send()
+    for k in range(1, chips):
+        direct(k).wait_send()
     for hop in near:
         hop.wait_send()
 

time: 325 us -> 324 us (level)
  no operation moved by 1% of the time
where the time goes in v17:
time: 324 us
  blocking collectives  120 us (37%)
  waiting for transfers between devices  101 us (31%)
  Pallas kernels  35.3 us (11%)
  starting transfers between devices  32.2 us (10%)
  local copies, waits for them, and re-layouts  16.1 us (5%)
  matrix products  11.9 us (4%)
  other arithmetic  6.06 us (2%)
    all_to_all x1, blocking collectives, rows_exchange(): return lax.all_to_all(x, 'rows', split_axis=0, concat_axis=0, tiled=True)  120 us
    all_to_all x3, waiting for transfers between devices, rows_exchange(): return lax.all_to_all(x, 'rows', split_axis=0, concat_axis=0, tiled=True)  101 us
    pallas_call x2, Pallas kernels, cols_gather(): pl.pallas_call(_cols_gather_kernel, out_shape=jax.ShapeDtypeStruct((n,) +...  35.3 us
    all_to_all x3, starting transfers between devices, rows_exchange(): return lax.all_to_all(x, 'rows', split_axis=0, concat_axis=0, tiled=True)  32.2 us
  transfers between devices with their start and end apart: 3, of which 2 were waited for; matrix products, arithmetic and copies ran while one was open for 3% of the time, Pallas kernels for 4%

profile of v17, /device:TPU:1, one launch (start us, length us, event | category | flops | bytes accessed | tf_op | source)
XLA Modules:
  0.0 323.6 jit_solution(7350012477298152783)
XLA Ops:
  0.6 0.0 copy-start
  0.6 0.9 convert_reduce_fusion
  1.6 0.7 iota_compare_fusion.1
  2.2 0.8 fusion.39
  3.0 0.7 copy.30
  3.7 19.3 %all-to-all-start = ((s32[64,1,2]{2,1,0:T(1,128)}), s32[64,1,2]{2,1,0:T(1,128)S(1)}, u32[]{:S(2)}, u32[]{:S(2)}) async-start(s32[64,1,2]{2,1,0:T(1,128)} %copy.30), calls=%async_computation | async-start | bytes 65536 | tf_op jit(solution)/shard_map/all_to_all | solution.py:103
  23.0 0.9 copy_bitcast_fusion.2
  23.9 12.3 %all-to-all-done = s32[64,1,2]{2,1,0:T(1,128)S(1)} async-done(((s32[64,1,2]{2,1,0:T(1,128)}), s32[64,1,2]{2,1,0:T(1,128)S(1)}, u32[]{:S(2)}, u32[]{:S(2)}) %all-to-all-start) | async-done | bytes 544 | tf_op jit(solution)/shard_map/all_to_all | solution.py:103
  36.2 0.1 copy.31
  36.3 0.1 copy.32
  36.4 0.1 reshape.150
  36.6 2.1 gather_fusion
  38.7 5.7 %all-to-all-start.1 = ((bf16[64,2,128,64]{2,3,1,0:T(8,128)(2,1)}), bf16[64,2,128,64]{2,3,1,0:T(8,128)(2,1)}, u32[]{:S(2)}, u32[]{:S(2)}) async-start(bf16[64,2,128,64]{2,3,1,0:T(8,128)(2,1)} %bitcast.140), calls=%async_computation.1 | async-start | bytes 4194304 | tf_op jit(solution)/shard_map/all_to_all | solution.py:103
  44.4 0.8 constant_dynamic-slice_fusion
  45.3 0.1 reshape.143
  45.4 0.0 copy-done.2
  45.4 1.0 constant_dynamic-slice_fusion.1
  46.5 88.7 %all-to-all-done.1 = bf16[64,2,128,64]{2,3,1,0:T(8,128)(2,1)} async-done(((bf16[64,2,128,64]{2,3,1,0:T(8,128)(2,1)}), bf16[64,2,128,64]{2,3,1,0:T(8,128)(2,1)}, u32[]{:S(2)}, u32[]{:S(2)}) %all-to-all-start.1) | async-done | bytes 2097184 | tf_op jit(solution)/shard_map/all_to_all | solution.py:103
  135.2 2.4 gather_fusion.1
  137.6 1.5 convolution_bitcast_fusion
  139.1 2.0 fusion.11
  141.1 0.0 copy-start.1
  141.1 0.7 copy.73
  141.8 21.7 %shard_map.97 = bf16[8,64,1024]{2,1,0:T(8,128)(2,1)} custom-call(bf16[64,1024]{1,0:T(8,128)(2,1)} %bitcast.144), custom_call_target="tpu_custom_call" | custom-call | tf_op jit(solution)/shard_map/pallas_call | solution.py:86
  163.5 2.2 fusion.37
  165.8 1.7 fusion.32
  167.5 0.8 fusion.22.x_ref
  168.3 0.8 reshape.180
  169.1 7.3 %all-to-all-start.2 = ((f32[64,1,512]{2,1,0:T(1,128)}), f32[64,1,512]{2,1,0:T(1,128)S(1)}, u32[]{:S(2)}, u32[]{:S(2)}) async-start(f32[64,1,512]{2,1,0:T(1,128)} %reshape.180), calls=%async_computation.2 | async-start | bytes 262144 | tf_op jit(solution)/shard_map/all_to_all | solution.py:103
  176.4 13.5 %shard_map.98 = bf16[8,64,1024]{2,1,0:T(8,128)(2,1)} custom-call(bf16[64,1024]{1,0:T(8,128)(2,1)} %fusion.22.x_ref), custom_call_target="tpu_custom_call" | custom-call | tf_op jit(solution)/shard_map/pallas_call | solution.py:86
  190.0 1.6 fusion.14
  191.6 0.7 gather_fusion.2
  192.3 0.7 convolution_convert_fusion.1
  193.0 1.0 convolution_convert_fusion
  194.0 2.7 copy.40
  196.7 0.0 all-to-all-done.2
  196.7 0.5 broadcast.125
  197.2 0.9 reduce
  198.2 0.1 reshape.181
  198.3 0.1 reduce_sum.32
  198.4 0.1 broadcast_in_dim.21
  198.5 1.8 pad_maximum_fusion
  200.3 120.1 %all_to_all.27 = bf16[64,136,128]{2,1,0:T(8,128)(2,1)S(1)} all-to-all(bf16[64,136,128]{2,1,0:T(8,128)(2,1)S(1)} %pad_maximum_fusion), channel_id=1, replica_groups=mesh['rows'=64,'cols'=8] {'rows'}, dimensions={0} | all-to-all | bytes 4456448 | tf_op jit(solution)/shard_map/all_to_all | solution.py:103
  320.4 0.3 slice.25
  320.7 1.2 fusion.8
  321.9 0.7 copy.72
  322.6 0.1 reshape.146
  322.8 0.8 copy.43
  (18 shorter events, 0.2 us)
Async XLA Ops:
  0.6 136.9 %copy-start = (bf16[64,128,128]{2,1,0:T(8,128)(2,1)S(1)}, bf16[64,128,128]{2,1,0:T(8,128)(2,1)}, u32[]{:S(2)}) copy-start(bf16[64,128,128]{2,1,0:T(8,128)(2,1)} %param.9) | copy-start | bytes 6291460
  3.7 32.5 %all-to-all-start = ((s32[64,1,2]{2,1,0:T(1,128)}), s32[64,1,2]{2,1,0:T(1,128)S(1)}, u32[]{:S(2)}, u32[]{:S(2)}) async-start(s32[64,1,2]{2,1,0:T(1,128)} %copy.30), calls=%async_computation | async-start | bytes 65536 | tf_op jit(solution)/shard_map/all_to_all | solution.py:103
  38.7 6.7 %copy-start.2 = (s32[64]{0:T(128)S(1)}, s32[64]{0:T(128)}, u32[]{:S(2)}) copy-start(s32[64]{0:T(128)} %param.10) | copy-start | bytes 772
  38.7 7.8 %copy-start.3 = (s32[64,1]{0,1:T(1,128)S(1)}, s32[64,1]{0,1:T(1,128)}, u32[]{:S(2)}) copy-start(s32[64,1]{0,1:T(1,128)} %param.11) | copy-start | bytes 772
  38.7 96.5 %all-to-all-start.1 = ((bf16[64,2,128,64]{2,3,1,0:T(8,128)(2,1)}), bf16[64,2,128,64]{2,3,1,0:T(8,128)(2,1)}, u32[]{:S(2)}, u32[]{:S(2)}) async-start(bf16[64,2,128,64]{2,3,1,0:T(8,128)(2,1)} %bitcast.140), calls=%async_computation.1 | async-start | bytes 4194304 | tf_op jit(solution)/shard_map/all_to_all | solution.py:103
  141.1 24.7 %copy-start.1 = (s32[1024]{0:T(1024)S(1)}, s32[1024]{0:T(1024)}, u32[]{:S(2)}) copy-start(s32[1024]{0:T(1024)} %param.13) | copy-start | bytes 12292
  169.1 27.6 %all-to-all-start.2 = ((f32[64,1,512]{2,1,0:T(1,128)}), f32[64,1,512]{2,1,0:T(1,128)S(1)}, u32[]{:S(2)}, u32[]{:S(2)}) async-start(f32[64,1,512]{2,1,0:T(1,128)} %reshape.180), calls=%async_computation.2 | async-start | bytes 262144 | tf_op jit(solution)/shard_map/all_to_all | solution.py:103

commit v18 on v17

--- a/solution.py
+++ b/solution.py
@@ -160,8 +160,10 @@
         "tji,tjf->tfi", tile_values, grad_rows, preferred_element_type=jnp.float32
     ).astype(jnp.bfloat16)
     slot_pick = in_slot.astype(jnp.bfloat16)
-    send_terms = jnp.einsum(
-        "tos,tfi->osfi", slot_pick, sent_terms, preferred_element_type=jnp.float32
+    send_terms = jnp.dot(
+        jnp.transpose(slot_pick, (1, 2, 0)).reshape(row_devices * capacity, tiles),
+        sent_terms.reshape(tiles, col_width * block_size),
+        preferred_element_type=jnp.float32,
     ).astype(jnp.bfloat16)
     payload = jnp.concatenate(
         [

time: 324 us -> 327 us (level)
  transfers between devices with their start and end apart: 3 -> 3, of which waited for: 2 -> 2; matrix products, arithmetic and copies ran while one was open for 3% -> 4% of each run, Pallas kernels for 4% -> 4%
where the time goes in v18:
time: 327 us; the launch traced here: 326 us
  blocking collectives  120 us (37%)
  waiting for transfers between devices  101 us (31%)
  Pallas kernels  35.3 us (11%)
  starting transfers between devices  32 us (10%)
  local copies, waits for them, and re-layouts  17.6 us (5%)
  matrix products  13.2 us (4%)
  other arithmetic  6.34 us (2%)
    all_to_all x1, blocking collectives, rows_exchange(): return lax.all_to_all(x, 'rows', split_axis=0, concat_axis=0, tiled=True)  120 us
    all_to_all x3, waiting for transfers between devices, rows_exchange(): return lax.all_to_all(x, 'rows', split_axis=0, concat_axis=0, tiled=True)  101 us
    pallas_call x2, Pallas kernels, cols_gather(): pl.pallas_call(_cols_gather_kernel, out_shape=jax.ShapeDtypeStruct((n,) +...  35.3 us
    all_to_all x3, starting transfers between devices, rows_exchange(): return lax.all_to_all(x, 'rows', split_axis=0, concat_axis=0, tiled=True)  32 us
  transfers between devices with their start and end apart: 3, of which 2 were waited for; matrix products, arithmetic and copies ran while one was open for 4% of the time, Pallas kernels for 4%

profile of v18, /device:TPU:1, one launch (start us, length us, event | category | flops | bytes accessed | tf_op | source)
XLA Modules:
  0.0 326.5 jit_solution(7625933271851759088)
XLA Ops:
  0.6 0.0 copy-start
  0.6 1.0 convert_reduce_fusion
  1.6 0.8 iota_compare_fusion
  2.5 0.8 select_reduce_fusion
  3.2 0.7 copy.47
  4.0 19.3 %all-to-all-start = ((s32[64,1,2]{2,1,0:T(1,128)}), s32[64,1,2]{2,1,0:T(1,128)S(1)}, u32[]{:S(2)}, u32[]{:S(2)}) async-start(s32[64,1,2]{2,1,0:T(1,128)} %copy.47), calls=%async_computation | async-start | bytes 65536 | tf_op jit(solution)/shard_map/all_to_all | solution.py:103
  23.2 0.9 copy_bitcast_fusion.2
  24.2 12.3 %all-to-all-done = s32[64,1,2]{2,1,0:T(1,128)S(1)} async-done(((s32[64,1,2]{2,1,0:T(1,128)}), s32[64,1,2]{2,1,0:T(1,128)S(1)}, u32[]{:S(2)}, u32[]{:S(2)}) %all-to-all-start) | async-done | bytes 544 | tf_op jit(solution)/shard_map/all_to_all | solution.py:103
  36.5 0.1 copy.48
  36.5 0.1 copy.49
  36.6 0.1 reshape.167
  36.8 2.1 gather_fusion
  38.9 5.7 %all-to-all-start.1 = ((bf16[64,2,128,64]{2,3,1,0:T(8,128)(2,1)}), bf16[64,2,128,64]{2,3,1,0:T(8,128)(2,1)}, u32[]{:S(2)}, u32[]{:S(2)}) async-start(bf16[64,2,128,64]{2,3,1,0:T(8,128)(2,1)} %bitcast.144), calls=%async_computation.1 | async-start | bytes 4194304 | tf_op jit(solution)/shard_map/all_to_all | solution.py:103
  44.7 0.9 constant_dynamic-slice_fusion
  45.6 0.1 reshape.159
  45.8 1.0 constant_dynamic-slice_fusion.1
  46.8 0.0 copy-done.2
  46.8 88.6 %all-to-all-done.1 = bf16[64,2,128,64]{2,3,1,0:T(8,128)(2,1)} async-done(((bf16[64,2,128,64]{2,3,1,0:T(8,128)(2,1)}), bf16[64,2,128,64]{2,3,1,0:T(8,128)(2,1)}, u32[]{:S(2)}, u32[]{:S(2)}) %all-to-all-start.1) | async-done | bytes 2097184 | tf_op jit(solution)/shard_map/all_to_all | solution.py:103
  135.4 2.4 gather_fusion.1
  137.8 1.5 convolution_bitcast_fusion
  139.3 2.0 fusion.11
  141.3 0.0 copy-start.1
  141.3 0.7 copy.92
  142.0 21.7 %shard_map.97 = bf16[8,64,1024]{2,1,0:T(8,128)(2,1)} custom-call(bf16[64,1024]{1,0:T(8,128)(2,1)} %bitcast.148), custom_call_target="tpu_custom_call" | custom-call | tf_op jit(solution)/shard_map/pallas_call | solution.py:86
  163.7 2.2 fusion.37
  166.0 1.7 fusion.32
  167.7 0.8 fusion.22.x_ref
  168.5 0.8 reshape.195
  169.4 7.1 %all-to-all-start.2 = ((f32[64,1,512]{2,1,0:T(1,128)}), f32[64,1,512]{2,1,0:T(1,128)S(1)}, u32[]{:S(2)}, u32[]{:S(2)}) async-start(f32[64,1,512]{2,1,0:T(1,128)} %reshape.195), calls=%async_computation.2 | async-start | bytes 262144 | tf_op jit(solution)/shard_map/all_to_all | solution.py:103
  176.4 13.6 %shard_map.98 = bf16[8,64,1024]{2,1,0:T(8,128)(2,1)} custom-call(bf16[64,1024]{1,0:T(8,128)(2,1)} %fusion.22.x_ref), custom_call_target="tpu_custom_call" | custom-call | tf_op jit(solution)/shard_map/pallas_call | solution.py:86
  190.0 1.6 fusion.14
  191.6 0.7 gather_fusion.2
  192.3 0.7 convolution_convert_fusion.1
  193.0 2.3 convolution_convert_fusion
  195.3 4.2 %reshape.162 = bf16[64,128,128]{2,1,0:T(8,128)(2,1)} reshape(bf16[128,8192]{1,0:T(8,128)(2,1)} %convolution_convert_fusion) | data formatting | bytes 4194304 | tf_op jit(solution)/shard_map/reshape | solution.py:170
  199.5 0.0 all-to-all-done.2
  199.5 0.5 broadcast.137
  200.0 0.9 reduce
  200.9 0.1 reshape.196
  201.0 0.1 reduce_sum.32
  201.1 0.1 broadcast_in_dim.21
  201.2 1.8 pad_maximum_fusion
  203.0 120.3 %all_to_all.27 = bf16[64,136,128]{2,1,0:T(8,128)(2,1)S(1)} all-to-all(bf16[64,136,128]{2,1,0:T(8,128)(2,1)S(1)} %pad_maximum_fusion), channel_id=1, replica_groups=mesh['rows'=64,'cols'=8] {'rows'}, dimensions={0} | all-to-all | bytes 4456448 | tf_op jit(solution)/shard_map/all_to_all | solution.py:103
  323.3 0.3 slice.25
  323.6 1.2 fusion.8
  324.8 0.7 copy.91
  325.5 0.1 reshape.163
  325.7 0.8 copy.60
  (21 shorter events, 0.3 us)
Async XLA Ops:
  0.6 137.2 %copy-start = (bf16[64,128,128]{2,1,0:T(8,128)(2,1)S(1)}, bf16[64,128,128]{2,1,0:T(8,128)(2,1)}, u32[]{:S(2)}) copy-start(bf16[64,128,128]{2,1,0:T(8,128)(2,1)} %param.9) | copy-start | bytes 6291460
  4.0 32.5 %all-to-all-start = ((s32[64,1,2]{2,1,0:T(1,128)}), s32[64,1,2]{2,1,0:T(1,128)S(1)}, u32[]{:S(2)}, u32[]{:S(2)}) async-start(s32[64,1,2]{2,1,0:T(1,128)} %copy.47), calls=%async_computation | async-start | bytes 65536 | tf_op jit(solution)/shard_map/all_to_all | solution.py:103
  38.9 6.8 %copy-start.3 = (s32[64]{0:T(128)S(1)}, s32[64]{0:T(128)}, u32[]{:S(2)}) copy-start(s32[64]{0:T(128)} %param.10) | copy-start | bytes 772
  38.9 7.9 %copy-start.2 = (s32[64,1]{0,1:T(1,128)S(1)}, s32[64,1]{0,1:T(1,128)}, u32[]{:S(2)}) copy-start(s32[64,1]{0,1:T(1,128)} %param.11) | copy-start | bytes 772
  38.9 96.5 %all-to-all-start.1 = ((bf16[64,2,128,64]{2,3,1,0:T(8,128)(2,1)}), bf16[64,2,128,64]{2,3,1,0:T(8,128)(2,1)}, u32[]{:S(2)}, u32[]{:S(2)}) async-start(bf16[64,2,128,64]{2,3,1,0:T(8,128)(2,1)} %bitcast.144), calls=%async_computation.1 | async-start | bytes 4194304 | tf_op jit(solution)/shard_map/all_to_all | solution.py:103
  141.3 24.7 %copy-start.1 = (s32[1024]{0:T(1024)S(1)}, s32[1024]{0:T(1024)}, u32[]{:S(2)}) copy-start(s32[1024]{0:T(1024)} %param.13) | copy-start | bytes 12292
  169.4 30.1 %all-to-all-start.2 = ((f32[64,1,512]{2,1,0:T(1,128)}), f32[64,1,512]{2,1,0:T(1,128)S(1)}, u32[]{:S(2)}, u32[]{:S(2)}) async-start(f32[64,1,512]{2,1,0:T(1,128)} %reshape.195), calls=%async_computation.2 | async-start | bytes 262144 | tf_op jit(solution)/shard_map/all_to_all | solution.py:103

commit v19 on v17

--- a/solution.py
+++ b/solution.py
@@ -126,7 +126,7 @@
     products = jnp.einsum(
         "tij,tjf->tif", tile_values, source_rows, preferred_element_type=jnp.float32
     )
-    summed = jnp.einsum("tb,tif->bif", row_onehot, products, precision=lax.Precision.HIGHEST)
+    summed = jnp.einsum("tb,tif->bif", row_onehot, products, precision=lax.Precision.HIGH)
     aggregated = summed.reshape(local_rows, col_width).astype(jnp.bfloat16)
     aggregated_all = cols_gather(aggregated.T, 2)
     col_index = lax.axis_index("cols")

time: 324 us -> 324 us (level)
  no operation moved by 1% of the time
where the time goes in v19:
time: 324 us; the launch traced here: 323 us
  blocking collectives  120 us (37%)
  waiting for transfers between devices  101 us (31%)
  Pallas kernels  35.3 us (11%)
  starting transfers between devices  32.2 us (10%)
  local copies, waits for them, and re-layouts  16.1 us (5%)
  matrix products  11.6 us (4%)
  other arithmetic  6.06 us (2%)
    all_to_all x1, blocking collectives, rows_exchange(): return lax.all_to_all(x, 'rows', split_axis=0, concat_axis=0, tiled=True)  120 us
    all_to_all x3, waiting for transfers between devices, rows_exchange(): return lax.all_to_all(x, 'rows', split_axis=0, concat_axis=0, tiled=True)  101 us
    pallas_call x2, Pallas kernels, cols_gather(): pl.pallas_call(_cols_gather_kernel, out_shape=jax.ShapeDtypeStruct((n,) +...  35.3 us
    all_to_all x3, starting transfers between devices, rows_exchange(): return lax.all_to_all(x, 'rows', split_axis=0, concat_axis=0, tiled=True)  32.2 us
  transfers between devices with their start and end apart: 3, of which 2 were waited for; matrix products, arithmetic and copies ran while one was open for 3% of the time, Pallas kernels for 4%

profile of v19, /device:TPU:1, one launch (start us, length us, event | category | flops | bytes accessed | tf_op | source)
XLA Modules:
  0.0 323.2 jit_solution(1673508070542221486)
XLA Ops:
  0.6 0.0 copy-start
  0.6 0.9 convert_reduce_fusion
  1.6 0.7 iota_compare_fusion.1
  2.2 0.8 fusion.39
  3.0 0.7 copy.30
  3.7 19.3 %all-to-all-start = ((s32[64,1,2]{2,1,0:T(1,128)}), s32[64,1,2]{2,1,0:T(1,128)S(1)}, u32[]{:S(2)}, u32[]{:S(2)}) async-start(s32[64,1,2]{2,1,0:T(1,128)} %copy.30), calls=%async_computation | async-start | bytes 65536 | tf_op jit(solution)/shard_map/all_to_all | solution.py:103
  23.0 0.9 copy_bitcast_fusion.2
  23.9 12.3 %all-to-all-done = s32[64,1,2]{2,1,0:T(1,128)S(1)} async-done(((s32[64,1,2]{2,1,0:T(1,128)}), s32[64,1,2]{2,1,0:T(1,128)S(1)}, u32[]{:S(2)}, u32[]{:S(2)}) %all-to-all-start) | async-done | bytes 544 | tf_op jit(solution)/shard_map/all_to_all | solution.py:103
  36.2 0.1 copy.31
  36.3 0.1 copy.32
  36.4 0.1 reshape.150
  36.6 2.1 gather_fusion
  38.7 5.7 %all-to-all-start.1 = ((bf16[64,2,128,64]{2,3,1,0:T(8,128)(2,1)}), bf16[64,2,128,64]{2,3,1,0:T(8,128)(2,1)}, u32[]{:S(2)}, u32[]{:S(2)}) async-start(bf16[64,2,128,64]{2,3,1,0:T(8,128)(2,1)} %bitcast.140), calls=%async_computation.1 | async-start | bytes 4194304 | tf_op jit(solution)/shard_map/all_to_all | solution.py:103
  44.4 0.8 constant_dynamic-slice_fusion
  45.3 0.1 reshape.143
  45.4 0.0 copy-done.2
  45.4 1.0 constant_dynamic-slice_fusion.1
  46.5 88.7 %all-to-all-done.1 = bf16[64,2,128,64]{2,3,1,0:T(8,128)(2,1)} async-done(((bf16[64,2,128,64]{2,3,1,0:T(8,128)(2,1)}), bf16[64,2,128,64]{2,3,1,0:T(8,128)(2,1)}, u32[]{:S(2)}, u32[]{:S(2)}) %all-to-all-start.1) | async-done | bytes 2097184 | tf_op jit(solution)/shard_map/all_to_all | solution.py:103
  135.2 2.4 gather_fusion.1
  137.6 1.5 convolution_bitcast_fusion
  139.1 1.6 fusion.11
  140.7 0.0 copy-start.1
  140.7 0.7 copy.73
  141.4 21.7 %shard_map.97 = bf16[8,64,1024]{2,1,0:T(8,128)(2,1)} custom-call(bf16[64,1024]{1,0:T(8,128)(2,1)} %bitcast.144), custom_call_target="tpu_custom_call" | custom-call | tf_op jit(solution)/shard_map/pallas_call | solution.py:86
  163.1 2.2 fusion.37
  165.4 1.7 fusion.32
  167.1 0.8 fusion.22.x_ref
  167.9 0.8 reshape.180
  168.8 7.3 %all-to-all-start.2 = ((f32[64,1,512]{2,1,0:T(1,128)}), f32[64,1,512]{2,1,0:T(1,128)S(1)}, u32[]{:S(2)}, u32[]{:S(2)}) async-start(f32[64,1,512]{2,1,0:T(1,128)} %reshape.180), calls=%async_computation.2 | async-start | bytes 262144 | tf_op jit(solution)/shard_map/all_to_all | solution.py:103
  176.0 13.5 %shard_map.98 = bf16[8,64,1024]{2,1,0:T(8,128)(2,1)} custom-call(bf16[64,1024]{1,0:T(8,128)(2,1)} %fusion.22.x_ref), custom_call_target="tpu_custom_call" | custom-call | tf_op jit(solution)/shard_map/pallas_call | solution.py:86
  189.6 1.6 fusion.14
  191.2 0.7 gather_fusion.2
  191.9 0.7 convolution_convert_fusion.1
  192.6 1.0 convolution_convert_fusion
  193.6 2.7 copy.40
  196.3 0.0 all-to-all-done.2
  196.3 0.5 broadcast.125
  196.9 0.9 reduce
  197.8 0.1 reshape.181
  197.9 0.1 reduce_sum.32
  198.0 0.1 broadcast_in_dim.21
  198.1 1.8 pad_maximum_fusion
  199.9 120.1 %all_to_all.27 = bf16[64,136,128]{2,1,0:T(8,128)(2,1)S(1)} all-to-all(bf16[64,136,128]{2,1,0:T(8,128)(2,1)S(1)} %pad_maximum_fusion), channel_id=1, replica_groups=mesh['rows'=64,'cols'=8] {'rows'}, dimensions={0} | all-to-all | bytes 4456448 | tf_op jit(solution)/shard_map/all_to_all | solution.py:103
  320.0 0.3 slice.25
  320.3 1.2 fusion.8
  321.5 0.7 copy.72
  322.2 0.1 reshape.146
  322.4 0.8 copy.43
  (18 shorter events, 0.2 us)
Async XLA Ops:
  0.6 136.9 %copy-start = (bf16[64,128,128]{2,1,0:T(8,128)(2,1)S(1)}, bf16[64,128,128]{2,1,0:T(8,128)(2,1)}, u32[]{:S(2)}) copy-start(bf16[64,128,128]{2,1,0:T(8,128)(2,1)} %param.9) | copy-start | bytes 6291460
  3.7 32.5 %all-to-all-start = ((s32[64,1,2]{2,1,0:T(1,128)}), s32[64,1,2]{2,1,0:T(1,128)S(1)}, u32[]{:S(2)}, u32[]{:S(2)}) async-start(s32[64,1,2]{2,1,0:T(1,128)} %copy.30), calls=%async_computation | async-start | bytes 65536 | tf_op jit(solution)/shard_map/all_to_all | solution.py:103
  38.7 6.7 %copy-start.2 = (s32[64]{0:T(128)S(1)}, s32[64]{0:T(128)}, u32[]{:S(2)}) copy-start(s32[64]{0:T(128)} %param.10) | copy-start | bytes 772
  38.7 7.8 %copy-start.3 = (s32[64,1]{0,1:T(1,128)S(1)}, s32[64,1]{0,1:T(1,128)}, u32[]{:S(2)}) copy-start(s32[64,1]{0,1:T(1,128)} %param.11) | copy-start | bytes 772
  38.7 96.5 %all-to-all-start.1 = ((bf16[64,2,128,64]{2,3,1,0:T(8,128)(2,1)}), bf16[64,2,128,64]{2,3,1,0:T(8,128)(2,1)}, u32[]{:S(2)}, u32[]{:S(2)}) async-start(bf16[64,2,128,64]{2,3,1,0:T(8,128)(2,1)} %bitcast.140), calls=%async_computation.1 | async-start | bytes 4194304 | tf_op jit(solution)/shard_map/all_to_all | solution.py:103
  140.7 24.7 %copy-start.1 = (s32[1024]{0:T(1024)S(1)}, s32[1024]{0:T(1024)}, u32[]{:S(2)}) copy-start(s32[1024]{0:T(1024)} %param.13) | copy-start | bytes 12292
  168.8 27.6 %all-to-all-start.2 = ((f32[64,1,512]{2,1,0:T(1,128)}), f32[64,1,512]{2,1,0:T(1,128)S(1)}, u32[]{:S(2)}, u32[]{:S(2)}) async-start(f32[64,1,512]{2,1,0:T(1,128)} %reshape.180), calls=%async_computation.2 | async-start | bytes 262144 | tf_op jit(solution)/shard_map/all_to_all | solution.py:103
